TPU v7x, 32 devices: a whole 2x2x4 slice. The times are simulated.
32 devices in a mesh: tile: 8 (over z, y), row: 4 (over x, core).
Axes of the slice: x: 2, y: 2, z: 4, core: 2. Of those that a mesh axis runs over, the one named last changes fastest.
Arguments:
- intensity: bfloat16 [8, 128, 11264], P('tile', 'row'), may hold values from 0.099609375 to 1
- volume: float32 [64, 128, 256], P('tile', 'row'), may hold values from 0 to 1
- footprint: bfloat16 [8, 256, 256], P('tile'), may hold values from 0.0010681152 to 0.021484375
- foot_offset: int32 [64, 8], replicated, may hold values from 2 to 84, as said below
- tile_count: int32 [8], replicated, may hold values from 1 to 8, as said below
Outputs:
- residual: float32 [8, 128, 11264], P('tile', 'row')
- correction: float32 [64, 128, 256], P('tile', 'row')
Inputs may be any that keep to these rules, and one draw needn't show every extreme that they name: `foot_offset`: slot j belongs to group j // 8. At every angle the offsets of one group's slots differ by at most 3; wherever a group has two or more slots, by exactly 3. `tile_count`: some group has all its slots live.
All inputs are finite; a program needn't handle non-finite values.
Results may differ from a plain program's by a relative error of at most 0.00065.
Values may be sent and summed in bfloat16 or wider, within the bound.
No kernel may reach another device: no remote copies, remote signals or barrier semaphores. Data moves between devices by JAX's collectives and lax.ppermute only.
A program may use at most 128 MiB of HBM per device.

v0:
```python
import jax
import jax.numpy as jnp
import numpy as np
from jax import lax
from jax.sharding import PartitionSpec as P

SPREAD = 4
RIM = 3


decay_length = 2.0
row_floor = 0.5


def with_halo(block, sides, width):
    for axis, dim in sides:
        count = lax.axis_size(axis)
        forward = [(i, i + 1) for i in range(count - 1)]
        backward = [(target, source) for source, target in forward]
        low = lax.ppermute(
            lax.slice_in_dim(block, block.shape[dim] - width, None, axis=dim), axis, forward
        )
        high = lax.ppermute(lax.slice_in_dim(block, 0, width, axis=dim), axis, backward)
        block = jnp.concatenate([low, block, high], axis=dim)
    return block


def smoothing_taps():
    spread_taps = np.exp(-np.abs(np.arange(-RIM, RIM + 1)) / decay_length)
    return spread_taps / spread_taps.sum()


def retrieve_phase(intensity):
    padded = with_halo(intensity, (("row", 1),), RIM)
    tap_weights = smoothing_taps()
    height_rows = intensity.shape[1]
    column_count = intensity.shape[2]
    across = float(tap_weights[0]) * padded[:, 0:height_rows, :].astype(jnp.float32)
    for tap_index in range(1, 2 * RIM + 1):
        across = across + float(tap_weights[tap_index]) * padded[
            :, tap_index : tap_index + height_rows, :
        ].astype(jnp.float32)
    widened = jnp.pad(across, ((0, 0), (0, 0), (RIM, RIM)))
    smoothed = float(tap_weights[0]) * widened[:, :, 0:column_count]
    for tap_index in range(1, 2 * RIM + 1):
        smoothed = (
            smoothed
            + float(tap_weights[tap_index]) * widened[:, :, tap_index : tap_index + column_count]
        )
    return -jnp.log(smoothed)


def live_flags(tile_count, slots_here):
    group_total = tile_count.shape[0]
    slot_ids = jnp.arange(group_total * slots_here, dtype=jnp.int32)
    repeated = jnp.broadcast_to(tile_count[:, None], (group_total, slots_here)).reshape(-1)
    return (slot_ids % slots_here < repeated).astype(jnp.float32)


def row_totals(footprint, offsets_here, live_all, block_count):
    half_cols = footprint.shape[2] // 2
    block_ids = jnp.arange(block_count, dtype=jnp.int32)
    matches = (offsets_here[:, :, None] == block_ids[None, None, :]).astype(jnp.float32)
    counts = jnp.sum(matches * live_all[:, None, None], axis=0)
    voxel_sums = jnp.sum(footprint, axis=1, dtype=jnp.float32)
    leading = counts[:, :, None] * voxel_sums[:, None, :half_cols]
    trailing = counts[:, :, None] * voxel_sums[:, None, half_cols:]
    trailing = jnp.concatenate([jnp.zeros_like(trailing[:, :1]), trailing[:, :-1]], axis=1)
    return (leading + trailing).reshape(counts.shape[0], -1)


def project_loads(load_half, footprint):
    half_cols = footprint.shape[2] // 2
    images = jnp.einsum("abrv,avc->arbc", load_half, footprint, preferred_element_type=jnp.float32)
    leading = images[..., :half_cols]
    trailing = images[..., half_cols:]
    trailing = jnp.concatenate([jnp.zeros_like(trailing[:, :, :1]), trailing[:, :, :-1]], axis=2)
    joined = leading + trailing
    return joined.reshape(joined.shape[0], joined.shape[1], -1)


def back_project(weighted, footprint):
    half_cols = footprint.shape[2] // 2
    halves = weighted.reshape(weighted.shape[0], weighted.shape[1], -1, half_cols)
    nearer = jnp.einsum(
        "arbc,avc->abrv", halves, footprint[:, :, :half_cols], preferred_element_type=jnp.float32
    )
    farther = jnp.einsum(
        "arbc,avc->abrv", halves, footprint[:, :, half_cols:], preferred_element_type=jnp.float32
    )
    farther = jnp.concatenate([farther[:, 1:], jnp.zeros_like(farther[:, :1])], axis=1)
    return nearer + farther


def local(intensity, volume, footprint, foot_offset, tile_count):
    phase_map = retrieve_phase(intensity)
    slots_here = volume.shape[0]
    angles_here = footprint.shape[0]
    half_cols = footprint.shape[2] // 2
    block_count = intensity.shape[2] // half_cols
    member = lax.axis_index("tile")
    live_all = live_flags(tile_count, slots_here)
    live_mine = lax.dynamic_slice_in_dim(live_all, member * slots_here, slots_here)
    masked = volume * live_mine[:, None, None]
    offsets_here = lax.dynamic_slice_in_dim(foot_offset, member * angles_here, angles_here, 1)
    column_sums = lax.psum(jnp.sum(footprint, axis=(0, 2), dtype=jnp.float32), "tile")
    row_sums = row_totals(footprint, offsets_here, live_all, block_count)
    group_total = tile_count.shape[0]
    grouped = foot_offset.reshape(group_total, slots_here, -1)
    starts = jnp.min(grouped, axis=1)
    deltas = lax.dynamic_slice_in_dim(grouped, member, 1, 0)[0] - lax.dynamic_slice_in_dim(
        starts, member, 1, 0
    )
    places = jnp.arange(SPREAD, dtype=jnp.int32)
    picked = (deltas[:, :, None] == places[None, None, :]).astype(jnp.float32)
    outgoing = jnp.einsum("jas,jrv->asrv", picked, masked, precision=lax.Precision.HIGHEST)
    arrived = lax.all_to_all(
        outgoing.astype(jnp.bfloat16), "tile", split_axis=0, concat_axis=1, tiled=True
    ).astype(outgoing.dtype)
    starts_here = lax.dynamic_slice_in_dim(starts, member * angles_here, angles_here, 1)
    targets = (jnp.transpose(starts_here)[:, :, None] + places[None, None, :]).reshape(
        angles_here, -1
    )
    load_blocks = jnp.stack([jax.ops.segment_sum(arrived[0], targets[0], num_segments=block_count)])
    projection = project_loads(load_blocks.astype(jnp.bfloat16), footprint)
    residual = phase_map - projection
    weighted = (residual / jnp.maximum(row_sums, row_floor)[:, None, :]).astype(jnp.bfloat16)
    back_blocks = back_project(weighted, footprint)
    returned = jnp.stack([jnp.take(back_blocks[0], targets[0], axis=0)])
    received = lax.all_to_all(returned, "tile", split_axis=1, concat_axis=0, tiled=True)
    summed = jnp.einsum("jas,asrv->jrv", picked, received, precision=lax.Precision.HIGHEST)
    correction = summed * live_mine[:, None, None] / column_sums[None, None, :]
    return (residual, correction)


def solution(mesh):
    placed = (P("tile", "row", None), P("tile", "row", None), P("tile", None, None), P(), P())
    return jax.shard_map(
        local,
        mesh=mesh,
        in_specs=placed,
        out_specs=(P("tile", "row", None), P("tile", "row", None)),
        check_vma=False,
    )
```

profile of v0, /device:TPU:8, one launch (start us, length us, event | category | flops | bytes accessed | tf_op | source)
XLA Modules:
  0.0 82.8 jit_solution(16312274930662407107)
XLA Ops:
  0.6 0.7 broadcast_in_dim.12
  1.4 0.8 copy.69
  2.3 1.7 %convolution_convert_fusion = bf16[8,4,32,256]{3,0,2,1:T(8,128)(2,1)S(1)} fusion(f32[8,32,256]{2,1,0:T(8,128)} %param.6, f32[8]{0:T(128)S(1)} %dynamic_slice.23, s32[8,8]{1,0:T(8,128)S(1)} %bitcast_subtract_fusion), kind=kOutput, calls=%fused_computation.16 | convolution fusion | flops 25493760 | bytes 786720 | tf_op jit(solution)/shard_map/jas,jrv->asrv/dot_general | solution.py:116
  4.0 0.9 %copy.72 = bf16[8,4,32,256]{3,2,1,0:T(8,128)(2,1)} copy(bf16[8,4,32,256]{3,0,2,1:T(8,128)(2,1)S(1)} %convolution_convert_fusion) | data formatting | bytes 1048576 | tf_op jit(solution)/shard_map/convert_element_type | solution.py:118
  4.9 6.4 %all-to-all-start = ((bf16[8,4,32,256]{3,2,1,0:T(8,128)(2,1)}), bf16[8,4,32,256]{3,2,1,0:T(8,128)(2,1)S(1)}, u32[]{:S(2)}, u32[]{:S(2)}) async-start(bf16[8,4,32,256]{3,2,1,0:T(8,128)(2,1)} %copy.72), calls=%async_computation | async-start | bytes 1048576 | tf_op jit(solution)/shard_map/all_to_all | solution.py:117
  11.4 1.3 %collective-permute-start = (bf16[1,3,11264]{2,1,0:T(4,128)(2,1)S(1)}, bf16[1,3,11264]{2,1,0:T(4,128)(2,1)S(1)}, u32[]{:S(2)}, u32[]{:S(2)}) collective-permute-start(bf16[1,3,11264]{2,1,0:T(4,128)(2,1)S(1)} %get-tuple-element.19), channel_id=1, source_target_pairs={{0,1},{1,2},{2,3},{4,5},{5,6},{6,7},{8,9},{9,10},{10,11},{12,13},{... | collective-permute-start | bytes 202760 | tf_op jit(solution)/shard_map/ppermute | solution.py:20
  12.7 1.3 %collective-permute-start.1 = (bf16[1,3,11264]{2,1,0:T(4,128)(2,1)S(1)}, bf16[1,3,11264]{2,1,0:T(4,128)(2,1)S(1)}, u32[]{:S(2)}, u32[]{:S(2)}) collective-permute-start(bf16[1,3,11264]{2,1,0:T(4,128)(2,1)S(1)} %get-tuple-element.18), channel_id=1, source_target_pairs={{1,0},{2,1},{3,2},{5,4},{6,5},{7,6},{9,8},{10,9},{11,10},{13,12},{... | collective-permute-start | bytes 202760 | tf_op jit(solution)/shard_map/ppermute | solution.py:23
  14.0 0.7 fusion.26
  14.7 0.2 dynamic-slice_reduce_fusion
  15.2 0.1 convert_reduce_fusion
  15.8 1.8 %collective-permute-done.1 = bf16[1,3,11264]{2,1,0:T(4,128)(2,1)S(1)} collective-permute-done((bf16[1,3,11264]{2,1,0:T(4,128)(2,1)S(1)}, bf16[1,3,11264]{2,1,0:T(4,128)(2,1)S(1)}, u32[]{:S(2)}, u32[]{:S(2)}) %collective-permute-start.1) | collective-permute-done | bytes 67616 | tf_op jit(solution)/shard_map/ppermute | solution.py:23
  17.7 2.5 %multiply_add_fusion = f32[1,32,11264]{2,1,0:T(8,128)} fusion(bf16[1,32,11264]{2,1,0:T(8,128)(2,1)S(1)} %copy-done.1, bf16[1,3,11264]{2,1,0:T(4,128)(2,1)S(1)} %collective-permute-done, bf16[1,35,11264]{2,1,0:T(8,128)(2,1)S(1)} %constant_dynamic-update-slice_fusion), kind=kLoop, calls=%fused_computation.15 | loop fusion | flops 10452992 | bytes 4392960 | tf_op jit(solution)/shard_map/add | solution.py:40
  20.2 4.4 %all-to-all-done = bf16[8,4,32,256]{3,2,1,0:T(8,128)(2,1)S(1)} async-done(((bf16[8,4,32,256]{3,2,1,0:T(8,128)(2,1)}), bf16[8,4,32,256]{3,2,1,0:T(8,128)(2,1)S(1)}, u32[]{:S(2)}, u32[]{:S(2)}) %all-to-all-start) | async-done | bytes 524320 | tf_op jit(solution)/shard_map/all_to_all | solution.py:117
  24.6 1.1 %bitcast_convert_fusion = f32[32,32,256]{2,1,0:T(8,128)} fusion(bf16[8,4,32,256]{3,2,1,0:T(8,128)(2,1)S(1)} %all-to-all-done), kind=kLoop, calls=%fused_computation.31 | loop fusion | flops 262144 | bytes 1572864 | tf_op jit(solution)/shard_map/convert_element_type | solution.py:119
  25.7 0.3 broadcast_in_dim.11
  26.0 3.8 %scatter_fusion = f32[88,32,256]{2,1,0:T(8,128)S(1)} fusion(f32[88,32,256]{2,1,0:T(8,128)S(1)} %broadcast_in_dim.11, s32[32]{0:T(128)S(1)} %get-tuple-element.21, f32[32,32,256]{2,1,0:T(8,128)} %bitcast_convert_fusion), kind=kCustom, calls=%fused_computation.1 | custom fusion | flops 262144 | bytes 3145856 | tf_op jit(solution)/shard_map/scatter-add | solution.py:124
  29.8 0.5 convolution_bitcast_fusion.1
  30.4 0.1 slice.107
  30.5 0.2 slice_add_fusion
  30.8 0.8 %copy.73 = f32[1,32,88,128]{3,2,0,1:T(8,128)S(1)} copy(f32[1,32,88,128]{3,1,2,0:T(8,128)S(1)} %slice_add_fusion) | data formatting | bytes 2883584 | tf_op jit(solution)/shard_map/add | solution.py:78
  31.6 0.5 copy-done
  32.1 3.4 %fusion.11 = (bf16[4,8,88,128]{3,1,2,0:T(8,128)(2,1)S(1)}, f32[1,32,11264]{2,1,0:T(8,128)}) fusion(f32[11264]{0:T(1024)S(1)} %maximum_bitcast_fusion, f32[1,32,11264]{2,0,1:T(1,128)S(1)} %bitcast.95, f32[1,32,11264]{2,1,0:T(8,128)S(1)} %copy-done), kind=kLoop, calls=%fused_computation.30 | loop fusion | flops 6127616 | bytes 5091328
  35.6 0.6 convolution_bitcast_fusion
  36.2 0.2 slice.111
  36.4 0.6 fusion
  37.0 0.9 %copy.75 = f32[88,32,256]{2,1,0:T(8,128)S(1)} copy(f32[88,32,256]{2,0,1:T(8,128)S(1)} %fusion) | data formatting | bytes 5767168 | tf_op jit(solution)/shard_map/squeeze | solution.py:129
  37.9 1.6 %gather_fusion = f32[32,32,256]{2,1,0:T(8,128)} fusion(f32[88,32,256]{2,1,0:T(8,128)S(1)} %copy.75, s32[1024]{0:T(1024)S(1)} %pad_clamp_fusion), kind=kCustom, calls=%fused_computation | custom fusion | bytes 2097280 | tf_op jit(solution)/shard_map/jit(_take)/gather | solution.py:129
  39.5 2.4 %fusion.7 = f32[1,32,32,256]{3,2,0,1:T(8,128)} fusion(f32[32,32,256]{2,1,0:T(8,128)} %gather_fusion, pred[32]{0:T(512)(128)(4,1)S(1)} %compare_and_fusion), kind=kLoop, calls=%fused_computation.23 | loop fusion | flops 262144 | bytes 2097184 | tf_op jit(solution)/shard_map/jit(_take)/select_n | solution.py:129
  41.9 4.9 %all-to-all-start.1 = ((f32[1,32,32,256]{3,2,0,1:T(8,128)}), f32[1,32,32,256]{3,2,0,1:T(8,128)S(1)}, u32[]{:S(2)}, u32[]{:S(2)}) async-start(f32[1,32,32,256]{3,2,0,1:T(8,128)} %fusion.7), calls=%async_computation.1 | async-start | bytes 2097152 | tf_op jit(solution)/shard_map/all_to_all | solution.py:130
  46.8 33.8 %psum.7 = f32[256]{0:T(256)S(1)} all-reduce(f32[256]{0:T(256)S(1)} %get-tuple-element.14), channel_id=1, replica_groups=mesh['tile'=8,'row'=4] {'tile'}, use_global_device_ids=true, to_apply=%region_5.6 | all-reduce | flops 256 | bytes 2048 | tf_op jit(solution)/shard_map/psum | solution.py:106
  80.6 1.5 %fusion.6 = f32[8,32,256]{2,0,1:T(8,128)S(1)} fusion(f32[8,4,32,256]{3,2,1,0:T(8,128)S(1)} %bitcast.96, f32[256]{0:T(256)S(1)} %psum.7, f32[8]{0:T(128)S(1)} %dynamic_slice.23, s32[8,8]{1,0:T(8,128)S(1)} %bitcast_subtract_fusion), kind=kOutput, calls=%fused_computation.21 | convolution fusion | flops 25297152 | bytes 1312032 | tf_op jit(solution)/shard_map/jas,asrv->jrv/dot_general | solution.py:131
  82.0 0.8 copy.78
  (31 shorter events, 1.2 us)
Async XLA Ops:
  2.3 9.0 %copy-start.1 = (bf16[1,32,11264]{2,1,0:T(8,128)(2,1)S(1)}, bf16[1,32,11264]{2,1,0:T(8,128)(2,1)}, u32[]{:S(2)}) copy-start(bf16[1,32,11264]{2,1,0:T(8,128)(2,1)} %param.5) | copy-start | bytes 2162692
  4.9 10.3 %copy-start.2 = (bf16[1,256,256]{2,1,0:T(8,128)(2,1)S(1)}, bf16[1,256,256]{2,1,0:T(8,128)(2,1)}, u32[]{:S(2)}) copy-start(bf16[1,256,256]{2,1,0:T(8,128)(2,1)} %param.7) | copy-start | bytes 393220
  4.9 19.6 %all-to-all-start = ((bf16[8,4,32,256]{3,2,1,0:T(8,128)(2,1)}), bf16[8,4,32,256]{3,2,1,0:T(8,128)(2,1)S(1)}, u32[]{:S(2)}, u32[]{:S(2)}) async-start(bf16[8,4,32,256]{3,2,1,0:T(8,128)(2,1)} %copy.72), calls=%async_computation | async-start | bytes 1048576 | tf_op jit(solution)/shard_map/all_to_all | solution.py:117
  11.4 6.3 %collective-permute-start = (bf16[1,3,11264]{2,1,0:T(4,128)(2,1)S(1)}, bf16[1,3,11264]{2,1,0:T(4,128)(2,1)S(1)}, u32[]{:S(2)}, u32[]{:S(2)}) collective-permute-start(bf16[1,3,11264]{2,1,0:T(4,128)(2,1)S(1)} %get-tuple-element.19), channel_id=1, source_target_pairs={{0,1},{1,2},{2,3},{4,5},{5,6},{6,7},{8,9},{9,10},{10,11},{12,13},{... | collective-permute-start | bytes 202760 | tf_op jit(solution)/shard_map/ppermute | solution.py:20
  12.7 4.9 %collective-permute-start.1 = (bf16[1,3,11264]{2,1,0:T(4,128)(2,1)S(1)}, bf16[1,3,11264]{2,1,0:T(4,128)(2,1)S(1)}, u32[]{:S(2)}, u32[]{:S(2)}) collective-permute-start(bf16[1,3,11264]{2,1,0:T(4,128)(2,1)S(1)} %get-tuple-element.18), channel_id=1, source_target_pairs={{1,0},{2,1},{3,2},{5,4},{6,5},{7,6},{9,8},{10,9},{11,10},{13,12},{... | collective-permute-start | bytes 202760 | tf_op jit(solution)/shard_map/ppermute | solution.py:23
  30.7 1.4 %copy-start = (f32[1,32,11264]{2,1,0:T(8,128)S(1)}, f32[1,32,11264]{2,1,0:T(8,128)}, u32[]{:S(2)}) copy-start(f32[1,32,11264]{2,1,0:T(8,128)} %multiply_add_fusion) | copy-start | bytes 4325380
  41.9 38.7 %all-to-all-start.1 = ((f32[1,32,32,256]{3,2,0,1:T(8,128)}), f32[1,32,32,256]{3,2,0,1:T(8,128)S(1)}, u32[]{:S(2)}, u32[]{:S(2)}) async-start(f32[1,32,32,256]{3,2,0,1:T(8,128)} %fusion.7), calls=%async_computation.1 | async-start | bytes 2097152 | tf_op jit(solution)/shard_map/all_to_all | solution.py:130
where the time goes:
time: 83.4 us; the launch traced here: 82.8 us
  blocking collectives  33.8 us (41%)
  starting transfers between devices  13.9 us (17%)
  other arithmetic  13.8 us (17%)
  local copies, waits for them, and re-layouts  9.5 us (11%)
  waiting for transfers between devices  6.21 us (7%)
  matrix products  4.79 us (6%)
  between operations  0.84 us (1%)
    psum x1, blocking collectives, local(): lax.psum(jnp.sum(footprint, axis=(0, 2), dtype=jnp.float32), 'tile')  33.8 us
    all_to_all x1, starting transfers between devices, local(): lax.all_to_all(outgoing.astype(jnp.bfloat16), 'tile', split_axis=0, conca...  6.41 us
    all_to_all x1, starting transfers between devices, local(): lax.all_to_all(returned, 'tile', split_axis=1, concat_axis=0, tiled=True)  4.89 us
    all_to_all x1, waiting for transfers between devices, local(): lax.all_to_all(outgoing.astype(jnp.bfloat16), 'tile', split_axis=0, conca...  4.39 us
    scatter-add x1, other arithmetic, local(): jax.ops.segment_sum(arrived[0], targets[0], num_segments=block_count)  3.77 us
    unnamed x1, other arithmetic  3.4 us
    add x1, other arithmetic, retrieve_phase(): across + float(tap_weights[tap_index]) * padded[:, tap_index:tap_index +...  2.47 us
    select_n x2, other arithmetic, local(): returned = jnp.stack([jnp.take(back_blocks[0], targets[0], axis=0)])  2.36 us
  transfers between devices with their start and end apart: 4, of which 2 were waited for; matrix products, arithmetic and copies ran while one was open for 5% of the time, Pallas kernels for 0%

commit v1 on v0

v1 whole, which is shorter than its diff:
```python
import jax
import jax.numpy as jnp
import numpy as np
from jax import lax
from jax.experimental import pallas as pl
from jax.experimental.pallas import tpu as pltpu
from jax.sharding import PartitionSpec as P


SPREAD = 4
RIM = 3
DIRECT_LIMIT = 16
EXTRA_ROWS = 8
SUM_SCALE = 2048.0
LOW_SCALE = 32000.0
CODE_TOP = 32000.0

decay_length = 2.0
row_floor = 0.5


SMEM = pl.BlockSpec(memory_space=pltpu.SMEM)
VMEM = pl.BlockSpec(memory_space=pltpu.VMEM)


def params(mib):
    return pltpu.CompilerParams(vmem_limit_bytes=mib << 20)


def halo_rows(block, width):
    count = lax.axis_size("row")
    forward = [(i, i + 1) for i in range(count - 1)]
    backward = [(target, source) for source, target in forward]
    rows = block.shape[1]
    low = lax.ppermute(block[:, rows - width :], "row", forward)
    high = lax.ppermute(block[:, :width], "row", backward)
    return low, high


def smoothing_taps():
    spread_taps = np.exp(-np.abs(np.arange(-RIM, RIM + 1)) / decay_length)
    return spread_taps / spread_taps.sum()


def retrieve_phase(intensity):
    low, high = halo_rows(intensity, RIM)
    padded = jnp.concatenate([low, intensity, high], axis=1)
    tap_weights = smoothing_taps()
    height_rows = intensity.shape[1]
    column_count = intensity.shape[2]
    across = float(tap_weights[0]) * padded[:, 0:height_rows, :].astype(jnp.float32)
    for tap_index in range(1, 2 * RIM + 1):
        across = across + float(tap_weights[tap_index]) * padded[
            :, tap_index : tap_index + height_rows, :
        ].astype(jnp.float32)
    widened = jnp.pad(across, ((0, 0), (0, 0), (RIM, RIM)))
    smoothed = float(tap_weights[0]) * widened[:, :, 0:column_count]
    for tap_index in range(1, 2 * RIM + 1):
        smoothed = (
            smoothed
            + float(tap_weights[tap_index]) * widened[:, :, tap_index : tap_index + column_count]
        )
    return -jnp.log(smoothed)


def each_piece(direct, count, member, refs, body):
    if direct:
        for k in range(count):
            body(refs[k], member ^ k)
    else:

        def step(k, carry):
            body(refs[0].at[k], k)
            return carry

        lax.fori_loop(0, count, step, 0)


def group_start(offsets, angle, group, slots):
    low = offsets[angle, group * slots]
    for j in range(1, slots):
        low = jnp.minimum(low, offsets[angle, group * slots + j])
    return low


def load_kernel(direct, count, slots, offsets, tile_count, volume, *pieces):
    member = lax.axis_index("tile")
    live = tile_count[member]

    def one(piece, angle):
        start = group_start(offsets, angle, member, slots)
        places = [offsets[angle, member * slots + j] - start for j in range(slots)]
        places = [jnp.where(j < live, places[j], -1) for j in range(slots)]
        for s in range(SPREAD):
            total = jnp.zeros(volume.shape[1:], jnp.float32)
            for j in range(slots):
                total = total + jnp.where(places[j] == s, 1.0, 0.0) * volume[j]
            piece[s] = total.astype(piece.dtype)

    each_piece(direct, count, member, pieces, one)


def table_kernel(slots, blocks, offsets, tile_count, offset_rows, footprint, inverse, sums):
    member = lax.axis_index("tile")
    half = footprint.shape[1] // 2
    padded = inverse.shape[0]
    total = offset_rows.shape[1]
    table = footprint[...]
    by_column = jnp.sum(table.astype(jnp.float32), axis=0, keepdims=True)
    mine = offset_rows[pl.ds(member, 1), :]
    lane = lax.broadcasted_iota(jnp.int32, (1, total), 1)
    alive = jnp.zeros((1, total), jnp.float32)
    for g in range(total // slots):
        here = (lane >= g * slots) & (lane < g * slots + tile_count[g])
        alive = jnp.where(here, 1.0, alive)
    block = lax.broadcasted_iota(jnp.int32, (padded, total), 0)
    hits = jnp.where(block == mine, alive, 0.0)
    counts = jnp.sum(hits, axis=1, keepdims=True)
    before = jnp.sum(jnp.where(block == mine + 1, alive, 0.0), axis=1, keepdims=True)
    rows = counts * by_column[:, :half] + before * by_column[:, half:]
    inside = lax.broadcasted_iota(jnp.int32, (padded, half), 0) < blocks
    inverse[...] = jnp.where(inside, 1.0 / jnp.maximum(rows, row_floor), 0.0)
    ones = jnp.ones((8, table.shape[1]), table.dtype)
    by_voxel = lax.dot_general(
        ones, table, (((1,), (1,)), ((), ())), preferred_element_type=jnp.float32
    )[0:1]
    scaled = by_voxel * SUM_SCALE
    whole = jnp.floor(scaled)
    low = jnp.floor((scaled - whole) * LOW_SCALE + 0.5)
    packed = jnp.concatenate(
        [whole[:, :half], whole[:, half:], low[:, :half], low[:, half:]], axis=0
    )
    sums[...] = jnp.concatenate([packed, jnp.zeros((4, half), jnp.float32)], axis=0)


def angle_kernel(direct, count, slots, offsets, phase, footprint, inverse, sums, *refs):
    lists = count if direct else 1
    arrived, residual, sent, windows = (
        refs[:lists],
        refs[lists],
        refs[lists + 1 : 2 * lists + 1],
        refs[2 * lists + 1],
    )
    member = lax.axis_index("tile")
    table = footprint[...]
    rows, columns = phase.shape
    voxels = footprint.shape[0]
    half = footprint.shape[1] // 2
    blocks = columns // half
    residual[...] = phase[...]

    def subtract(piece, group):
        start = group_start(offsets, member, group, slots)
        image = jnp.dot(
            piece[...].reshape(SPREAD * rows, voxels), table, preferred_element_type=jnp.float32
        )
        for s in range(SPREAD + 1):
            part = None
            if s < SPREAD:
                part = image[s * rows : (s + 1) * rows, :half]
            if s > 0:
                far = image[(s - 1) * rows : s * rows, half:]
                part = far if part is None else part + far
            block = jnp.minimum(start + s, blocks - 1)
            if s >= SPREAD - 1:
                part = jnp.where(start + s < blocks, part, 0.0)
            at = pl.ds(pl.multiple_of(block * half, half), half)
            residual[:, at] = residual[:, at] - part

    each_piece(direct, count, member, arrived, subtract)

    def send(piece, group):
        start = group_start(offsets, member, group, slots)
        for s in range(SPREAD + 1):
            block = jnp.minimum(start + s, blocks - 1)
            at = pl.ds(pl.multiple_of(block * half, half), half)
            scale = inverse[pl.ds(start + s, 1), :]
            windows[:, s * half : (s + 1) * half] = (residual[:, at] * scale).astype(windows.dtype)
        stacked = jnp.concatenate(
            [windows[:, s * half : (s + 2) * half] for s in range(SPREAD)], axis=0
        )
        back = lax.dot_general(
            stacked, table, (((1,), (1,)), ((), ())), preferred_element_type=jnp.float32
        )
        top = jnp.max(jnp.max(jnp.abs(back), axis=1, keepdims=True), axis=0, keepdims=True)
        power = jnp.floor(jnp.log2(CODE_TOP / jnp.maximum(top, 1e-30)))
        code = jnp.round(back * jnp.exp2(power)).astype(jnp.int32)
        for s in range(SPREAD):
            for h in range(2):
                base = (2 * s + h) * rows
                piece[base : base + rows, :] = code[
                    s * rows : (s + 1) * rows, h * half : (h + 1) * half
                ].astype(piece.dtype)
        base = 2 * SPREAD * rows
        line = lax.broadcasted_iota(jnp.int32, (EXTRA_ROWS, half), 0)
        extra = jnp.where(line < 4, sums[...], jnp.broadcast_to(power, (EXTRA_ROWS, half)))
        piece[base : base + EXTRA_ROWS, :] = extra.astype(jnp.int32).astype(piece.dtype)

    each_piece(direct, count, member, sent, send)


def gather_kernel(direct, count, slots, rows, offsets, tile_count, *refs):
    lists = count if direct else 1
    received, correction, decoded, column_sums = (
        refs[:lists],
        refs[lists],
        refs[lists + 1],
        refs[lists + 2],
    )
    member = lax.axis_index("tile")
    live = tile_count[member]
    half = column_sums.shape[1]
    base = 2 * SPREAD * rows
    column_sums[...] = jnp.zeros_like(column_sums)
    correction[...] = jnp.zeros_like(correction)

    def one(piece, angle):
        extra = piece[base : base + EXTRA_ROWS, :].astype(jnp.float32)
        column_sums[...] += (extra[0:2] + extra[2:4] * (1.0 / LOW_SCALE)) * (1.0 / SUM_SCALE)
        scale = jnp.exp2(-extra[4:5])
        start = group_start(offsets, angle, member, slots)
        decoded[...] = piece[0:base, :].astype(jnp.float32) * scale
        for j in range(slots):
            place = offsets[angle, member * slots + j] - start
            at = pl.multiple_of(place * (2 * rows), 2 * rows)
            for h in range(2):
                correction[j, :, h * half : (h + 1) * half] += decoded[
                    pl.ds(at + h * rows, rows), :
                ]

    each_piece(direct, count, member, received, one)
    inverse = 1.0 / column_sums[...]
    for j in range(slots):
        weight = jnp.where(j < live, 1.0, 0.0)
        for h in range(2):
            part = correction[j, :, h * half : (h + 1) * half]
            correction[j, :, h * half : (h + 1) * half] = part * (inverse[h : h + 1] * weight)


def exchange(direct, count, pieces):
    if not direct:
        return [lax.all_to_all(pieces[0], "tile", split_axis=0, concat_axis=0, tiled=True)]
    arrived = [pieces[0]]
    for k in range(1, count):
        arrived.append(lax.ppermute(pieces[k], "tile", [(i, i ^ k) for i in range(count)]))
    return arrived


def use_direct(count):
    return count <= DIRECT_LIMIT and count & (count - 1) == 0


def local(intensity, volume, footprint, foot_offset, tile_count):
    count = lax.axis_size("tile")
    direct = use_direct(count)
    slots, rows, voxels = volume.shape
    angles_here, _, window = footprint.shape
    assert angles_here == 1
    half = window // 2
    columns = intensity.shape[2]
    blocks = columns // half
    padded_blocks = -(-(blocks + SPREAD + 1) // 8) * 8
    offsets = jnp.transpose(foot_offset)
    table = footprint[0]

    def piece_shapes(shape, dtype):
        if direct:
            return [jax.ShapeDtypeStruct(shape, dtype)] * count
        return [jax.ShapeDtypeStruct((count,) + shape, dtype)]

    load_shapes = piece_shapes((SPREAD, rows, voxels), jnp.bfloat16)
    loads = pl.pallas_call(
        lambda *refs: load_kernel(direct, count, slots, *refs),
        out_shape=load_shapes,
        in_specs=[SMEM, SMEM, VMEM],
        out_specs=[VMEM] * len(load_shapes),
        compiler_params=params(16),
        name="loads",
    )(offsets, tile_count, volume)
    arrived = exchange(direct, count, loads)

    phase_map = retrieve_phase(intensity)[0]
    inverse, sums = pl.pallas_call(
        lambda *refs: table_kernel(slots, blocks, *refs),
        out_shape=[
            jax.ShapeDtypeStruct((padded_blocks, half), jnp.float32),
            jax.ShapeDtypeStruct((EXTRA_ROWS, half), jnp.float32),
        ],
        in_specs=[SMEM, SMEM, VMEM, VMEM],
        out_specs=[VMEM, VMEM],
        compiler_params=params(16),
        name="tables",
    )(offsets, tile_count, offsets, table)

    back_shapes = piece_shapes((2 * SPREAD * rows + EXTRA_ROWS, half), jnp.int16)
    residual, *backs = pl.pallas_call(
        lambda *refs: angle_kernel(direct, count, slots, *refs),
        out_shape=[jax.ShapeDtypeStruct((rows, columns), jnp.float32)] + back_shapes,
        in_specs=[SMEM] + [VMEM] * (4 + len(arrived)),
        out_specs=[VMEM] * (1 + len(back_shapes)),
        scratch_shapes=[pltpu.VMEM((rows, (SPREAD + 1) * half), jnp.bfloat16)],
        compiler_params=params(24),
        name="angle",
    )(offsets, phase_map, table, inverse, sums, *arrived)
    received = exchange(direct, count, backs)

    correction = pl.pallas_call(
        lambda *refs: gather_kernel(direct, count, slots, rows, *refs),
        out_shape=jax.ShapeDtypeStruct((slots, rows, voxels), jnp.float32),
        in_specs=[SMEM, SMEM] + [VMEM] * len(received),
        out_specs=VMEM,
        scratch_shapes=[
            pltpu.VMEM((2 * SPREAD * rows, half), jnp.float32),
            pltpu.VMEM((2, half), jnp.float32),
        ],
        compiler_params=params(16),
        name="gather",
    )(offsets, tile_count, *received)
    return residual[None], correction


def solution(mesh):
    placed = (P("tile", "row", None), P("tile", "row", None), P("tile", None, None), P(), P())
    return jax.shard_map(
        local,
        mesh=mesh,
        in_specs=placed,
        out_specs=(P("tile", "row", None), P("tile", "row", None)),
        check_vma=False,
    )
```

time: 83.4 us -> 53.5 us (0.64)
  blocking collectives: 33.8 us -> 0 us
  starting transfers between devices: 13.9 us -> 24.6 us
  other arithmetic: 13.8 us -> 3.67 us
  waiting for transfers between devices: 6.21 us -> 13.2 us
  Pallas kernels: 0 us -> 6.38 us
  local copies, waits for them, and re-layouts: 9.5 us -> 4.64 us
  matrix products: 4.79 us -> 0 us
    psum x1 -> x0, blocking collectives: 33.8 us -> none  [local(): lax.psum(jnp.sum(footprint, axis=(0, 2), dtype=jnp.float32), 'tile')]
    ppermute x2 -> x16, starting transfers between devices: 2.59 us -> 24.6 us  [the longest x14 20.3 us: exchange(): lax.ppermute(pieces[k], 'tile', [(i, i ^ k) for i in range(count)])]
    ppermute x2 -> x16, waiting for transfers between devices: 1.82 us -> 13.2 us  [the longest x14 13.2 us: exchange(): lax.ppermute(pieces[k], 'tile', [(i, i ^ k) for i in range(count)])]
    all_to_all x2 -> x0, starting transfers between devices: 11.3 us -> none  [the longest x1 6.41 us: local(): lax.all_to_all(outgoing.astype(jnp.bfloat16), 'tile', split_axis=0, conca...]
    pallas_call x0 -> x4, Pallas kernels: none -> 6.38 us  [the longest x1 2.66 us: local(): pl.pallas_call(lambda *refs: angle_kernel(direct, count, slots, *refs), o...]
    dot_general x5 -> x0, matrix products: 4.79 us -> none  [the longest x1 1.66 us: local(): jnp.einsum('jas,jrv->asrv', picked, masked, precision=lax.Precision.HIGHEST)]
    all_to_all x2 -> x0, waiting for transfers between devices: 4.39 us -> none  [the longest x1 4.39 us: local(): lax.all_to_all(outgoing.astype(jnp.bfloat16), 'tile', split_axis=0, conca...]
    scatter-add x1 -> x0, other arithmetic: 3.77 us -> none  [local(): jax.ops.segment_sum(arrived[0], targets[0], num_segments=block_count)]
  transfers between devices with their start and end apart: 4 -> 16, of which waited for: 2 -> 6; matrix products, arithmetic and copies ran while one was open for 5% -> 9% of each run, Pallas kernels for 0% -> 4%
where the time goes in v1:
time: 53.5 us; the launch traced here: 53.2 us
  starting transfers between devices  24.6 us (46%)
  waiting for transfers between devices  13.2 us (25%)
  Pallas kernels  6.38 us (12%)
  local copies, waits for them, and re-layouts  4.64 us (9%)
  other arithmetic  3.67 us (7%)
  between operations  0.78 us (1%)
    ppermute x14, starting transfers between devices, exchange(): lax.ppermute(pieces[k], 'tile', [(i, i ^ k) for i in range(count)])  20.3 us
    ppermute x14, waiting for transfers between devices, exchange(): lax.ppermute(pieces[k], 'tile', [(i, i ^ k) for i in range(count)])  13.2 us
    unnamed x15, local copies, waits for them, and re-layouts  3.46 us
    ppermute x1, starting transfers between devices, halo_rows(): low = lax.ppermute(block[:, rows - width:], 'row', forward)  3.04 us
    pallas_call x1, Pallas kernels, local(): pl.pallas_call(lambda *refs: angle_kernel(direct, count, slots, *refs), o...  2.66 us
    squeeze x1, other arithmetic, local(): phase_map = retrieve_phase(intensity)[0]  2.3 us
    pallas_call x1, Pallas kernels, local(): pl.pallas_call(lambda *refs: gather_kernel(direct, count, slots, rows, *r...  1.71 us
    add x1, other arithmetic, retrieve_phase(): across + float(tap_weights[tap_index]) * padded[:, tap_index:tap_index +...  1.37 us
  transfers between devices with their start and end apart: 16, of which 6 were waited for; matrix products, arithmetic and copies ran while one was open for 9% of the time, Pallas kernels for 4%

profile of v1, /device:TPU:8, one launch (start us, length us, event | category | flops | bytes accessed | tf_op | source)
XLA Modules:
  0.0 53.2 jit_solution(17055624159643829721)
XLA Ops:
  0.6 1.1 %fusion.5 = (bf16[1,3,11264]{2,1,0:T(4,128)(2,1)S(1)}, bf16[1,3,11264]{2,1,0:T(4,128)(2,1)S(1)}) fusion(bf16[1,32,11264]{2,1,0:T(8,128)(2,1)} %param.5), kind=kLoop, calls=%fused_computation.16 | loop fusion | bytes 270336 | tf_op jit(solution)/shard_map/slice | solution.py:36
  1.8 1.3 %collective-permute-start.1 = (bf16[1,3,11264]{2,1,0:T(4,128)(2,1)S(1)}, bf16[1,3,11264]{2,1,0:T(4,128)(2,1)S(1)}, u32[]{:S(2)}, u32[]{:S(2)}) collective-permute-start(bf16[1,3,11264]{2,1,0:T(4,128)(2,1)S(1)} %get-tuple-element.40), channel_id=1, source_target_pairs={{1,0},{2,1},{3,2},{5,4},{6,5},{7,6},{9,8},{10,9},{11,10},{13,12},{... | collective-permute-start | bytes 202760 | tf_op jit(solution)/shard_map/ppermute | solution.py:36
  3.1 3.0 %collective-permute-start = (bf16[1,3,11264]{2,1,0:T(4,128)(2,1)S(1)}, bf16[1,3,11264]{2,1,0:T(4,128)(2,1)S(1)}, u32[]{:S(2)}, u32[]{:S(2)}) collective-permute-start(bf16[1,3,11264]{2,1,0:T(4,128)(2,1)S(1)} %get-tuple-element.41), channel_id=1, source_target_pairs={{0,1},{1,2},{2,3},{4,5},{5,6},{6,7},{8,9},{9,10},{10,11},{12,13},{... | collective-permute-start | bytes 202760 | tf_op jit(solution)/shard_map/ppermute | solution.py:35
  6.1 0.9 %copy-done.1 = f32[8,32,256]{2,1,0:T(8,128)S(1)} copy-done((f32[8,32,256]{2,1,0:T(8,128)S(1)}, f32[8,32,256]{2,1,0:T(8,128)}, u32[]{:S(2)}) %copy-start.1) | copy-done | bytes 262168
  7.1 0.7 %copy-done.2 = s32[64,8]{0,1:T(8,128)S(1)} copy-done((s32[64,8]{0,1:T(8,128)S(1)}, s32[64,8]{0,1:T(8,128)}, u32[]{:S(2)}) %copy-start.2) | copy-done | bytes 2072
  7.7 0.7 %copy-done.4 = s32[8]{0:T(128)S(1)} copy-done((s32[8]{0:T(128)S(1)}, s32[8]{0:T(128)}, u32[]{:S(2)}) %copy-start.4) | copy-done | bytes 56
  8.4 1.2 %loads.1 = (bf16[4,32,256]{2,1,0:T(8,128)(2,1)S(1)}, bf16[4,32,256]{2,1,0:T(8,128)(2,1)S(1)}, bf16[4,32,256]{2,1,0:T(8,128)(2,1)S(1)}, bf16[4,32,256]{2,1,0:T(8,...) custom-call(s32[8,64]{1,0:T(8,128)S(1)} %bitcast.7, ...), custom_call_target="tpu_custom_call" | custom-call | tf_op jit(solution)/shard_map/loads/pallas_call | solution.py:272
  9.6 1.6 %collective-permute-start.2 = (bf16[4,32,256]{2,1,0:T(8,128)(2,1)S(1)}, bf16[4,32,256]{2,1,0:T(8,128)(2,1)S(1)}, u32[]{:S(2)}, u32[]{:S(2)}) collective-permute-start(bf16[4,32,256]{2,1,0:T(8,128)(2,1)S(1)} %get-tuple-element.24), channel_id=1, source_target_pairs={{0,4},{4,0},{8,12},{12,8},{16,20},{20,16},{24,28},{28,24},{1,5},{5... | collective-permute-start | bytes 196616 | tf_op jit(solution)/shard_map/ppermute | solution.py:245
  11.2 0.4 collective-permute-start.3
  11.7 1.5 %collective-permute-start.4 = (bf16[4,32,256]{2,1,0:T(8,128)(2,1)S(1)}, bf16[4,32,256]{2,1,0:T(8,128)(2,1)S(1)}, u32[]{:S(2)}, u32[]{:S(2)}) collective-permute-start(bf16[4,32,256]{2,1,0:T(8,128)(2,1)S(1)} %get-tuple-element.26), channel_id=1, source_target_pairs={{0,12},{4,8},{8,4},{12,0},{16,28},{20,24},{24,20},{28,16},{1,13},{... | collective-permute-start | bytes 196616 | tf_op jit(solution)/shard_map/ppermute | solution.py:245
  13.2 1.2 %constant_dynamic-update-slice_fusion.1 = bf16[1,35,11264]{2,1,0:T(8,128)(2,1)S(1)} fusion(bf16[1,32,11264]{2,1,0:T(8,128)(2,1)} %param.5), kind=kLoop, calls=%fused_computation.15 | loop fusion | bytes 1441792
  14.4 0.8 %tables.1 = (f32[96,128]{1,0:T(8,128)S(1)}, f32[8,128]{1,0:T(8,128)S(1)}) custom-call(s32[8,64]{1,0:T(8,128)S(1)} %bitcast.8, s32[8]{0:T(128)S(1)} %copy-done.4, s32[8,64]{1,0:T(8,128)S(1)} %bitcast.9, bf16[256,256]{1,0:T(8,128)(2,1)S(1)} %bitcast.5), custom_call_target="tpu_custom_call" | custom-call | tf_op jit(solution)/shard_map/tables/pallas_call | solution.py:283
  15.2 2.7 %collective-permute-start.5 = (bf16[4,32,256]{2,1,0:T(8,128)(2,1)S(1)}, bf16[4,32,256]{2,1,0:T(8,128)(2,1)S(1)}, u32[]{:S(2)}, u32[]{:S(2)}) collective-permute-start(bf16[4,32,256]{2,1,0:T(8,128)(2,1)S(1)} %get-tuple-element.27), channel_id=1, source_target_pairs={{0,16},{4,20},{8,24},{12,28},{16,0},{20,4},{24,8},{28,12},{1,17},{... | collective-permute-start | bytes 196616 | tf_op jit(solution)/shard_map/ppermute | solution.py:245
  17.9 1.4 %collective-permute-start.6 = (bf16[4,32,256]{2,1,0:T(8,128)(2,1)S(1)}, bf16[4,32,256]{2,1,0:T(8,128)(2,1)S(1)}, u32[]{:S(2)}, u32[]{:S(2)}) collective-permute-start(bf16[4,32,256]{2,1,0:T(8,128)(2,1)S(1)} %get-tuple-element.28), channel_id=1, source_target_pairs={{0,20},{4,16},{8,28},{12,24},{16,4},{20,0},{24,12},{28,8},{1,21},{... | collective-permute-start | bytes 196616 | tf_op jit(solution)/shard_map/ppermute | solution.py:245
  19.3 1.4 %multiply_add_fusion = f32[1,32,11264]{2,1,0:T(8,128)S(1)} fusion(bf16[1,32,11264]{2,1,0:T(8,128)(2,1)S(1)} %copy-done.6, bf16[1,3,11264]{2,1,0:T(4,128)(2,1)S(1)} %collective-permute-done, bf16[1,35,11264]{2,1,0:T(8,128)(2,1)S(1)} %constant_dynamic-update-slice_fusion), kind=kLoop, calls=%fused_computation.6 | loop fusion | flops 10452992 | bytes 4392960 | tf_op jit(solution)/shard_map/add | solution.py:53
  20.6 1.6 %collective-permute-start.7 = (bf16[4,32,256]{2,1,0:T(8,128)(2,1)S(1)}, bf16[4,32,256]{2,1,0:T(8,128)(2,1)S(1)}, u32[]{:S(2)}, u32[]{:S(2)}) collective-permute-start(bf16[4,32,256]{2,1,0:T(8,128)(2,1)S(1)} %get-tuple-element.29), channel_id=1, source_target_pairs={{0,24},{4,28},{8,16},{12,20},{16,8},{20,12},{24,0},{28,4},{1,25},{... | collective-permute-start | bytes 196616 | tf_op jit(solution)/shard_map/ppermute | solution.py:245
  22.7 2.3 %negate_bitcast_fusion.refs_1_ = f32[32,11264]{1,0:T(8,128)S(1)} fusion(f32[1,32,11264]{2,1,0:T(8,128)S(1)} %multiply_add_fusion), kind=kLoop, calls=%fused_computation | loop fusion | flops 5046272 | bytes 2883584 | tf_op jit(solution)/shard_map/squeeze | solution.py:282
  25.0 3.5 %collective-permute-done.7.refs_11_ = bf16[4,32,256]{2,1,0:T(8,128)(2,1)S(1)} collective-permute-done((bf16[4,32,256]{2,1,0:T(8,128)(2,1)S(1)}, bf16[4,32,256]{2,1,0:T(8,128)(2,1)S(1)}, u32[]{:S(2)}, u32[]{:S(2)}) %collective-permute-start.7) | collective-permute-done | bytes 65568 | tf_op jit(solution)/shard_map/ppermute | solution.py:245
  28.6 0.9 %collective-permute-done.8.refs_12_ = bf16[4,32,256]{2,1,0:T(8,128)(2,1)S(1)} collective-permute-done((bf16[4,32,256]{2,1,0:T(8,128)(2,1)S(1)}, bf16[4,32,256]{2,1,0:T(8,128)(2,1)S(1)}, u32[]{:S(2)}, u32[]{:S(2)}) %collective-permute-start.8) | collective-permute-done | bytes 65568 | tf_op jit(solution)/shard_map/ppermute | solution.py:245
  29.5 2.7 %angle.1 = (f32[32,11264]{1,0:T(8,128)}, s16[264,128]{1,0:T(8,128)(2,1)S(1)}, s16[264,128]{1,0:T(8,128)(2,1)S(1)}, s16[264,128]{1,0:T(8,128)(2,1)S(1)}, s16[264,...) custom-call(s32[8,64]{1,0:T(8,128)S(1)} %bitcast.10, ...), custom_call_target="tpu_custom_call" | custom-call | tf_op jit(solution)/shard_map/angle/pallas_call | solution.py:296
  32.1 2.1 %collective-permute-start.9 = (s16[264,128]{1,0:T(8,128)(2,1)S(1)}, s16[264,128]{1,0:T(8,128)(2,1)S(1)}, u32[]{:S(2)}, u32[]{:S(2)}) collective-permute-start(s16[264,128]{1,0:T(8,128)(2,1)S(1)} %get-tuple-element.33), channel_id=1, source_target_pairs={{0,4},{4,0},{8,12},{12,8},{16,20},{20,16},{24,28},{28,24},{1,5},{5... | collective-permute-start | bytes 202760 | tf_op jit(solution)/shard_map/ppermute | solution.py:245
  34.2 0.8 %collective-permute-start.10 = (s16[264,128]{1,0:T(8,128)(2,1)S(1)}, s16[264,128]{1,0:T(8,128)(2,1)S(1)}, u32[]{:S(2)}, u32[]{:S(2)}) collective-permute-start(s16[264,128]{1,0:T(8,128)(2,1)S(1)} %get-tuple-element.34), channel_id=1, source_target_pairs={{0,8},{4,12},{8,0},{12,4},{16,24},{20,28},{24,16},{28,20},{1,9},{5... | collective-permute-start | bytes 202760 | tf_op jit(solution)/shard_map/ppermute | solution.py:245
  35.0 0.9 %collective-permute-start.11 = (s16[264,128]{1,0:T(8,128)(2,1)S(1)}, s16[264,128]{1,0:T(8,128)(2,1)S(1)}, u32[]{:S(2)}, u32[]{:S(2)}) collective-permute-start(s16[264,128]{1,0:T(8,128)(2,1)S(1)} %get-tuple-element.35), channel_id=1, source_target_pairs={{0,12},{4,8},{8,4},{12,0},{16,28},{20,24},{24,20},{28,16},{1,13},{... | collective-permute-start | bytes 202760 | tf_op jit(solution)/shard_map/ppermute | solution.py:245
  35.9 2.5 %collective-permute-start.12 = (s16[264,128]{1,0:T(8,128)(2,1)S(1)}, s16[264,128]{1,0:T(8,128)(2,1)S(1)}, u32[]{:S(2)}, u32[]{:S(2)}) collective-permute-start(s16[264,128]{1,0:T(8,128)(2,1)S(1)} %get-tuple-element.36), channel_id=1, source_target_pairs={{0,16},{4,20},{8,24},{12,28},{16,0},{20,4},{24,8},{28,12},{1,17},{... | collective-permute-start | bytes 202760 | tf_op jit(solution)/shard_map/ppermute | solution.py:245
  38.3 1.7 %collective-permute-start.13 = (s16[264,128]{1,0:T(8,128)(2,1)S(1)}, s16[264,128]{1,0:T(8,128)(2,1)S(1)}, u32[]{:S(2)}, u32[]{:S(2)}) collective-permute-start(s16[264,128]{1,0:T(8,128)(2,1)S(1)} %get-tuple-element.37), channel_id=1, source_target_pairs={{0,20},{4,16},{8,28},{12,24},{16,4},{20,0},{24,12},{28,8},{1,21},{... | collective-permute-start | bytes 202760 | tf_op jit(solution)/shard_map/ppermute | solution.py:245
  40.1 1.7 %collective-permute-start.14 = (s16[264,128]{1,0:T(8,128)(2,1)S(1)}, s16[264,128]{1,0:T(8,128)(2,1)S(1)}, u32[]{:S(2)}, u32[]{:S(2)}) collective-permute-start(s16[264,128]{1,0:T(8,128)(2,1)S(1)} %get-tuple-element.38), channel_id=1, source_target_pairs={{0,24},{4,28},{8,16},{12,20},{16,8},{20,12},{24,0},{28,4},{1,25},{... | collective-permute-start | bytes 202760 | tf_op jit(solution)/shard_map/ppermute | solution.py:245
  41.8 1.0 %collective-permute-start.15 = (s16[264,128]{1,0:T(8,128)(2,1)S(1)}, s16[264,128]{1,0:T(8,128)(2,1)S(1)}, u32[]{:S(2)}, u32[]{:S(2)}) collective-permute-start(s16[264,128]{1,0:T(8,128)(2,1)S(1)} %get-tuple-element.39), channel_id=1, source_target_pairs={{0,28},{4,24},{8,20},{12,16},{16,12},{20,8},{24,4},{28,0},{1,29},{... | collective-permute-start | bytes 202760 | tf_op jit(solution)/shard_map/ppermute | solution.py:245
  42.8 2.9 %collective-permute-done.12.refs_6_ = s16[264,128]{1,0:T(8,128)(2,1)S(1)} collective-permute-done((s16[264,128]{1,0:T(8,128)(2,1)S(1)}, s16[264,128]{1,0:T(8,128)(2,1)S(1)}, u32[]{:S(2)}, u32[]{:S(2)}) %collective-permute-start.12) | collective-permute-done | bytes 67616 | tf_op jit(solution)/shard_map/ppermute | solution.py:245
  45.7 2.2 %collective-permute-done.13.refs_7_ = s16[264,128]{1,0:T(8,128)(2,1)S(1)} collective-permute-done((s16[264,128]{1,0:T(8,128)(2,1)S(1)}, s16[264,128]{1,0:T(8,128)(2,1)S(1)}, u32[]{:S(2)}, u32[]{:S(2)}) %collective-permute-start.13) | collective-permute-done | bytes 67616 | tf_op jit(solution)/shard_map/ppermute | solution.py:245
  47.9 2.4 %collective-permute-done.14.refs_8_ = s16[264,128]{1,0:T(8,128)(2,1)S(1)} collective-permute-done((s16[264,128]{1,0:T(8,128)(2,1)S(1)}, s16[264,128]{1,0:T(8,128)(2,1)S(1)}, u32[]{:S(2)}, u32[]{:S(2)}) %collective-permute-start.14) | collective-permute-done | bytes 67616 | tf_op jit(solution)/shard_map/ppermute | solution.py:245
  50.3 1.2 %collective-permute-done.15.refs_9_ = s16[264,128]{1,0:T(8,128)(2,1)S(1)} collective-permute-done((s16[264,128]{1,0:T(8,128)(2,1)S(1)}, s16[264,128]{1,0:T(8,128)(2,1)S(1)}, u32[]{:S(2)}, u32[]{:S(2)}) %collective-permute-start.15) | collective-permute-done | bytes 67616 | tf_op jit(solution)/shard_map/ppermute | solution.py:245
  51.5 1.7 %gather.1 = f32[8,32,256]{2,1,0:T(8,128)} custom-call(s32[8,64]{1,0:T(8,128)S(1)} %bitcast.11, s32[8]{0:T(128)S(1)} %copy-done.5, s16[264,128]{1,0:T(8,128)(2,1)S(1)} %get-tuple-element.32.refs_2_, s16[264,128]{1,0:T(8,128)(2,1)S(1)} %collective-permute-done.9.refs_3_, s16[264,128]{1,0:T(8,128)(2,1)S(1)} %collective-permute-done.10.refs_4_, ...), custom_call_target="tpu_custom_call" | custom-call | tf_op jit(solution)/shard_map/gather/pallas_call | solution.py:307
  (23 shorter events, 0.5 us)
Async XLA Ops:
  0.6 13.7 %copy-start = (bf16[1,256,256]{2,1,0:T(8,128)(2,1)S(1)}, bf16[1,256,256]{2,1,0:T(8,128)(2,1)}, u32[]{:S(2)}) copy-start(bf16[1,256,256]{2,1,0:T(8,128)(2,1)} %param.7) | copy-start | bytes 393220
  1.8 13.4 %collective-permute-start.1 = (bf16[1,3,11264]{2,1,0:T(4,128)(2,1)S(1)}, bf16[1,3,11264]{2,1,0:T(4,128)(2,1)S(1)}, u32[]{:S(2)}, u32[]{:S(2)}) collective-permute-start(bf16[1,3,11264]{2,1,0:T(4,128)(2,1)S(1)} %get-tuple-element.40), channel_id=1, source_target_pairs={{1,0},{2,1},{3,2},{5,4},{6,5},{7,6},{9,8},{10,9},{11,10},{13,12},{... | collective-permute-start | bytes 202760 | tf_op jit(solution)/shard_map/ppermute | solution.py:36
  3.1 14.8 %collective-permute-start = (bf16[1,3,11264]{2,1,0:T(4,128)(2,1)S(1)}, bf16[1,3,11264]{2,1,0:T(4,128)(2,1)S(1)}, u32[]{:S(2)}, u32[]{:S(2)}) collective-permute-start(bf16[1,3,11264]{2,1,0:T(4,128)(2,1)S(1)} %get-tuple-element.41), channel_id=1, source_target_pairs={{0,1},{1,2},{2,3},{4,5},{5,6},{6,7},{8,9},{9,10},{10,11},{12,13},{... | collective-permute-start | bytes 202760 | tf_op jit(solution)/shard_map/ppermute | solution.py:35
  6.1 1.0 %copy-start.1 = (f32[8,32,256]{2,1,0:T(8,128)S(1)}, f32[8,32,256]{2,1,0:T(8,128)}, u32[]{:S(2)}) copy-start(f32[8,32,256]{2,1,0:T(8,128)} %refs_2_.1) | copy-start | bytes 786436
  7.1 0.7 %copy-start.2 = (s32[64,8]{0,1:T(8,128)S(1)}, s32[64,8]{0,1:T(8,128)}, u32[]{:S(2)}) copy-start(s32[64,8]{0,1:T(8,128)} %param.8) | copy-start | bytes 6148
  7.7 0.7 %copy-start.4 = (s32[8]{0:T(128)S(1)}, s32[8]{0:T(128)}, u32[]{:S(2)}) copy-start(s32[8]{0:T(128)} %refs_1_.5) | copy-start | bytes 100
  8.4 10.8 %copy-start.6 = (bf16[1,32,11264]{2,1,0:T(8,128)(2,1)S(1)}, bf16[1,32,11264]{2,1,0:T(8,128)(2,1)}, u32[]{:S(2)}) copy-start(bf16[1,32,11264]{2,1,0:T(8,128)(2,1)} %param.5) | copy-start | bytes 2162692
  9.6 11.0 %collective-permute-start.2 = (bf16[4,32,256]{2,1,0:T(8,128)(2,1)S(1)}, bf16[4,32,256]{2,1,0:T(8,128)(2,1)S(1)}, u32[]{:S(2)}, u32[]{:S(2)}) collective-permute-start(bf16[4,32,256]{2,1,0:T(8,128)(2,1)S(1)} %get-tuple-element.24), channel_id=1, source_target_pairs={{0,4},{4,0},{8,12},{12,8},{16,20},{20,16},{24,28},{28,24},{1,5},{5... | collective-permute-start | bytes 196616 | tf_op jit(solution)/shard_map/ppermute | solution.py:245
  11.2 11.1 %collective-permute-start.3 = (bf16[4,32,256]{2,1,0:T(8,128)(2,1)S(1)}, bf16[4,32,256]{2,1,0:T(8,128)(2,1)S(1)}, u32[]{:S(2)}, u32[]{:S(2)}) collective-permute-start(bf16[4,32,256]{2,1,0:T(8,128)(2,1)S(1)} %get-tuple-element.25), channel_id=1, source_target_pairs={{0,8},{4,12},{8,0},{12,4},{16,24},{20,28},{24,16},{28,20},{1,9},{5... | collective-permute-start | bytes 196616 | tf_op jit(solution)/shard_map/ppermute | solution.py:245
  11.7 13.3 %collective-permute-start.4 = (bf16[4,32,256]{2,1,0:T(8,128)(2,1)S(1)}, bf16[4,32,256]{2,1,0:T(8,128)(2,1)S(1)}, u32[]{:S(2)}, u32[]{:S(2)}) collective-permute-start(bf16[4,32,256]{2,1,0:T(8,128)(2,1)S(1)} %get-tuple-element.26), channel_id=1, source_target_pairs={{0,12},{4,8},{8,4},{12,0},{16,28},{20,24},{24,20},{28,16},{1,13},{... | collective-permute-start | bytes 196616 | tf_op jit(solution)/shard_map/ppermute | solution.py:245
  15.2 9.8 %collective-permute-start.5 = (bf16[4,32,256]{2,1,0:T(8,128)(2,1)S(1)}, bf16[4,32,256]{2,1,0:T(8,128)(2,1)S(1)}, u32[]{:S(2)}, u32[]{:S(2)}) collective-permute-start(bf16[4,32,256]{2,1,0:T(8,128)(2,1)S(1)} %get-tuple-element.27), channel_id=1, source_target_pairs={{0,16},{4,20},{8,24},{12,28},{16,0},{20,4},{24,8},{28,12},{1,17},{... | collective-permute-start | bytes 196616 | tf_op jit(solution)/shard_map/ppermute | solution.py:245
  17.9 7.1 %collective-permute-start.6 = (bf16[4,32,256]{2,1,0:T(8,128)(2,1)S(1)}, bf16[4,32,256]{2,1,0:T(8,128)(2,1)S(1)}, u32[]{:S(2)}, u32[]{:S(2)}) collective-permute-start(bf16[4,32,256]{2,1,0:T(8,128)(2,1)S(1)} %get-tuple-element.28), channel_id=1, source_target_pairs={{0,20},{4,16},{8,28},{12,24},{16,4},{20,0},{24,12},{28,8},{1,21},{... | collective-permute-start | bytes 196616 | tf_op jit(solution)/shard_map/ppermute | solution.py:245
  20.6 7.9 %collective-permute-start.7 = (bf16[4,32,256]{2,1,0:T(8,128)(2,1)S(1)}, bf16[4,32,256]{2,1,0:T(8,128)(2,1)S(1)}, u32[]{:S(2)}, u32[]{:S(2)}) collective-permute-start(bf16[4,32,256]{2,1,0:T(8,128)(2,1)S(1)} %get-tuple-element.29), channel_id=1, source_target_pairs={{0,24},{4,28},{8,16},{12,20},{16,8},{20,12},{24,0},{28,4},{1,25},{... | collective-permute-start | bytes 196616 | tf_op jit(solution)/shard_map/ppermute | solution.py:245
  22.3 7.2 %copy-start.3 = (s32[64,8]{0,1:T(8,128)S(1)}, s32[64,8]{0,1:T(8,128)}, u32[]{:S(2)}) copy-start(s32[64,8]{0,1:T(8,128)} %param.8) | copy-start | bytes 6148
  22.3 7.2 %collective-permute-start.8 = (bf16[4,32,256]{2,1,0:T(8,128)(2,1)S(1)}, bf16[4,32,256]{2,1,0:T(8,128)(2,1)S(1)}, u32[]{:S(2)}, u32[]{:S(2)}) collective-permute-start(bf16[4,32,256]{2,1,0:T(8,128)(2,1)S(1)} %get-tuple-element.30), channel_id=1, source_target_pairs={{0,28},{4,24},{8,20},{12,16},{16,12},{20,8},{24,4},{28,0},{1,29},{... | collective-permute-start | bytes 196616 | tf_op jit(solution)/shard_map/ppermute | solution.py:245
  25.0 26.5 %copy-start.5 = (s32[8]{0:T(128)S(1)}, s32[8]{0:T(128)}, u32[]{:S(2)}) copy-start(s32[8]{0:T(128)} %refs_1_.5) | copy-start | bytes 100
  32.1 7.9 %collective-permute-start.9 = (s16[264,128]{1,0:T(8,128)(2,1)S(1)}, s16[264,128]{1,0:T(8,128)(2,1)S(1)}, u32[]{:S(2)}, u32[]{:S(2)}) collective-permute-start(s16[264,128]{1,0:T(8,128)(2,1)S(1)} %get-tuple-element.33), channel_id=1, source_target_pairs={{0,4},{4,0},{8,12},{12,8},{16,20},{20,16},{24,28},{28,24},{1,5},{5... | collective-permute-start | bytes 202760 | tf_op jit(solution)/shard_map/ppermute | solution.py:245
  34.2 7.6 %collective-permute-start.10 = (s16[264,128]{1,0:T(8,128)(2,1)S(1)}, s16[264,128]{1,0:T(8,128)(2,1)S(1)}, u32[]{:S(2)}, u32[]{:S(2)}) collective-permute-start(s16[264,128]{1,0:T(8,128)(2,1)S(1)} %get-tuple-element.34), channel_id=1, source_target_pairs={{0,8},{4,12},{8,0},{12,4},{16,24},{20,28},{24,16},{28,20},{1,9},{5... | collective-permute-start | bytes 202760 | tf_op jit(solution)/shard_map/ppermute | solution.py:245
  35.0 7.8 %collective-permute-start.11 = (s16[264,128]{1,0:T(8,128)(2,1)S(1)}, s16[264,128]{1,0:T(8,128)(2,1)S(1)}, u32[]{:S(2)}, u32[]{:S(2)}) collective-permute-start(s16[264,128]{1,0:T(8,128)(2,1)S(1)} %get-tuple-element.35), channel_id=1, source_target_pairs={{0,12},{4,8},{8,4},{12,0},{16,28},{20,24},{24,20},{28,16},{1,13},{... | collective-permute-start | bytes 202760 | tf_op jit(solution)/shard_map/ppermute | solution.py:245
  35.9 9.9 %collective-permute-start.12 = (s16[264,128]{1,0:T(8,128)(2,1)S(1)}, s16[264,128]{1,0:T(8,128)(2,1)S(1)}, u32[]{:S(2)}, u32[]{:S(2)}) collective-permute-start(s16[264,128]{1,0:T(8,128)(2,1)S(1)} %get-tuple-element.36), channel_id=1, source_target_pairs={{0,16},{4,20},{8,24},{12,28},{16,0},{20,4},{24,8},{28,12},{1,17},{... | collective-permute-start | bytes 202760 | tf_op jit(solution)/shard_map/ppermute | solution.py:245
  38.3 9.6 %collective-permute-start.13 = (s16[264,128]{1,0:T(8,128)(2,1)S(1)}, s16[264,128]{1,0:T(8,128)(2,1)S(1)}, u32[]{:S(2)}, u32[]{:S(2)}) collective-permute-start(s16[264,128]{1,0:T(8,128)(2,1)S(1)} %get-tuple-element.37), channel_id=1, source_target_pairs={{0,20},{4,16},{8,28},{12,24},{16,4},{20,0},{24,12},{28,8},{1,21},{... | collective-permute-start | bytes 202760 | tf_op jit(solution)/shard_map/ppermute | solution.py:245
  40.1 10.3 %collective-permute-start.14 = (s16[264,128]{1,0:T(8,128)(2,1)S(1)}, s16[264,128]{1,0:T(8,128)(2,1)S(1)}, u32[]{:S(2)}, u32[]{:S(2)}) collective-permute-start(s16[264,128]{1,0:T(8,128)(2,1)S(1)} %get-tuple-element.38), channel_id=1, source_target_pairs={{0,24},{4,28},{8,16},{12,20},{16,8},{20,12},{24,0},{28,4},{1,25},{... | collective-permute-start | bytes 202760 | tf_op jit(solution)/shard_map/ppermute | solution.py:245
  41.8 9.7 %collective-permute-start.15 = (s16[264,128]{1,0:T(8,128)(2,1)S(1)}, s16[264,128]{1,0:T(8,128)(2,1)S(1)}, u32[]{:S(2)}, u32[]{:S(2)}) collective-permute-start(s16[264,128]{1,0:T(8,128)(2,1)S(1)} %get-tuple-element.39), channel_id=1, source_target_pairs={{0,28},{4,24},{8,20},{12,16},{16,12},{20,8},{24,4},{28,0},{1,29},{... | collective-permute-start | bytes 202760 | tf_op jit(solution)/shard_map/ppermute | solution.py:245

commit v2 on v1

--- a/solution.py
+++ b/solution.py
@@ -9,6 +9,9 @@
 
 SPREAD = 4
 RIM = 3
+HALO = 8
+TALL = 256
+WIDE = 1024
 DIRECT_LIMIT = 16
 EXTRA_ROWS = 8
 SUM_SCALE = 2048.0
@@ -21,46 +24,16 @@
 
 SMEM = pl.BlockSpec(memory_space=pltpu.SMEM)
 VMEM = pl.BlockSpec(memory_space=pltpu.VMEM)
+HBM = pl.BlockSpec(memory_space=pltpu.HBM)
 
 
 def params(mib):
     return pltpu.CompilerParams(vmem_limit_bytes=mib << 20)
-
-
-def halo_rows(block, width):
-    count = lax.axis_size("row")
-    forward = [(i, i + 1) for i in range(count - 1)]
-    backward = [(target, source) for source, target in forward]
-    rows = block.shape[1]
-    low = lax.ppermute(block[:, rows - width :], "row", forward)
-    high = lax.ppermute(block[:, :width], "row", backward)
-    return low, high
 
 
 def smoothing_taps():
     spread_taps = np.exp(-np.abs(np.arange(-RIM, RIM + 1)) / decay_length)
     return spread_taps / spread_taps.sum()
-
-
-def retrieve_phase(intensity):
-    low, high = halo_rows(intensity, RIM)
-    padded = jnp.concatenate([low, intensity, high], axis=1)
-    tap_weights = smoothing_taps()
-    height_rows = intensity.shape[1]
-    column_count = intensity.shape[2]
-    across = float(tap_weights[0]) * padded[:, 0:height_rows, :].astype(jnp.float32)
-    for tap_index in range(1, 2 * RIM + 1):
-        across = across + float(tap_weights[tap_index]) * padded[
-            :, tap_index : tap_index + height_rows, :
-        ].astype(jnp.float32)
-    widened = jnp.pad(across, ((0, 0), (0, 0), (RIM, RIM)))
-    smoothed = float(tap_weights[0]) * widened[:, :, 0:column_count]
-    for tap_index in range(1, 2 * RIM + 1):
-        smoothed = (
-            smoothed
-            + float(tap_weights[tap_index]) * widened[:, :, tap_index : tap_index + column_count]
-        )
-    return -jnp.log(smoothed)
 
 
 def each_piece(direct, count, member, refs, body):
@@ -83,9 +56,35 @@
     return low
 
 
-def load_kernel(direct, count, slots, offsets, tile_count, volume, *pieces):
+def load_kernel(direct, count, slots, offsets_in, count_in, volume_in, table_in, intensity, *refs):
+    lists = count if direct else 1
+    near_rows, far_rows, table_out, offsets_out, count_out = refs[:5]
+    pieces = refs[5 : 5 + lists]
+    offsets, tile_count, volume, sems = refs[5 + lists :]
     member = lax.axis_index("tile")
+    even = lax.rem(lax.axis_index("row"), 2) == 0
+    last = intensity.shape[0] - HALO
+    first_copy = pltpu.make_async_copy(offsets_in, offsets, sems.at[0])
+    count_copy = pltpu.make_async_copy(count_in, tile_count, sems.at[1])
+    volume_copy = pltpu.make_async_copy(volume_in, volume, sems.at[2])
+    near = pl.multiple_of(jnp.where(even, last, 0), HALO)
+    far = pl.multiple_of(jnp.where(even, 0, last), HALO)
+    near_copy = pltpu.make_async_copy(intensity.at[pl.ds(near, HALO)], near_rows, sems.at[3])
+    far_copy = pltpu.make_async_copy(intensity.at[pl.ds(far, HALO)], far_rows, sems.at[4])
+    later = [near_copy, far_copy]
+    for i, (here, there) in enumerate(
+        ((table_in, table_out), (offsets_in, offsets_out), (count_in, count_out))
+    ):
+        later.append(pltpu.make_async_copy(here, there, sems.at[5 + i]))
+    first_copy.start()
+    count_copy.start()
+    volume_copy.start()
+    for copy in later:
+        copy.start()
+    first_copy.wait()
+    count_copy.wait()
     live = tile_count[member]
+    volume_copy.wait()
 
     def one(piece, angle):
         start = group_start(offsets, angle, member, slots)
@@ -98,14 +97,15 @@
             piece[s] = total.astype(piece.dtype)
 
     each_piece(direct, count, member, pieces, one)
-
-
-def table_kernel(slots, blocks, offsets, tile_count, offset_rows, footprint, inverse, sums):
+    for copy in later:
+        copy.wait()
+
+
+def tables(slots, blocks, offset_rows, tile_count, table, inverse, sums):
     member = lax.axis_index("tile")
-    half = footprint.shape[1] // 2
+    half = table.shape[1] // 2
     padded = inverse.shape[0]
     total = offset_rows.shape[1]
-    table = footprint[...]
     by_column = jnp.sum(table.astype(jnp.float32), axis=0, keepdims=True)
     mine = offset_rows[pl.ds(member, 1), :]
     lane = lax.broadcasted_iota(jnp.int32, (1, total), 1)
@@ -131,6 +131,57 @@
         [whole[:, :half], whole[:, half:], low[:, :half], low[:, half:]], axis=0
     )
     sums[...] = jnp.concatenate([packed, jnp.zeros((4, half), jnp.float32)], axis=0)
+
+
+def spread_sum(x, axis, decay):
+    size = x.shape[axis]
+    down = x + decay * pltpu.roll(x, 1, axis)
+    down = down + decay**2 * pltpu.roll(down, 2, axis)
+    up = x + decay * pltpu.roll(x, size - 1, axis)
+    up = up + decay**2 * pltpu.roll(up, size - 2, axis)
+    return down + up - x
+
+
+def phase_kernel(
+    slots, tile_count, offset_rows, intensity, near_rows, far_rows, footprint, *refs
+):
+    phase, inverse, sums, across = refs
+    rows, columns = intensity.shape
+    half = footprint.shape[1] // 2
+    blocks = columns // half
+    tables(slots, blocks, offset_rows, tile_count, footprint[...], inverse, sums)
+    even = lax.rem(lax.axis_index("row"), 2) == 0
+    decay = float(np.exp(-1.0 / decay_length))
+    centre = float(smoothing_taps()[RIM])
+    across[:, :half] = jnp.zeros((rows, half), jnp.float32)
+    across[:, half + columns :] = jnp.zeros((rows, half), jnp.float32)
+
+    def vertical(step, carry):
+        at = pl.ds(pl.multiple_of(step * TALL, half), TALL)
+        near = near_rows[:, at].astype(jnp.float32)
+        far = far_rows[:, at].astype(jnp.float32)
+        x = jnp.concatenate(
+            [
+                jnp.where(even, far, near),
+                intensity[:, at].astype(jnp.float32),
+                jnp.where(even, near, far),
+            ],
+            axis=0,
+        )
+        filtered = spread_sum(x, 0, decay)[HALO : HALO + rows]
+        across[:, pl.ds(pl.multiple_of(step * TALL + half, half), TALL)] = filtered
+        return carry
+
+    lax.fori_loop(0, columns // TALL, vertical, 0)
+
+    def horizontal(step, carry):
+        base = pl.multiple_of(step * WIDE, half)
+        x = across[:, pl.ds(base, WIDE + 2 * half)]
+        filtered = spread_sum(x, 1, decay)[:, half : half + WIDE]
+        phase[:, pl.ds(base, WIDE)] = -jnp.log(filtered * centre**2)
+        return carry
+
+    lax.fori_loop(0, columns // WIDE, horizontal, 0)
 
 
 def angle_kernel(direct, count, slots, offsets, phase, footprint, inverse, sums, *refs):
@@ -246,6 +297,15 @@
     return arrived
 
 
+def swap_halos(near_rows, far_rows):
+    count = lax.axis_size("row")
+    pairs = [(i, i + 1) for i in range(0, count - 1, 2)]
+    between = [(i, i + 1) for i in range(1, count - 1, 2)]
+    far_rows = lax.ppermute(far_rows, "row", between + [(b, a) for a, b in between])
+    near_rows = lax.ppermute(near_rows, "row", pairs + [(b, a) for a, b in pairs])
+    return near_rows, far_rows
+
+
 def use_direct(count):
     return count <= DIRECT_LIMIT and count & (count - 1) == 0
 
@@ -268,29 +328,40 @@
             return [jax.ShapeDtypeStruct(shape, dtype)] * count
         return [jax.ShapeDtypeStruct((count,) + shape, dtype)]
 
+    halo_shape = jax.ShapeDtypeStruct((HALO, columns), intensity.dtype)
     load_shapes = piece_shapes((SPREAD, rows, voxels), jnp.bfloat16)
-    loads = pl.pallas_call(
+    near_rows, far_rows, table, offsets_here, counts_here, *loads = pl.pallas_call(
         lambda *refs: load_kernel(direct, count, slots, *refs),
-        out_shape=load_shapes,
-        in_specs=[SMEM, SMEM, VMEM],
-        out_specs=[VMEM] * len(load_shapes),
+        out_shape=[halo_shape, halo_shape]
+        + [jax.ShapeDtypeStruct(x.shape, x.dtype) for x in (table, offsets, tile_count)]
+        + load_shapes,
+        in_specs=[HBM] * 5,
+        out_specs=[VMEM] * (5 + len(load_shapes)),
+        scratch_shapes=[
+            pltpu.SMEM(offsets.shape, jnp.int32),
+            pltpu.SMEM(tile_count.shape, jnp.int32),
+            pltpu.VMEM(volume.shape, volume.dtype),
+            pltpu.SemaphoreType.DMA((8,)),
+        ],
         compiler_params=params(16),
         name="loads",
-    )(offsets, tile_count, volume)
+    )(*[pltpu.with_memory_space_constraint(x, pltpu.HBM) for x in (offsets, tile_count, volume, table, intensity[0])])
     arrived = exchange(direct, count, loads)
-
-    phase_map = retrieve_phase(intensity)[0]
-    inverse, sums = pl.pallas_call(
-        lambda *refs: table_kernel(slots, blocks, *refs),
+    near_rows, far_rows = swap_halos(near_rows, far_rows)
+
+    phase_map, inverse, sums = pl.pallas_call(
+        lambda *refs: phase_kernel(slots, *refs),
         out_shape=[
+            jax.ShapeDtypeStruct((rows, columns), jnp.float32),
             jax.ShapeDtypeStruct((padded_blocks, half), jnp.float32),
             jax.ShapeDtypeStruct((EXTRA_ROWS, half), jnp.float32),
         ],
-        in_specs=[SMEM, SMEM, VMEM, VMEM],
-        out_specs=[VMEM, VMEM],
+        in_specs=[SMEM] + [VMEM] * 5,
+        out_specs=[VMEM] * 3,
+        scratch_shapes=[pltpu.VMEM((rows, columns + 2 * half), jnp.float32)],
         compiler_params=params(16),
-        name="tables",
-    )(offsets, tile_count, offsets, table)
+        name="phase",
+    )(counts_here, offsets_here, intensity[0], near_rows, far_rows, table)
 
     back_shapes = piece_shapes((2 * SPREAD * rows + EXTRA_ROWS, half), jnp.int16)
     residual, *backs = pl.pallas_call(
@@ -301,7 +372,7 @@
         scratch_shapes=[pltpu.VMEM((rows, (SPREAD + 1) * half), jnp.bfloat16)],
         compiler_params=params(24),
         name="angle",
-    )(offsets, phase_map, table, inverse, sums, *arrived)
+    )(offsets_here, phase_map, table, inverse, sums, *arrived)
     received = exchange(direct, count, backs)
 
     correction = pl.pallas_call(
@@ -315,7 +386,7 @@
         ],
         compiler_params=params(16),
         name="gather",
-    )(offsets, tile_count, *received)
+    )(offsets_here, counts_here, *received)
     return residual[None], correction
 
 

time: 53.5 us -> 46.2 us (0.86)
  Pallas kernels: 6.38 us -> 12 us
  local copies, waits for them, and re-layouts: 4.64 us -> 0.01 us
  starting transfers between devices: 24.6 us -> 20.9 us
  other arithmetic: 3.67 us -> 0 us
  waiting for transfers between devices: 13.2 us -> 12.5 us
    pallas_call x1, Pallas kernels: 0.79 us -> 5.95 us  [local(): pl.pallas_call(lambda *refs: phase_kernel(slots, *refs), out_shape=[jax.S...]
    ppermute x2, starting transfers between devices: 4.33 us -> 0.74 us  [the longest x1 0.67 us: swap_halos(): lax.ppermute(far_rows, 'row', between + [(b, a) for a, b in between])]
    unnamed x15 -> x2, local copies, waits for them, and re-layouts: 3.46 us -> 0.01 us
    squeeze x1 -> x0, other arithmetic: 2.3 us -> none  [local(): phase_map = retrieve_phase(intensity)[0]]
    add x1 -> x0, other arithmetic: 1.37 us -> none  [retrieve_phase(): across + float(tap_weights[tap_index]) * padded[:, tap_index:tap_index +...]
    slice x1 -> x0, local copies, waits for them, and re-layouts: 1.12 us -> none  [halo_rows(): high = lax.ppermute(block[:, :width], 'row', backward)]
    ppermute x14, waiting for transfers between devices: 13.2 us -> 12.5 us  [exchange(): lax.ppermute(pieces[k], 'tile', [(i, i ^ k) for i in range(count)])]
  transfers between devices with their start and end apart: 16 -> 16, of which waited for: 6 -> 7; matrix products, arithmetic and copies ran while one was open for 9% -> 0% of each run, Pallas kernels for 4% -> 13%
where the time goes in v2:
time: 46.2 us; the launch traced here: 46.1 us
  starting transfers between devices  20.9 us (45%)
  waiting for transfers between devices  12.5 us (27%)
  Pallas kernels  12 us (26%)
  between operations  0.71 us (2%)
    ppermute x14, starting transfers between devices, exchange(): lax.ppermute(pieces[k], 'tile', [(i, i ^ k) for i in range(count)])  20.1 us
    ppermute x14, waiting for transfers between devices, exchange(): lax.ppermute(pieces[k], 'tile', [(i, i ^ k) for i in range(count)])  12.5 us
    pallas_call x1, Pallas kernels, local(): pl.pallas_call(lambda *refs: phase_kernel(slots, *refs), out_shape=[jax.S...  5.95 us
    pallas_call x1, Pallas kernels, local(): pl.pallas_call(lambda *refs: angle_kernel(direct, count, slots, *refs), o...  2.66 us
    pallas_call x1, Pallas kernels, local(): pl.pallas_call(lambda *refs: gather_kernel(direct, count, slots, rows, *r...  1.71 us
    pallas_call x1, Pallas kernels, local(): pl.pallas_call(lambda *refs: load_kernel(direct, count, slots, *refs), ou...  1.69 us
  transfers between devices with their start and end apart: 16, of which 7 were waited for; matrix products, arithmetic and copies ran while one was open for 0% of the time, Pallas kernels for 13%

profile of v2, /device:TPU:8, one launch (start us, length us, event | category | flops | bytes accessed | tf_op | source)
XLA Modules:
  0.0 46.1 jit_solution(9092357915826168184)
XLA Ops:
  0.6 1.7 %loads.1 = (bf16[8,11264]{1,0:T(8,128)(2,1)S(1)}, bf16[8,11264]{1,0:T(8,128)(2,1)S(1)}, bf16[256,256]{1,0:T(8,128)(2,1)S(1)}, s32[8,64]{1,0:T(8,128)S(1)}, s32[8...) custom-call(s32[8,64]{1,0:T(8,128)} %bitcast.7, ...), custom_call_target="tpu_custom_call" | custom-call | tf_op jit(solution)/shard_map/loads/pallas_call | solution.py:333
  2.3 0.1 collective-permute-start
  2.4 0.7 %collective-permute-start.1 = (bf16[8,11264]{1,0:T(8,128)(2,1)S(1)}, bf16[8,11264]{1,0:T(8,128)(2,1)S(1)}, u32[]{:S(2)}, u32[]{:S(2)}) collective-permute-start(bf16[8,11264]{1,0:T(8,128)(2,1)S(1)} %get-tuple-element.30), channel_id=1, source_target_pairs={{1,2},{2,1},{5,6},{6,5},{9,10},{10,9},{13,14},{14,13},{17,18},{18,... | collective-permute-start | bytes 540680 | tf_op jit(solution)/shard_map/ppermute | solution.py:304
  3.1 1.6 %collective-permute-start.2 = (bf16[4,32,256]{2,1,0:T(8,128)(2,1)S(1)}, bf16[4,32,256]{2,1,0:T(8,128)(2,1)S(1)}, u32[]{:S(2)}, u32[]{:S(2)}) collective-permute-start(bf16[4,32,256]{2,1,0:T(8,128)(2,1)S(1)} %get-tuple-element.36), channel_id=1, source_target_pairs={{0,4},{4,0},{8,12},{12,8},{16,20},{20,16},{24,28},{28,24},{1,5},{5... | collective-permute-start | bytes 196616 | tf_op jit(solution)/shard_map/ppermute | solution.py:296
  4.7 0.4 collective-permute-start.3
  5.1 1.5 %collective-permute-start.4 = (bf16[4,32,256]{2,1,0:T(8,128)(2,1)S(1)}, bf16[4,32,256]{2,1,0:T(8,128)(2,1)S(1)}, u32[]{:S(2)}, u32[]{:S(2)}) collective-permute-start(bf16[4,32,256]{2,1,0:T(8,128)(2,1)S(1)} %get-tuple-element.38), channel_id=1, source_target_pairs={{0,12},{4,8},{8,4},{12,0},{16,28},{20,24},{24,20},{28,16},{1,13},{... | collective-permute-start | bytes 196616 | tf_op jit(solution)/shard_map/ppermute | solution.py:296
  6.6 0.8 %collective-permute-done.2.refs_6_ = bf16[4,32,256]{2,1,0:T(8,128)(2,1)S(1)} collective-permute-done((bf16[4,32,256]{2,1,0:T(8,128)(2,1)S(1)}, bf16[4,32,256]{2,1,0:T(8,128)(2,1)S(1)}, u32[]{:S(2)}, u32[]{:S(2)}) %collective-permute-start.2) | collective-permute-done | bytes 65568 | tf_op jit(solution)/shard_map/ppermute | solution.py:296
  7.4 2.6 %collective-permute-start.5 = (bf16[4,32,256]{2,1,0:T(8,128)(2,1)S(1)}, bf16[4,32,256]{2,1,0:T(8,128)(2,1)S(1)}, u32[]{:S(2)}, u32[]{:S(2)}) collective-permute-start(bf16[4,32,256]{2,1,0:T(8,128)(2,1)S(1)} %get-tuple-element.39), channel_id=1, source_target_pairs={{0,16},{4,20},{8,24},{12,28},{16,0},{20,4},{24,8},{28,12},{1,17},{... | collective-permute-start | bytes 196616 | tf_op jit(solution)/shard_map/ppermute | solution.py:296
  10.0 0.0 collective-permute-done.3.refs_7_
  10.0 1.5 %collective-permute-start.6 = (bf16[4,32,256]{2,1,0:T(8,128)(2,1)S(1)}, bf16[4,32,256]{2,1,0:T(8,128)(2,1)S(1)}, u32[]{:S(2)}, u32[]{:S(2)}) collective-permute-start(bf16[4,32,256]{2,1,0:T(8,128)(2,1)S(1)} %get-tuple-element.40), channel_id=1, source_target_pairs={{0,20},{4,16},{8,28},{12,24},{16,4},{20,0},{24,12},{28,8},{1,21},{... | collective-permute-start | bytes 196616 | tf_op jit(solution)/shard_map/ppermute | solution.py:296
  11.5 0.0 collective-permute-done.refs_3_
  11.5 1.4 %collective-permute-start.7 = (bf16[4,32,256]{2,1,0:T(8,128)(2,1)S(1)}, bf16[4,32,256]{2,1,0:T(8,128)(2,1)S(1)}, u32[]{:S(2)}, u32[]{:S(2)}) collective-permute-start(bf16[4,32,256]{2,1,0:T(8,128)(2,1)S(1)} %get-tuple-element.41), channel_id=1, source_target_pairs={{0,24},{4,28},{8,16},{12,20},{16,8},{20,12},{24,0},{28,4},{1,25},{... | collective-permute-start | bytes 196616 | tf_op jit(solution)/shard_map/ppermute | solution.py:296
  12.9 0.0 collective-permute-done.1.refs_4_
  12.9 1.6 %collective-permute-start.8 = (bf16[4,32,256]{2,1,0:T(8,128)(2,1)S(1)}, bf16[4,32,256]{2,1,0:T(8,128)(2,1)S(1)}, u32[]{:S(2)}, u32[]{:S(2)}) collective-permute-start(bf16[4,32,256]{2,1,0:T(8,128)(2,1)S(1)} %get-tuple-element.42), channel_id=1, source_target_pairs={{0,28},{4,24},{8,20},{12,16},{16,12},{20,8},{24,4},{28,0},{1,29},{... | collective-permute-start | bytes 196616 | tf_op jit(solution)/shard_map/ppermute | solution.py:296
  14.5 6.0 %phase.1 = (f32[32,11264]{1,0:T(8,128)S(1)}, f32[96,128]{1,0:T(8,128)S(1)}, f32[8,128]{1,0:T(8,128)S(1)}) custom-call(s32[8]{0:T(128)S(1)} %get-tuple-element.28.refs_0_.refs_1_, s32[8,64]{1,0:T(8,128)S(1)} %get-tuple-element.27.refs_1_.refs_0_, bf16[32,11264]{1,0:T(8,128)(2,1)S(1)} %bitcast.5, bf16[8,11264]{1,0:T(8,128)(2,1)S(1)} %collective-permute-done.refs_3_, ...), custom_call_target="tpu_custom_call" | custom-call | tf_op jit(solution)/shard_map/phase/pallas_call | solution.py:352
  20.4 0.0 collective-permute-done.4.refs_8_
  20.5 0.0 collective-permute-done.6.refs_10_
  20.5 0.5 %collective-permute-done.7.refs_11_ = bf16[4,32,256]{2,1,0:T(8,128)(2,1)S(1)} collective-permute-done((bf16[4,32,256]{2,1,0:T(8,128)(2,1)S(1)}, bf16[4,32,256]{2,1,0:T(8,128)(2,1)S(1)}, u32[]{:S(2)}, u32[]{:S(2)}) %collective-permute-start.7) | collective-permute-done | bytes 65568 | tf_op jit(solution)/shard_map/ppermute | solution.py:296
  21.0 2.4 %collective-permute-done.8.refs_12_ = bf16[4,32,256]{2,1,0:T(8,128)(2,1)S(1)} collective-permute-done((bf16[4,32,256]{2,1,0:T(8,128)(2,1)S(1)}, bf16[4,32,256]{2,1,0:T(8,128)(2,1)S(1)}, u32[]{:S(2)}, u32[]{:S(2)}) %collective-permute-start.8) | collective-permute-done | bytes 65568 | tf_op jit(solution)/shard_map/ppermute | solution.py:296
  23.4 2.7 %angle.1 = (f32[32,11264]{1,0:T(8,128)}, s16[264,128]{1,0:T(8,128)(2,1)S(1)}, s16[264,128]{1,0:T(8,128)(2,1)S(1)}, s16[264,128]{1,0:T(8,128)(2,1)S(1)}, s16[264,...) custom-call(s32[8,64]{1,0:T(8,128)S(1)} %get-tuple-element.27.refs_1, ...), custom_call_target="tpu_custom_call" | custom-call | tf_op jit(solution)/shard_map/angle/pallas_call | solution.py:367
  26.1 0.5 %collective-permute-start.9 = (s16[264,128]{1,0:T(8,128)(2,1)S(1)}, s16[264,128]{1,0:T(8,128)(2,1)S(1)}, u32[]{:S(2)}, u32[]{:S(2)}) collective-permute-start(s16[264,128]{1,0:T(8,128)(2,1)S(1)} %get-tuple-element.45), channel_id=1, source_target_pairs={{0,4},{4,0},{8,12},{12,8},{16,20},{20,16},{24,28},{28,24},{1,5},{5... | collective-permute-start | bytes 202760 | tf_op jit(solution)/shard_map/ppermute | solution.py:296
  26.5 3.0 %collective-permute-start.11 = (s16[264,128]{1,0:T(8,128)(2,1)S(1)}, s16[264,128]{1,0:T(8,128)(2,1)S(1)}, u32[]{:S(2)}, u32[]{:S(2)}) collective-permute-start(s16[264,128]{1,0:T(8,128)(2,1)S(1)} %get-tuple-element.47), channel_id=1, source_target_pairs={{0,12},{4,8},{8,4},{12,0},{16,28},{20,24},{24,20},{28,16},{1,13},{... | collective-permute-start | bytes 202760 | tf_op jit(solution)/shard_map/ppermute | solution.py:296
  29.5 1.6 %collective-permute-start.12 = (s16[264,128]{1,0:T(8,128)(2,1)S(1)}, s16[264,128]{1,0:T(8,128)(2,1)S(1)}, u32[]{:S(2)}, u32[]{:S(2)}) collective-permute-start(s16[264,128]{1,0:T(8,128)(2,1)S(1)} %get-tuple-element.48), channel_id=1, source_target_pairs={{0,16},{4,20},{8,24},{12,28},{16,0},{20,4},{24,8},{28,12},{1,17},{... | collective-permute-start | bytes 202760 | tf_op jit(solution)/shard_map/ppermute | solution.py:296
  31.2 1.2 %collective-permute-start.13 = (s16[264,128]{1,0:T(8,128)(2,1)S(1)}, s16[264,128]{1,0:T(8,128)(2,1)S(1)}, u32[]{:S(2)}, u32[]{:S(2)}) collective-permute-start(s16[264,128]{1,0:T(8,128)(2,1)S(1)} %get-tuple-element.49), channel_id=1, source_target_pairs={{0,20},{4,16},{8,28},{12,24},{16,4},{20,0},{24,12},{28,8},{1,21},{... | collective-permute-start | bytes 202760 | tf_op jit(solution)/shard_map/ppermute | solution.py:296
  32.4 2.2 %collective-permute-start.14 = (s16[264,128]{1,0:T(8,128)(2,1)S(1)}, s16[264,128]{1,0:T(8,128)(2,1)S(1)}, u32[]{:S(2)}, u32[]{:S(2)}) collective-permute-start(s16[264,128]{1,0:T(8,128)(2,1)S(1)} %get-tuple-element.50), channel_id=1, source_target_pairs={{0,24},{4,28},{8,16},{12,20},{16,8},{20,12},{24,0},{28,4},{1,25},{... | collective-permute-start | bytes 202760 | tf_op jit(solution)/shard_map/ppermute | solution.py:296
  34.6 1.0 %collective-permute-start.15 = (s16[264,128]{1,0:T(8,128)(2,1)S(1)}, s16[264,128]{1,0:T(8,128)(2,1)S(1)}, u32[]{:S(2)}, u32[]{:S(2)}) collective-permute-start(s16[264,128]{1,0:T(8,128)(2,1)S(1)} %get-tuple-element.51), channel_id=1, source_target_pairs={{0,28},{4,24},{8,20},{12,16},{16,12},{20,8},{24,4},{28,0},{1,29},{... | collective-permute-start | bytes 202760 | tf_op jit(solution)/shard_map/ppermute | solution.py:296
  35.6 0.0 collective-permute-done.11.refs_5_
  35.6 3.0 %collective-permute-done.12.refs_6_ = s16[264,128]{1,0:T(8,128)(2,1)S(1)} collective-permute-done((s16[264,128]{1,0:T(8,128)(2,1)S(1)}, s16[264,128]{1,0:T(8,128)(2,1)S(1)}, u32[]{:S(2)}, u32[]{:S(2)}) %collective-permute-start.12) | collective-permute-done | bytes 67616 | tf_op jit(solution)/shard_map/ppermute | solution.py:296
  38.6 2.1 %collective-permute-done.13.refs_7_ = s16[264,128]{1,0:T(8,128)(2,1)S(1)} collective-permute-done((s16[264,128]{1,0:T(8,128)(2,1)S(1)}, s16[264,128]{1,0:T(8,128)(2,1)S(1)}, u32[]{:S(2)}, u32[]{:S(2)}) %collective-permute-start.13) | collective-permute-done | bytes 67616 | tf_op jit(solution)/shard_map/ppermute | solution.py:296
  40.8 1.9 %collective-permute-done.14.refs_8_ = s16[264,128]{1,0:T(8,128)(2,1)S(1)} collective-permute-done((s16[264,128]{1,0:T(8,128)(2,1)S(1)}, s16[264,128]{1,0:T(8,128)(2,1)S(1)}, u32[]{:S(2)}, u32[]{:S(2)}) %collective-permute-start.14) | collective-permute-done | bytes 67616 | tf_op jit(solution)/shard_map/ppermute | solution.py:296
  42.7 1.7 %collective-permute-done.15.refs_9_ = s16[264,128]{1,0:T(8,128)(2,1)S(1)} collective-permute-done((s16[264,128]{1,0:T(8,128)(2,1)S(1)}, s16[264,128]{1,0:T(8,128)(2,1)S(1)}, u32[]{:S(2)}, u32[]{:S(2)}) %collective-permute-start.15) | collective-permute-done | bytes 67616 | tf_op jit(solution)/shard_map/ppermute | solution.py:296
  44.4 1.7 %gather.1 = f32[8,32,256]{2,1,0:T(8,128)} custom-call(s32[8,64]{1,0:T(8,128)S(1)} %get-tuple-element.27.refs_1_.refs_0_, s32[8]{0:T(128)S(1)} %get-tuple-element.28.refs_0_.refs_1_, s16[264,128]{1,0:T(8,128)(2,1)S(1)} %get-tuple-element.44.refs_2_, s16[264,128]{1,0:T(8,128)(2,1)S(1)} %collective-permute-done.9.refs_3_, ...), custom_call_target="tpu_custom_call" | custom-call | tf_op jit(solution)/shard_map/gather/pallas_call | solution.py:378
  (6 shorter events, 0.0 us)
Async XLA Ops:
  0.6 13.8 %copy-start = (bf16[1,32,11264]{2,1,0:T(8,128)(2,1)S(1)}, bf16[1,32,11264]{2,1,0:T(8,128)(2,1)}, u32[]{:S(2)}) copy-start(bf16[1,32,11264]{2,1,0:T(8,128)(2,1)} %param.5) | copy-start | bytes 2162692
  2.3 9.1 %collective-permute-start = (bf16[8,11264]{1,0:T(8,128)(2,1)S(1)}, bf16[8,11264]{1,0:T(8,128)(2,1)S(1)}, u32[]{:S(2)}, u32[]{:S(2)}) collective-permute-start(bf16[8,11264]{1,0:T(8,128)(2,1)S(1)} %get-tuple-element.29), channel_id=1, source_target_pairs={{0,1},{2,3},{1,0},{3,2},{4,5},{6,7},{5,4},{7,6},{8,9},{10,11},{9,8... | collective-permute-start | bytes 540680 | tf_op jit(solution)/shard_map/ppermute | solution.py:305
  2.4 10.5 %collective-permute-start.1 = (bf16[8,11264]{1,0:T(8,128)(2,1)S(1)}, bf16[8,11264]{1,0:T(8,128)(2,1)S(1)}, u32[]{:S(2)}, u32[]{:S(2)}) collective-permute-start(bf16[8,11264]{1,0:T(8,128)(2,1)S(1)} %get-tuple-element.30), channel_id=1, source_target_pairs={{1,2},{2,1},{5,6},{6,5},{9,10},{10,9},{13,14},{14,13},{17,18},{18,... | collective-permute-start | bytes 540680 | tf_op jit(solution)/shard_map/ppermute | solution.py:304
  3.1 4.3 %collective-permute-start.2 = (bf16[4,32,256]{2,1,0:T(8,128)(2,1)S(1)}, bf16[4,32,256]{2,1,0:T(8,128)(2,1)S(1)}, u32[]{:S(2)}, u32[]{:S(2)}) collective-permute-start(bf16[4,32,256]{2,1,0:T(8,128)(2,1)S(1)} %get-tuple-element.36), channel_id=1, source_target_pairs={{0,4},{4,0},{8,12},{12,8},{16,20},{20,16},{24,28},{28,24},{1,5},{5... | collective-permute-start | bytes 196616 | tf_op jit(solution)/shard_map/ppermute | solution.py:296
  4.7 5.3 %collective-permute-start.3 = (bf16[4,32,256]{2,1,0:T(8,128)(2,1)S(1)}, bf16[4,32,256]{2,1,0:T(8,128)(2,1)S(1)}, u32[]{:S(2)}, u32[]{:S(2)}) collective-permute-start(bf16[4,32,256]{2,1,0:T(8,128)(2,1)S(1)} %get-tuple-element.37), channel_id=1, source_target_pairs={{0,8},{4,12},{8,0},{12,4},{16,24},{20,28},{24,16},{28,20},{1,9},{5... | collective-permute-start | bytes 196616 | tf_op jit(solution)/shard_map/ppermute | solution.py:296
  5.1 15.3 %collective-permute-start.4 = (bf16[4,32,256]{2,1,0:T(8,128)(2,1)S(1)}, bf16[4,32,256]{2,1,0:T(8,128)(2,1)S(1)}, u32[]{:S(2)}, u32[]{:S(2)}) collective-permute-start(bf16[4,32,256]{2,1,0:T(8,128)(2,1)S(1)} %get-tuple-element.38), channel_id=1, source_target_pairs={{0,12},{4,8},{8,4},{12,0},{16,28},{20,24},{24,20},{28,16},{1,13},{... | collective-permute-start | bytes 196616 | tf_op jit(solution)/shard_map/ppermute | solution.py:296
  7.4 13.0 %collective-permute-start.5 = (bf16[4,32,256]{2,1,0:T(8,128)(2,1)S(1)}, bf16[4,32,256]{2,1,0:T(8,128)(2,1)S(1)}, u32[]{:S(2)}, u32[]{:S(2)}) collective-permute-start(bf16[4,32,256]{2,1,0:T(8,128)(2,1)S(1)} %get-tuple-element.39), channel_id=1, source_target_pairs={{0,16},{4,20},{8,24},{12,28},{16,0},{20,4},{24,8},{28,12},{1,17},{... | collective-permute-start | bytes 196616 | tf_op jit(solution)/shard_map/ppermute | solution.py:296
  10.0 10.4 %collective-permute-start.6 = (bf16[4,32,256]{2,1,0:T(8,128)(2,1)S(1)}, bf16[4,32,256]{2,1,0:T(8,128)(2,1)S(1)}, u32[]{:S(2)}, u32[]{:S(2)}) collective-permute-start(bf16[4,32,256]{2,1,0:T(8,128)(2,1)S(1)} %get-tuple-element.40), channel_id=1, source_target_pairs={{0,20},{4,16},{8,28},{12,24},{16,4},{20,0},{24,12},{28,8},{1,21},{... | collective-permute-start | bytes 196616 | tf_op jit(solution)/shard_map/ppermute | solution.py:296
  11.5 9.5 %collective-permute-start.7 = (bf16[4,32,256]{2,1,0:T(8,128)(2,1)S(1)}, bf16[4,32,256]{2,1,0:T(8,128)(2,1)S(1)}, u32[]{:S(2)}, u32[]{:S(2)}) collective-permute-start(bf16[4,32,256]{2,1,0:T(8,128)(2,1)S(1)} %get-tuple-element.41), channel_id=1, source_target_pairs={{0,24},{4,28},{8,16},{12,20},{16,8},{20,12},{24,0},{28,4},{1,25},{... | collective-permute-start | bytes 196616 | tf_op jit(solution)/shard_map/ppermute | solution.py:296
  12.9 10.5 %collective-permute-start.8 = (bf16[4,32,256]{2,1,0:T(8,128)(2,1)S(1)}, bf16[4,32,256]{2,1,0:T(8,128)(2,1)S(1)}, u32[]{:S(2)}, u32[]{:S(2)}) collective-permute-start(bf16[4,32,256]{2,1,0:T(8,128)(2,1)S(1)} %get-tuple-element.42), channel_id=1, source_target_pairs={{0,28},{4,24},{8,20},{12,16},{16,12},{20,8},{24,4},{28,0},{1,29},{... | collective-permute-start | bytes 196616 | tf_op jit(solution)/shard_map/ppermute | solution.py:296
  26.1 6.3 %collective-permute-start.9 = (s16[264,128]{1,0:T(8,128)(2,1)S(1)}, s16[264,128]{1,0:T(8,128)(2,1)S(1)}, u32[]{:S(2)}, u32[]{:S(2)}) collective-permute-start(s16[264,128]{1,0:T(8,128)(2,1)S(1)} %get-tuple-element.45), channel_id=1, source_target_pairs={{0,4},{4,0},{8,12},{12,8},{16,20},{20,16},{24,28},{28,24},{1,5},{5... | collective-permute-start | bytes 202760 | tf_op jit(solution)/shard_map/ppermute | solution.py:296
  26.5 8.1 %collective-permute-start.10 = (s16[264,128]{1,0:T(8,128)(2,1)S(1)}, s16[264,128]{1,0:T(8,128)(2,1)S(1)}, u32[]{:S(2)}, u32[]{:S(2)}) collective-permute-start(s16[264,128]{1,0:T(8,128)(2,1)S(1)} %get-tuple-element.46), channel_id=1, source_target_pairs={{0,8},{4,12},{8,0},{12,4},{16,24},{20,28},{24,16},{28,20},{1,9},{5... | collective-permute-start | bytes 202760 | tf_op jit(solution)/shard_map/ppermute | solution.py:296
  26.5 9.1 %collective-permute-start.11 = (s16[264,128]{1,0:T(8,128)(2,1)S(1)}, s16[264,128]{1,0:T(8,128)(2,1)S(1)}, u32[]{:S(2)}, u32[]{:S(2)}) collective-permute-start(s16[264,128]{1,0:T(8,128)(2,1)S(1)} %get-tuple-element.47), channel_id=1, source_target_pairs={{0,12},{4,8},{8,4},{12,0},{16,28},{20,24},{24,20},{28,16},{1,13},{... | collective-permute-start | bytes 202760 | tf_op jit(solution)/shard_map/ppermute | solution.py:296
  29.5 9.1 %collective-permute-start.12 = (s16[264,128]{1,0:T(8,128)(2,1)S(1)}, s16[264,128]{1,0:T(8,128)(2,1)S(1)}, u32[]{:S(2)}, u32[]{:S(2)}) collective-permute-start(s16[264,128]{1,0:T(8,128)(2,1)S(1)} %get-tuple-element.48), channel_id=1, source_target_pairs={{0,16},{4,20},{8,24},{12,28},{16,0},{20,4},{24,8},{28,12},{1,17},{... | collective-permute-start | bytes 202760 | tf_op jit(solution)/shard_map/ppermute | solution.py:296
  31.2 9.6 %collective-permute-start.13 = (s16[264,128]{1,0:T(8,128)(2,1)S(1)}, s16[264,128]{1,0:T(8,128)(2,1)S(1)}, u32[]{:S(2)}, u32[]{:S(2)}) collective-permute-start(s16[264,128]{1,0:T(8,128)(2,1)S(1)} %get-tuple-element.49), channel_id=1, source_target_pairs={{0,20},{4,16},{8,28},{12,24},{16,4},{20,0},{24,12},{28,8},{1,21},{... | collective-permute-start | bytes 202760 | tf_op jit(solution)/shard_map/ppermute | solution.py:296
  32.4 10.3 %collective-permute-start.14 = (s16[264,128]{1,0:T(8,128)(2,1)S(1)}, s16[264,128]{1,0:T(8,128)(2,1)S(1)}, u32[]{:S(2)}, u32[]{:S(2)}) collective-permute-start(s16[264,128]{1,0:T(8,128)(2,1)S(1)} %get-tuple-element.50), channel_id=1, source_target_pairs={{0,24},{4,28},{8,16},{12,20},{16,8},{20,12},{24,0},{28,4},{1,25},{... | collective-permute-start | bytes 202760 | tf_op jit(solution)/shard_map/ppermute | solution.py:296
  34.6 9.8 %collective-permute-start.15 = (s16[264,128]{1,0:T(8,128)(2,1)S(1)}, s16[264,128]{1,0:T(8,128)(2,1)S(1)}, u32[]{:S(2)}, u32[]{:S(2)}) collective-permute-start(s16[264,128]{1,0:T(8,128)(2,1)S(1)} %get-tuple-element.51), channel_id=1, source_target_pairs={{0,28},{4,24},{8,20},{12,16},{16,12},{20,8},{24,4},{28,0},{1,29},{... | collective-permute-start | bytes 202760 | tf_op jit(solution)/shard_map/ppermute | solution.py:296

commit v3 on v2

--- a/solution.py
+++ b/solution.py
@@ -10,8 +10,9 @@
 SPREAD = 4
 RIM = 3
 HALO = 8
-TALL = 256
-WIDE = 1024
+GROUP = 22
+TERMS = 2
+FIRST = 3
 DIRECT_LIMIT = 16
 EXTRA_ROWS = 8
 SUM_SCALE = 2048.0
@@ -133,19 +134,21 @@
     sums[...] = jnp.concatenate([packed, jnp.zeros((4, half), jnp.float32)], axis=0)
 
 
-def spread_sum(x, axis, decay):
-    size = x.shape[axis]
-    down = x + decay * pltpu.roll(x, 1, axis)
-    down = down + decay**2 * pltpu.roll(down, 2, axis)
-    up = x + decay * pltpu.roll(x, size - 1, axis)
-    up = up + decay**2 * pltpu.roll(up, size - 2, axis)
-    return down + up - x
-
-
-def phase_kernel(
-    slots, tile_count, offset_rows, intensity, near_rows, far_rows, footprint, *refs
-):
-    phase, inverse, sums, across = refs
+def tap_matrix(half, terms):
+    place = np.arange(4 * half)[:, None] - half
+    apart = np.abs(place - np.arange(2 * half)[None, :])
+    taps = smoothing_taps()
+    rest = np.where(apart <= RIM, np.exp(-apart / decay_length) * taps[RIM], 0.0)
+    parts = []
+    for _ in range(terms):
+        part = rest.astype(jnp.bfloat16)
+        parts.append(part)
+        rest = rest - part.astype(np.float64)
+    return np.concatenate(parts, axis=0)
+
+
+def phase_kernel(slots, tile_count, offset_rows, intensity, near_rows, far_rows, footprint, *refs):
+    taps, phase, inverse, sums, padded, across = refs
     rows, columns = intensity.shape
     half = footprint.shape[1] // 2
     blocks = columns // half
@@ -153,52 +156,88 @@
     even = lax.rem(lax.axis_index("row"), 2) == 0
     decay = float(np.exp(-1.0 / decay_length))
     centre = float(smoothing_taps()[RIM])
-    across[:, :half] = jnp.zeros((rows, half), jnp.float32)
-    across[:, half + columns :] = jnp.zeros((rows, half), jnp.float32)
-
-    def vertical(step, carry):
-        at = pl.ds(pl.multiple_of(step * TALL, half), TALL)
-        near = near_rows[:, at].astype(jnp.float32)
-        far = far_rows[:, at].astype(jnp.float32)
-        x = jnp.concatenate(
-            [
-                jnp.where(even, far, near),
-                intensity[:, at].astype(jnp.float32),
-                jnp.where(even, near, far),
-            ],
-            axis=0,
-        )
-        filtered = spread_sum(x, 0, decay)[HALO : HALO + rows]
-        across[:, pl.ds(pl.multiple_of(step * TALL + half, half), TALL)] = filtered
+    tall = rows + 2 * HALO
+    edge = jnp.zeros((tall, half), padded.dtype)
+    padded[:, :half] = edge
+    padded[:, half + columns :] = edge
+    inner = slice(half, half + columns)
+    padded[HALO : HALO + rows, inner] = intensity[...]
+    near = near_rows[...].astype(jnp.float32)
+    far = far_rows[...].astype(jnp.float32)
+    padded[:HALO, inner] = jnp.where(even, far, near).astype(padded.dtype)
+    padded[HALO + rows :, inner] = jnp.where(even, near, far).astype(padded.dtype)
+    terms = taps.shape[0] // (4 * half)
+    pairs = blocks // 2
+    group = max(d for d in range(1, min(GROUP, pairs) + 1) if pairs % d == 0)
+    stride = rows // 8
+
+    def step(g, carry):
+        tiles = [
+            padded[:, pl.ds(pl.multiple_of((g * group + i) * 2 * half, half), 4 * half)]
+            for i in range(group)
+        ]
+        stacked = jnp.concatenate([jnp.concatenate(tiles, axis=0)] * terms, axis=1)
+        filtered = jnp.dot(stacked, taps[...], preferred_element_type=jnp.float32)
+        for i in range(group):
+            for h in range(2):
+                across[(g * group + i) * 2 + h] = filtered[
+                    i * tall : (i + 1) * tall, h * half : (h + 1) * half
+                ]
+        for i in range(2 * group):
+            block = g * 2 * group + i
+            lines = [
+                across[block, pl.ds(HALO - RIM + m, 8, stride=stride), :]
+                for m in range(stride + 2 * RIM)
+            ]
+            for k in range(stride):
+                mid = k + RIM
+                total = lines[mid - RIM] + lines[mid + RIM]
+                for m in range(RIM - 1, 0, -1):
+                    total = total * decay + (lines[mid - m] + lines[mid + m])
+                total = total * decay + lines[mid]
+                phase[block, pl.ds(k, 8, stride=stride), :] = -jnp.log(total * centre)
         return carry
 
-    lax.fori_loop(0, columns // TALL, vertical, 0)
-
-    def horizontal(step, carry):
-        base = pl.multiple_of(step * WIDE, half)
-        x = across[:, pl.ds(base, WIDE + 2 * half)]
-        filtered = spread_sum(x, 1, decay)[:, half : half + WIDE]
-        phase[:, pl.ds(base, WIDE)] = -jnp.log(filtered * centre**2)
-        return carry
-
-    lax.fori_loop(0, columns // WIDE, horizontal, 0)
-
-
-def angle_kernel(direct, count, slots, offsets, phase, footprint, inverse, sums, *refs):
+    lax.fori_loop(0, pairs // group, step, 0)
+
+
+def write_kernel(residual, out):
+    blocks, _, half = residual.shape
+    for block in range(blocks):
+        out[:, block * half : (block + 1) * half] = residual[block]
+
+
+def encode(window, table, sums, piece):
+    rows = window.shape[0]
+    half = table.shape[1] // 2
+    stacked = jnp.concatenate(
+        [window[:, s * half : (s + 2) * half] for s in range(SPREAD)], axis=0
+    )
+    back = lax.dot_general(
+        stacked, table, (((1,), (1,)), ((), ())), preferred_element_type=jnp.float32
+    )
+    top = jnp.max(jnp.max(jnp.abs(back), axis=0, keepdims=True), axis=1, keepdims=True)
+    power = jnp.floor(jnp.log2(CODE_TOP / jnp.maximum(top, 1e-30)))
+    code = jnp.round(back * jnp.exp2(power)).astype(jnp.int32)
+    for s in range(SPREAD):
+        for h in range(2):
+            base = (2 * s + h) * rows
+            piece[base : base + rows, :] = code[
+                s * rows : (s + 1) * rows, h * half : (h + 1) * half
+            ].astype(piece.dtype)
+    base = 2 * SPREAD * rows
+    line = lax.broadcasted_iota(jnp.int32, (EXTRA_ROWS, half), 0)
+    extra = jnp.where(line < 4, sums, jnp.broadcast_to(power, (EXTRA_ROWS, half)))
+    piece[base : base + EXTRA_ROWS, :] = extra.astype(jnp.int32).astype(piece.dtype)
+
+
+def angle_kernel(direct, count, slots, first, offsets, phase, footprint, inverse, sums, *refs):
     lists = count if direct else 1
-    arrived, residual, sent, windows = (
-        refs[:lists],
-        refs[lists],
-        refs[lists + 1 : 2 * lists + 1],
-        refs[2 * lists + 1],
-    )
+    arrived, residual, windows, sent = refs[:lists], refs[lists], refs[lists + 1], refs[lists + 2 :]
     member = lax.axis_index("tile")
     table = footprint[...]
-    rows, columns = phase.shape
+    blocks, rows, half = phase.shape
     voxels = footprint.shape[0]
-    half = footprint.shape[1] // 2
-    blocks = columns // half
-    residual[...] = phase[...]
 
     def subtract(piece, group):
         start = group_start(offsets, member, group, slots)
@@ -212,80 +251,112 @@
             if s > 0:
                 far = image[(s - 1) * rows : s * rows, half:]
                 part = far if part is None else part + far
-            block = jnp.minimum(start + s, blocks - 1)
-            if s >= SPREAD - 1:
-                part = jnp.where(start + s < blocks, part, 0.0)
-            at = pl.ds(pl.multiple_of(block * half, half), half)
-            residual[:, at] = residual[:, at] - part
+            block = start + s
+            if s == SPREAD:
+                part = jnp.where(block < blocks, part, 0.0)
+                block = jnp.minimum(block, blocks - 1)
+            residual[block] = residual[block] - part
 
     each_piece(direct, count, member, arrived, subtract)
 
-    def send(piece, group):
+    def weigh(window, group):
         start = group_start(offsets, member, group, slots)
         for s in range(SPREAD + 1):
             block = jnp.minimum(start + s, blocks - 1)
-            at = pl.ds(pl.multiple_of(block * half, half), half)
             scale = inverse[pl.ds(start + s, 1), :]
-            windows[:, s * half : (s + 1) * half] = (residual[:, at] * scale).astype(windows.dtype)
-        stacked = jnp.concatenate(
-            [windows[:, s * half : (s + 2) * half] for s in range(SPREAD)], axis=0
-        )
-        back = lax.dot_general(
-            stacked, table, (((1,), (1,)), ((), ())), preferred_element_type=jnp.float32
-        )
-        top = jnp.max(jnp.max(jnp.abs(back), axis=1, keepdims=True), axis=0, keepdims=True)
-        power = jnp.floor(jnp.log2(CODE_TOP / jnp.maximum(top, 1e-30)))
-        code = jnp.round(back * jnp.exp2(power)).astype(jnp.int32)
-        for s in range(SPREAD):
-            for h in range(2):
-                base = (2 * s + h) * rows
-                piece[base : base + rows, :] = code[
-                    s * rows : (s + 1) * rows, h * half : (h + 1) * half
-                ].astype(piece.dtype)
-        base = 2 * SPREAD * rows
-        line = lax.broadcasted_iota(jnp.int32, (EXTRA_ROWS, half), 0)
-        extra = jnp.where(line < 4, sums[...], jnp.broadcast_to(power, (EXTRA_ROWS, half)))
-        piece[base : base + EXTRA_ROWS, :] = extra.astype(jnp.int32).astype(piece.dtype)
-
-    each_piece(direct, count, member, sent, send)
-
-
-def gather_kernel(direct, count, slots, rows, offsets, tile_count, *refs):
-    lists = count if direct else 1
-    received, correction, decoded, column_sums = (
-        refs[:lists],
-        refs[lists],
-        refs[lists + 1],
-        refs[lists + 2],
-    )
+            window[:, s * half : (s + 1) * half] = (residual[block] * scale).astype(window.dtype)
+
+    if direct:
+        for k in first:
+            weigh(windows.at[k], member ^ k)
+        for piece, k in zip(sent, first):
+            encode(windows[k], table, sums[...], piece)
+        for k in range(count):
+            if k not in first:
+                weigh(windows.at[k], member ^ k)
+    else:
+
+        def step(k, carry):
+            weigh(windows.at[k], k)
+            encode(windows[k], table, sums[...], sent[0].at[k])
+            return carry
+
+        lax.fori_loop(0, count, step, 0)
+
+
+def back_kernel(ks, windows, footprint, sums, *sent):
+    for piece, k in zip(sent, ks):
+        encode(windows[k], footprint[...], sums[...], piece)
+
+
+def gather_kernel(direct, ks, slots, rows, last, offsets, tile_count, *refs):
+    lists = len(ks) if direct else 1
+    received = refs[:lists]
+    refs = refs[lists:]
+    earlier = None
+    if direct and last:
+        earlier, earlier_sums, refs = refs[0], refs[1], refs[2:]
+    correction, column_sums, decoded = refs
     member = lax.axis_index("tile")
     live = tile_count[member]
     half = column_sums.shape[1]
     base = 2 * SPREAD * rows
-    column_sums[...] = jnp.zeros_like(column_sums)
-    correction[...] = jnp.zeros_like(correction)
-
-    def one(piece, angle):
+
+    def unpack(piece, into):
         extra = piece[base : base + EXTRA_ROWS, :].astype(jnp.float32)
-        column_sums[...] += (extra[0:2] + extra[2:4] * (1.0 / LOW_SCALE)) * (1.0 / SUM_SCALE)
-        scale = jnp.exp2(-extra[4:5])
-        start = group_start(offsets, angle, member, slots)
-        decoded[...] = piece[0:base, :].astype(jnp.float32) * scale
-        for j in range(slots):
-            place = offsets[angle, member * slots + j] - start
-            at = pl.multiple_of(place * (2 * rows), 2 * rows)
+        into[...] = piece[0:base, :].astype(jnp.float32) * jnp.exp2(-extra[4:5])
+        return (extra[0:2] + extra[2:4] * (1.0 / LOW_SCALE)) * (1.0 / SUM_SCALE)
+
+    def block_of(into, angle, start, j):
+        at = (offsets[angle, member * slots + j] - start) * (2 * rows)
+        return into[pl.ds(pl.multiple_of(at, 2 * rows), 2 * rows), :]
+
+    if direct:
+        total = earlier_sums[0:2] if last else jnp.zeros((2, half), jnp.float32)
+        angles = [member ^ k for k in ks]
+        starts = []
+        for i, piece in enumerate(received):
+            total = total + unpack(piece, decoded.at[i])
+            starts.append(group_start(offsets, angles[i], member, slots))
+    else:
+        column_sums[...] = jnp.zeros_like(column_sums)
+        correction[...] = jnp.zeros_like(correction)
+
+        def step(k, carry):
+            column_sums[0:2] += unpack(received[0].at[k], decoded.at[0])
+            start = group_start(offsets, k, member, slots)
+            for j in range(slots):
+                correction[j] += block_of(decoded.at[0], k, start, j)
+            return carry
+
+        lax.fori_loop(0, len(ks), step, 0)
+        total = column_sums[0:2]
+
+    if last:
+        inverse = 1.0 / total
+    else:
+        column_sums[0:2] = total
+    for j in range(slots):
+        if direct:
+            sum_here = earlier[j] if last else None
+            for i, angle in enumerate(angles):
+                part = block_of(decoded.at[i], angle, starts[i], j)
+                sum_here = part if sum_here is None else sum_here + part
+        else:
+            sum_here = correction[j]
+        if not last:
+            correction[j] = sum_here
+        elif direct:
+            weight = jnp.where(j < live, 1.0, 0.0)
             for h in range(2):
-                correction[j, :, h * half : (h + 1) * half] += decoded[
-                    pl.ds(at + h * rows, rows), :
-                ]
-
-    each_piece(direct, count, member, received, one)
-    inverse = 1.0 / column_sums[...]
-    for j in range(slots):
-        weight = jnp.where(j < live, 1.0, 0.0)
-        for h in range(2):
-            part = correction[j, :, h * half : (h + 1) * half]
-            correction[j, :, h * half : (h + 1) * half] = part * (inverse[h : h + 1] * weight)
+                correction[j, :, h * half : (h + 1) * half] = sum_here[
+                    h * rows : (h + 1) * rows
+                ] * (inverse[h : h + 1] * weight)
+        else:
+            weight = jnp.where(j < live, 1.0, 0.0)
+            correction[j] = sum_here * weight * jnp.concatenate(
+                [jnp.broadcast_to(inverse[h : h + 1], (rows, half)) for h in range(2)], axis=0
+            )
 
 
 def exchange(direct, count, pieces):
@@ -346,47 +417,95 @@
         compiler_params=params(16),
         name="loads",
     )(*[pltpu.with_memory_space_constraint(x, pltpu.HBM) for x in (offsets, tile_count, volume, table, intensity[0])])
+    near_rows, far_rows = swap_halos(near_rows, far_rows)
     arrived = exchange(direct, count, loads)
-    near_rows, far_rows = swap_halos(near_rows, far_rows)
-
+
+    taps = jnp.asarray(tap_matrix(half, TERMS))
+    tall = rows + 2 * HALO
     phase_map, inverse, sums = pl.pallas_call(
         lambda *refs: phase_kernel(slots, *refs),
         out_shape=[
-            jax.ShapeDtypeStruct((rows, columns), jnp.float32),
+            jax.ShapeDtypeStruct((blocks, rows, half), jnp.float32),
             jax.ShapeDtypeStruct((padded_blocks, half), jnp.float32),
             jax.ShapeDtypeStruct((EXTRA_ROWS, half), jnp.float32),
         ],
-        in_specs=[SMEM] + [VMEM] * 5,
+        in_specs=[SMEM] + [VMEM] * 6,
         out_specs=[VMEM] * 3,
-        scratch_shapes=[pltpu.VMEM((rows, columns + 2 * half), jnp.float32)],
+        scratch_shapes=[
+            pltpu.VMEM((tall, columns + 2 * half), intensity.dtype),
+            pltpu.VMEM((blocks, tall, half), jnp.float32),
+        ],
         compiler_params=params(16),
         name="phase",
-    )(counts_here, offsets_here, intensity[0], near_rows, far_rows, table)
-
-    back_shapes = piece_shapes((2 * SPREAD * rows + EXTRA_ROWS, half), jnp.int16)
-    residual, *backs = pl.pallas_call(
-        lambda *refs: angle_kernel(direct, count, slots, *refs),
-        out_shape=[jax.ShapeDtypeStruct((rows, columns), jnp.float32)] + back_shapes,
+    )(counts_here, offsets_here, intensity[0], near_rows, far_rows, table, taps)
+
+    piece_shape = (2 * SPREAD * rows + EXTRA_ROWS, half)
+    one_piece = jax.ShapeDtypeStruct(piece_shape, jnp.int16)
+    first = list(range(count - 1, 0, -1))[:FIRST] if direct else []
+    rest = [k for k in range(count) if k not in first]
+    sent_shapes = [one_piece] * len(first) if direct else piece_shapes(piece_shape, jnp.int16)
+    residual, windows, *sent = pl.pallas_call(
+        lambda *refs: angle_kernel(direct, count, slots, first, *refs),
+        out_shape=[
+            jax.ShapeDtypeStruct((blocks, rows, half), jnp.float32),
+            jax.ShapeDtypeStruct((count, rows, (SPREAD + 1) * half), jnp.bfloat16),
+        ]
+        + sent_shapes,
         in_specs=[SMEM] + [VMEM] * (4 + len(arrived)),
-        out_specs=[VMEM] * (1 + len(back_shapes)),
-        scratch_shapes=[pltpu.VMEM((rows, (SPREAD + 1) * half), jnp.bfloat16)],
-        compiler_params=params(24),
+        out_specs=[VMEM] * (2 + len(sent_shapes)),
+        input_output_aliases={1: 0},
+        compiler_params=params(16),
         name="angle",
     )(offsets_here, phase_map, table, inverse, sums, *arrived)
-    received = exchange(direct, count, backs)
-
-    correction = pl.pallas_call(
-        lambda *refs: gather_kernel(direct, count, slots, rows, *refs),
-        out_shape=jax.ShapeDtypeStruct((slots, rows, voxels), jnp.float32),
-        in_specs=[SMEM, SMEM] + [VMEM] * len(received),
+    if direct:
+        others = pl.pallas_call(
+            lambda *refs: back_kernel(rest, *refs),
+            out_shape=[one_piece] * len(rest),
+            in_specs=[VMEM] * 3,
+            out_specs=[VMEM] * len(rest),
+            compiler_params=params(16),
+            name="back",
+        )(windows, table, sums)
+        by_partner = dict(zip(first + rest, [*sent, *others]))
+        sent = [by_partner[k] for k in range(count)]
+    received = exchange(direct, count, sent)
+
+    residual = pl.pallas_call(
+        write_kernel,
+        out_shape=jax.ShapeDtypeStruct((rows, columns), jnp.float32),
+        in_specs=[VMEM],
         out_specs=VMEM,
-        scratch_shapes=[
-            pltpu.VMEM((2 * SPREAD * rows, half), jnp.float32),
-            pltpu.VMEM((2, half), jnp.float32),
-        ],
         compiler_params=params(16),
-        name="gather",
-    )(offsets_here, counts_here, *received)
+        name="write",
+    )(residual)
+
+    def gather(ks, pieces, last, *earlier):
+        flat = (slots, 2 * rows, half)
+        shape = (slots, rows, voxels) if direct and last else flat
+        return pl.pallas_call(
+            lambda *refs: gather_kernel(direct, ks, slots, rows, last, *refs),
+            out_shape=[
+                jax.ShapeDtypeStruct(shape, jnp.float32),
+                jax.ShapeDtypeStruct((8, half), jnp.float32),
+            ],
+            in_specs=[SMEM, SMEM] + [VMEM] * (len(pieces) + len(earlier)),
+            out_specs=[VMEM, VMEM],
+            scratch_shapes=[
+                pltpu.VMEM((len(pieces), 2 * SPREAD * rows, half), jnp.float32),
+            ],
+            compiler_params=params(16),
+            name="gather_last" if last else "gather_first",
+        )(offsets_here, counts_here, *pieces, *earlier)
+
+    if direct:
+        near = list(range(count // 2))
+        far = list(range(count // 2, count))
+        partial = gather(near, received[: count // 2], False)
+        correction = gather(far, received[count // 2 :], True, *partial)[0]
+    else:
+        flat = gather(list(range(count)), received, True)[0]
+        correction = jnp.swapaxes(flat.reshape(slots, 2, rows, half), 1, 2)
+        correction = correction.reshape(slots, rows, voxels)
     return residual[None], correction
 
 

time: 46.2 us -> 46.2 us (level)
  the two profiles are of different devices: /device:TPU:8 before, /device:TPU:0 now
where the time goes in v3:
time: 46.2 us; the launch traced here: 46 us
  starting transfers between devices  26.6 us (58%)
  Pallas kernels  9.55 us (21%)
  waiting for transfers between devices  8.1 us (18%)
  local copies, waits for them, and re-layouts  1.05 us (2%)
  between operations  0.73 us (2%)
    ppermute x14, starting transfers between devices, exchange(): lax.ppermute(pieces[k], 'tile', [(i, i ^ k) for i in range(count)])  25.3 us
    ppermute x14, waiting for transfers between devices, exchange(): lax.ppermute(pieces[k], 'tile', [(i, i ^ k) for i in range(count)])  8.1 us
    pallas_call x1, Pallas kernels, local(): pl.pallas_call(lambda *refs: phase_kernel(slots, *refs), out_shape=[jax.S...  2.57 us
    pallas_call x2, Pallas kernels, gather(): pl.pallas_call(lambda *refs: gather_kernel(direct, ks, slots, rows, last,...  2.18 us
    pallas_call x1, Pallas kernels, local(): pl.pallas_call(lambda *refs: load_kernel(direct, count, slots, *refs), ou...  1.69 us
    pallas_call x1, Pallas kernels, local(): pl.pallas_call(lambda *refs: angle_kernel(direct, count, slots, first, *r...  1.41 us
    pallas_call x1, Pallas kernels, local(): pl.pallas_call(write_kernel, out_shape=jax.ShapeDtypeStruct((rows, column...  1.19 us
    unnamed x4, local copies, waits for them, and re-layouts  1.05 us
  transfers between devices with their start and end apart: 16, of which 6 were waited for; matrix products, arithmetic and copies ran while one was open for 0% of the time, Pallas kernels for 10%

profile of v3, /device:TPU:0, one launch (start us, length us, event | category | flops | bytes accessed | tf_op | source)
XLA Modules:
  0.0 46.0 jit_solution(7108100294519855638)
XLA Ops:
  0.6 1.7 %loads.1 = (bf16[8,11264]{1,0:T(8,128)(2,1)S(1)}, bf16[8,11264]{1,0:T(8,128)(2,1)S(1)}, bf16[256,256]{1,0:T(8,128)(2,1)S(1)}, s32[8,64]{1,0:T(8,128)S(1)}, s32[8...) custom-call(s32[8,64]{1,0:T(8,128)} %bitcast.8, ...), custom_call_target="tpu_custom_call" | custom-call | tf_op jit(solution)/shard_map/loads/pallas_call | solution.py:404
  2.3 0.6 %collective-permute-start = (bf16[8,11264]{1,0:T(8,128)(2,1)S(1)}, bf16[8,11264]{1,0:T(8,128)(2,1)S(1)}, u32[]{:S(2)}, u32[]{:S(2)}) collective-permute-start(bf16[8,11264]{1,0:T(8,128)(2,1)S(1)} %get-tuple-element.33), channel_id=1, source_target_pairs={{0,1},{2,3},{1,0},{3,2},{4,5},{6,7},{5,4},{7,6},{8,9},{10,11},{9,8... | collective-permute-start | bytes 540680 | tf_op jit(solution)/shard_map/ppermute | solution.py:376
  2.9 0.7 %collective-permute-start.1 = (bf16[8,11264]{1,0:T(8,128)(2,1)S(1)}, bf16[8,11264]{1,0:T(8,128)(2,1)S(1)}, u32[]{:S(2)}, u32[]{:S(2)}) collective-permute-start(bf16[8,11264]{1,0:T(8,128)(2,1)S(1)} %get-tuple-element.34), channel_id=1, source_target_pairs={{1,2},{2,1},{5,6},{6,5},{9,10},{10,9},{13,14},{14,13},{17,18},{18,... | collective-permute-start | bytes 540680 | tf_op jit(solution)/shard_map/ppermute | solution.py:375
  3.6 2.6 %collective-permute-start.2 = (bf16[4,32,256]{2,1,0:T(8,128)(2,1)S(1)}, bf16[4,32,256]{2,1,0:T(8,128)(2,1)S(1)}, u32[]{:S(2)}, u32[]{:S(2)}) collective-permute-start(bf16[4,32,256]{2,1,0:T(8,128)(2,1)S(1)} %get-tuple-element.40), channel_id=1, source_target_pairs={{0,4},{4,0},{8,12},{12,8},{16,20},{20,16},{24,28},{28,24},{1,5},{5... | collective-permute-start | bytes 196616 | tf_op jit(solution)/shard_map/ppermute | solution.py:367
  6.2 1.6 %collective-permute-start.3 = (bf16[4,32,256]{2,1,0:T(8,128)(2,1)S(1)}, bf16[4,32,256]{2,1,0:T(8,128)(2,1)S(1)}, u32[]{:S(2)}, u32[]{:S(2)}) collective-permute-start(bf16[4,32,256]{2,1,0:T(8,128)(2,1)S(1)} %get-tuple-element.41), channel_id=1, source_target_pairs={{0,8},{4,12},{8,0},{12,4},{16,24},{20,28},{24,16},{28,20},{1,9},{5... | collective-permute-start | bytes 196616 | tf_op jit(solution)/shard_map/ppermute | solution.py:367
  7.7 0.7 %collective-permute-done.2.refs_6_ = bf16[4,32,256]{2,1,0:T(8,128)(2,1)S(1)} collective-permute-done((bf16[4,32,256]{2,1,0:T(8,128)(2,1)S(1)}, bf16[4,32,256]{2,1,0:T(8,128)(2,1)S(1)}, u32[]{:S(2)}, u32[]{:S(2)}) %collective-permute-start.2) | collective-permute-done | bytes 65568 | tf_op jit(solution)/shard_map/ppermute | solution.py:367
  8.4 3.1 %collective-permute-start.5 = (bf16[4,32,256]{2,1,0:T(8,128)(2,1)S(1)}, bf16[4,32,256]{2,1,0:T(8,128)(2,1)S(1)}, u32[]{:S(2)}, u32[]{:S(2)}) collective-permute-start(bf16[4,32,256]{2,1,0:T(8,128)(2,1)S(1)} %get-tuple-element.43), channel_id=1, source_target_pairs={{0,16},{4,20},{8,24},{12,28},{16,0},{20,4},{24,8},{28,12},{1,17},{... | collective-permute-start | bytes 196616 | tf_op jit(solution)/shard_map/ppermute | solution.py:367
  11.5 0.0 collective-permute-done.3.refs_7_
  11.5 1.5 %collective-permute-start.6 = (bf16[4,32,256]{2,1,0:T(8,128)(2,1)S(1)}, bf16[4,32,256]{2,1,0:T(8,128)(2,1)S(1)}, u32[]{:S(2)}, u32[]{:S(2)}) collective-permute-start(bf16[4,32,256]{2,1,0:T(8,128)(2,1)S(1)} %get-tuple-element.44), channel_id=1, source_target_pairs={{0,20},{4,16},{8,28},{12,24},{16,4},{20,0},{24,12},{28,8},{1,21},{... | collective-permute-start | bytes 196616 | tf_op jit(solution)/shard_map/ppermute | solution.py:367
  13.0 3.4 %collective-permute-start.7 = (bf16[4,32,256]{2,1,0:T(8,128)(2,1)S(1)}, bf16[4,32,256]{2,1,0:T(8,128)(2,1)S(1)}, u32[]{:S(2)}, u32[]{:S(2)}) collective-permute-start(bf16[4,32,256]{2,1,0:T(8,128)(2,1)S(1)} %get-tuple-element.45), channel_id=1, source_target_pairs={{0,24},{4,28},{8,16},{12,20},{16,8},{20,12},{24,0},{28,4},{1,25},{... | collective-permute-start | bytes 196616 | tf_op jit(solution)/shard_map/ppermute | solution.py:367
  16.4 0.0 collective-permute-done.1.refs_4_
  16.4 1.3 %collective-permute-start.8 = (bf16[4,32,256]{2,1,0:T(8,128)(2,1)S(1)}, bf16[4,32,256]{2,1,0:T(8,128)(2,1)S(1)}, u32[]{:S(2)}, u32[]{:S(2)}) collective-permute-start(bf16[4,32,256]{2,1,0:T(8,128)(2,1)S(1)} %get-tuple-element.46), channel_id=1, source_target_pairs={{0,28},{4,24},{8,20},{12,16},{16,12},{20,8},{24,4},{28,0},{1,29},{... | collective-permute-start | bytes 196616 | tf_op jit(solution)/shard_map/ppermute | solution.py:367
  17.7 1.0 %copy-done.1 = bf16[1024,256]{1,0:T(8,128)(2,1)S(1)} copy-done((bf16[1024,256]{1,0:T(8,128)(2,1)S(1)}, bf16[1024,256]{1,0:T(8,128)(2,1)}, u32[]{:S(2)}) %copy-start.1) | copy-done | bytes 524312
  18.8 2.6 %phase.1 = (f32[88,32,128]{2,1,0:T(8,128)S(1)}, f32[96,128]{1,0:T(8,128)S(1)}, f32[8,128]{1,0:T(8,128)S(1)}) custom-call(s32[8]{0:T(128)S(1)} %get-tuple-element.32.refs_0_.refs_1_, s32[8,64]{1,0:T(8,128)S(1)} %get-tuple-element.31.refs_1_.refs_0_, bf16[32,11264]{1,0:T(8,128)(2,1)S(1)} %bitcast.5, bf16[8,11264]{1,0:T(8,128)(2,1)S(1)} %collective-permute-done.refs_3_, ...), custom_call_target="tpu_custom_call" | custom-call | tf_op jit(solution)/shard_map/phase/pallas_call | solution.py:425
  21.4 0.0 collective-permute-done.5.refs_9_
  21.4 0.3 collective-permute-done.6.refs_10_
  21.7 0.0 collective-permute-done.7.refs_11_
  21.7 1.9 %collective-permute-done.8.refs_12_ = bf16[4,32,256]{2,1,0:T(8,128)(2,1)S(1)} collective-permute-done((bf16[4,32,256]{2,1,0:T(8,128)(2,1)S(1)}, bf16[4,32,256]{2,1,0:T(8,128)(2,1)S(1)}, u32[]{:S(2)}, u32[]{:S(2)}) %collective-permute-start.8) | collective-permute-done | bytes 65568 | tf_op jit(solution)/shard_map/ppermute | solution.py:367
  23.6 1.4 %angle.1 = (f32[88,32,128]{2,1,0:T(8,128)S(1)}, bf16[8,32,640]{2,1,0:T(8,128)(2,1)S(1)}, s16[264,128]{1,0:T(8,128)(2,1)S(1)}, s16[264,128]{1,0:T(8,128)(2,1)S(1)}, s16[264,128]{1,0:T(8,128)(2,1)S(1)}) custom-call(s32[8,64]{1,0:T(8,128)S(1)} %get-tuple-element.31.refs_1_.refs_0_, ...), custom_call_target="tpu_custom_call", output_to_operand_aliasing={{0}: (1, {})} | custom-call | tf_op jit(solution)/shard_map/angle/pallas_call | solution.py:447
  25.0 0.5 %back.1 = (s16[264,128]{1,0:T(8,128)(2,1)S(1)}, s16[264,128]{1,0:T(8,128)(2,1)S(1)}, s16[264,128]{1,0:T(8,128)(2,1)S(1)}, s16[264,128]{1,0:T(8,128)(2,1)S(1)}, s16[264,128]{1,0:T(8,128)(2,1)S(1)}) custom-call(bf16[8,32,640]{2,1,0:T(8,128)(2,1)S(1)} %get-tuple-element.48.refs_0_, bf16[256,256]{1,0:T(8,128)(2,1)S(1)} %get-tuple-element.35.refs_5_.refs_2_.refs_1_, ...), custom_call_target="tpu_custom_call" | custom-call | tf_op jit(solution)/shard_map/back/pallas_call | solution.py:461
  25.5 1.1 %collective-permute-start.13 = (s16[264,128]{1,0:T(8,128)(2,1)S(1)}, s16[264,128]{1,0:T(8,128)(2,1)S(1)}, u32[]{:S(2)}, u32[]{:S(2)}) collective-permute-start(s16[264,128]{1,0:T(8,128)(2,1)S(1)} %get-tuple-element.54), channel_id=1, source_target_pairs={{0,4},{4,0},{8,12},{12,8},{16,20},{20,16},{24,28},{28,24},{1,5},{5... | collective-permute-start | bytes 202760 | tf_op jit(solution)/shard_map/ppermute | solution.py:367
  26.6 2.3 %collective-permute-start.14 = (s16[264,128]{1,0:T(8,128)(2,1)S(1)}, s16[264,128]{1,0:T(8,128)(2,1)S(1)}, u32[]{:S(2)}, u32[]{:S(2)}) collective-permute-start(s16[264,128]{1,0:T(8,128)(2,1)S(1)} %get-tuple-element.55), channel_id=1, source_target_pairs={{0,8},{4,12},{8,0},{12,4},{16,24},{20,28},{24,16},{28,20},{1,9},{5... | collective-permute-start | bytes 202760 | tf_op jit(solution)/shard_map/ppermute | solution.py:367
  28.9 2.6 %collective-permute-start.10 = (s16[264,128]{1,0:T(8,128)(2,1)S(1)}, s16[264,128]{1,0:T(8,128)(2,1)S(1)}, u32[]{:S(2)}, u32[]{:S(2)}) collective-permute-start(s16[264,128]{1,0:T(8,128)(2,1)S(1)} %get-tuple-element.50), channel_id=1, source_target_pairs={{0,20},{4,16},{8,28},{12,24},{16,4},{20,0},{24,12},{28,8},{1,21},{... | collective-permute-start | bytes 202760 | tf_op jit(solution)/shard_map/ppermute | solution.py:367
  31.5 0.8 %collective-permute-start.11 = (s16[264,128]{1,0:T(8,128)(2,1)S(1)}, s16[264,128]{1,0:T(8,128)(2,1)S(1)}, u32[]{:S(2)}, u32[]{:S(2)}) collective-permute-start(s16[264,128]{1,0:T(8,128)(2,1)S(1)} %get-tuple-element.51), channel_id=1, source_target_pairs={{0,24},{4,28},{8,16},{12,20},{16,8},{20,12},{24,0},{28,4},{1,25},{... | collective-permute-start | bytes 202760 | tf_op jit(solution)/shard_map/ppermute | solution.py:367
  32.3 1.2 %collective-permute-start.15 = (s16[264,128]{1,0:T(8,128)(2,1)S(1)}, s16[264,128]{1,0:T(8,128)(2,1)S(1)}, u32[]{:S(2)}, u32[]{:S(2)}) collective-permute-start(s16[264,128]{1,0:T(8,128)(2,1)S(1)} %get-tuple-element.56), channel_id=1, source_target_pairs={{0,12},{4,8},{8,4},{12,0},{16,28},{20,24},{24,20},{28,16},{1,13},{... | collective-permute-start | bytes 202760 | tf_op jit(solution)/shard_map/ppermute | solution.py:367
  33.5 3.9 %collective-permute-start.12 = (s16[264,128]{1,0:T(8,128)(2,1)S(1)}, s16[264,128]{1,0:T(8,128)(2,1)S(1)}, u32[]{:S(2)}, u32[]{:S(2)}) collective-permute-start(s16[264,128]{1,0:T(8,128)(2,1)S(1)} %get-tuple-element.52), channel_id=1, source_target_pairs={{0,28},{4,24},{8,20},{12,16},{16,12},{20,8},{24,4},{28,0},{1,29},{... | collective-permute-start | bytes 202760 | tf_op jit(solution)/shard_map/ppermute | solution.py:367
  37.4 1.2 %write.1 = f32[32,11264]{1,0:T(8,128)} custom-call(f32[88,32,128]{2,1,0:T(8,128)S(1)} %get-tuple-element.47.residual), custom_call_target="tpu_custom_call" | custom-call | tf_op jit(solution)/shard_map/write/pallas_call | solution.py:473
  38.6 0.5 %collective-permute-done.15.refs_5_ = s16[264,128]{1,0:T(8,128)(2,1)S(1)} collective-permute-done((s16[264,128]{1,0:T(8,128)(2,1)S(1)}, s16[264,128]{1,0:T(8,128)(2,1)S(1)}, u32[]{:S(2)}, u32[]{:S(2)}) %collective-permute-start.15) | collective-permute-done | bytes 67616 | tf_op jit(solution)/shard_map/ppermute | solution.py:367
  39.1 0.7 %gather_first.1 = (f32[8,64,128]{2,1,0:T(8,128)S(1)}, f32[8,128]{1,0:T(8,128)S(1)}) custom-call(s32[8,64]{1,0:T(8,128)S(1)} %get-tuple-element.31.refs_1_.refs_0_, s32[8]{0:T(128)S(1)} %get-tuple-element.32.refs_0_.refs_1_, s16[264,128]{1,0:T(8,128)(2,1)S(1)} %get-tuple-element.53.refs_2_, s16[264,128]{1,0:T(8,128)(2,1)S(1)} %collective-permute-done.13.refs_3_, ...), custom_call_target="tpu_custom_call" | custom-call | tf_op jit(solution)/shard_map/gather_first/pallas_call | solution.py:485
  39.9 1.5 %collective-permute-done.12.refs_5_ = s16[264,128]{1,0:T(8,128)(2,1)S(1)} collective-permute-done((s16[264,128]{1,0:T(8,128)(2,1)S(1)}, s16[264,128]{1,0:T(8,128)(2,1)S(1)}, u32[]{:S(2)}, u32[]{:S(2)}) %collective-permute-start.12) | collective-permute-done | bytes 67616 | tf_op jit(solution)/shard_map/ppermute | solution.py:367
  41.3 3.2 %collective-permute-done.9.refs_2_ = s16[264,128]{1,0:T(8,128)(2,1)S(1)} collective-permute-done((s16[264,128]{1,0:T(8,128)(2,1)S(1)}, s16[264,128]{1,0:T(8,128)(2,1)S(1)}, u32[]{:S(2)}, u32[]{:S(2)}) %collective-permute-start.9) | collective-permute-done | bytes 67616 | tf_op jit(solution)/shard_map/ppermute | solution.py:367
  44.5 1.4 %gather_last.1 = (f32[8,32,256]{2,1,0:T(8,128)}, f32[8,128]{1,0:T(8,128)}) custom-call(s32[8,64]{1,0:T(8,128)S(1)} %get-tuple-element.31.refs_1_.refs_0_, s32[8]{0:T(128)S(1)} %get-tuple-element.32.refs_0_.refs_1_, s16[264,128]{1,0:T(8,128)(2,1)S(1)} %collective-permute-done.9.refs_2_, s16[264,128]{1,0:T(8,128)(2,1)S(1)} %collective-permute-done.10.refs_3_, ...), custom_call_target="tpu_custom_call" | custom-call | tf_op jit(solution)/shard_map/gather_last/pallas_call | solution.py:485
  (11 shorter events, 0.0 us)
Async XLA Ops:
  0.6 17.1 %copy-start = (bf16[1,32,11264]{2,1,0:T(8,128)(2,1)S(1)}, bf16[1,32,11264]{2,1,0:T(8,128)(2,1)}, u32[]{:S(2)}) copy-start(bf16[1,32,11264]{2,1,0:T(8,128)(2,1)} %param.6) | copy-start | bytes 2162692
  2.3 10.6 %collective-permute-start = (bf16[8,11264]{1,0:T(8,128)(2,1)S(1)}, bf16[8,11264]{1,0:T(8,128)(2,1)S(1)}, u32[]{:S(2)}, u32[]{:S(2)}) collective-permute-start(bf16[8,11264]{1,0:T(8,128)(2,1)S(1)} %get-tuple-element.33), channel_id=1, source_target_pairs={{0,1},{2,3},{1,0},{3,2},{4,5},{6,7},{5,4},{7,6},{8,9},{10,11},{9,8... | collective-permute-start | bytes 540680 | tf_op jit(solution)/shard_map/ppermute | solution.py:376
  2.9 13.5 %collective-permute-start.1 = (bf16[8,11264]{1,0:T(8,128)(2,1)S(1)}, bf16[8,11264]{1,0:T(8,128)(2,1)S(1)}, u32[]{:S(2)}, u32[]{:S(2)}) collective-permute-start(bf16[8,11264]{1,0:T(8,128)(2,1)S(1)} %get-tuple-element.34), channel_id=1, source_target_pairs={{1,2},{2,1},{5,6},{6,5},{9,10},{10,9},{13,14},{14,13},{17,18},{18,... | collective-permute-start | bytes 540680 | tf_op jit(solution)/shard_map/ppermute | solution.py:375
  3.6 4.8 %collective-permute-start.2 = (bf16[4,32,256]{2,1,0:T(8,128)(2,1)S(1)}, bf16[4,32,256]{2,1,0:T(8,128)(2,1)S(1)}, u32[]{:S(2)}, u32[]{:S(2)}) collective-permute-start(bf16[4,32,256]{2,1,0:T(8,128)(2,1)S(1)} %get-tuple-element.40), channel_id=1, source_target_pairs={{0,4},{4,0},{8,12},{12,8},{16,20},{20,16},{24,28},{28,24},{1,5},{5... | collective-permute-start | bytes 196616 | tf_op jit(solution)/shard_map/ppermute | solution.py:367
  6.2 5.3 %collective-permute-start.3 = (bf16[4,32,256]{2,1,0:T(8,128)(2,1)S(1)}, bf16[4,32,256]{2,1,0:T(8,128)(2,1)S(1)}, u32[]{:S(2)}, u32[]{:S(2)}) collective-permute-start(bf16[4,32,256]{2,1,0:T(8,128)(2,1)S(1)} %get-tuple-element.41), channel_id=1, source_target_pairs={{0,8},{4,12},{8,0},{12,4},{16,24},{20,28},{24,16},{28,20},{1,9},{5... | collective-permute-start | bytes 196616 | tf_op jit(solution)/shard_map/ppermute | solution.py:367
  7.7 13.6 %collective-permute-start.4 = (bf16[4,32,256]{2,1,0:T(8,128)(2,1)S(1)}, bf16[4,32,256]{2,1,0:T(8,128)(2,1)S(1)}, u32[]{:S(2)}, u32[]{:S(2)}) collective-permute-start(bf16[4,32,256]{2,1,0:T(8,128)(2,1)S(1)} %get-tuple-element.42), channel_id=1, source_target_pairs={{0,12},{4,8},{8,4},{12,0},{16,28},{20,24},{24,20},{28,16},{1,13},{... | collective-permute-start | bytes 196616 | tf_op jit(solution)/shard_map/ppermute | solution.py:367
  8.4 13.0 %collective-permute-start.5 = (bf16[4,32,256]{2,1,0:T(8,128)(2,1)S(1)}, bf16[4,32,256]{2,1,0:T(8,128)(2,1)S(1)}, u32[]{:S(2)}, u32[]{:S(2)}) collective-permute-start(bf16[4,32,256]{2,1,0:T(8,128)(2,1)S(1)} %get-tuple-element.43), channel_id=1, source_target_pairs={{0,16},{4,20},{8,24},{12,28},{16,0},{20,4},{24,8},{28,12},{1,17},{... | collective-permute-start | bytes 196616 | tf_op jit(solution)/shard_map/ppermute | solution.py:367
  11.5 10.2 %collective-permute-start.6 = (bf16[4,32,256]{2,1,0:T(8,128)(2,1)S(1)}, bf16[4,32,256]{2,1,0:T(8,128)(2,1)S(1)}, u32[]{:S(2)}, u32[]{:S(2)}) collective-permute-start(bf16[4,32,256]{2,1,0:T(8,128)(2,1)S(1)} %get-tuple-element.44), channel_id=1, source_target_pairs={{0,20},{4,16},{8,28},{12,24},{16,4},{20,0},{24,12},{28,8},{1,21},{... | collective-permute-start | bytes 196616 | tf_op jit(solution)/shard_map/ppermute | solution.py:367
  13.0 8.7 %collective-permute-start.7 = (bf16[4,32,256]{2,1,0:T(8,128)(2,1)S(1)}, bf16[4,32,256]{2,1,0:T(8,128)(2,1)S(1)}, u32[]{:S(2)}, u32[]{:S(2)}) collective-permute-start(bf16[4,32,256]{2,1,0:T(8,128)(2,1)S(1)} %get-tuple-element.45), channel_id=1, source_target_pairs={{0,24},{4,28},{8,16},{12,20},{16,8},{20,12},{24,0},{28,4},{1,25},{... | collective-permute-start | bytes 196616 | tf_op jit(solution)/shard_map/ppermute | solution.py:367
  16.4 7.2 %collective-permute-start.8 = (bf16[4,32,256]{2,1,0:T(8,128)(2,1)S(1)}, bf16[4,32,256]{2,1,0:T(8,128)(2,1)S(1)}, u32[]{:S(2)}, u32[]{:S(2)}) collective-permute-start(bf16[4,32,256]{2,1,0:T(8,128)(2,1)S(1)} %get-tuple-element.46), channel_id=1, source_target_pairs={{0,28},{4,24},{8,20},{12,16},{16,12},{20,8},{24,4},{28,0},{1,29},{... | collective-permute-start | bytes 196616 | tf_op jit(solution)/shard_map/ppermute | solution.py:367
  17.7 1.0 %copy-start.1 = (bf16[1024,256]{1,0:T(8,128)(2,1)S(1)}, bf16[1024,256]{1,0:T(8,128)(2,1)}, u32[]{:S(2)}) copy-start(bf16[1024,256]{1,0:T(8,128)(2,1)} %constant.2.clone.refs_6_) | copy-start | bytes 1572868
  25.5 8.0 %collective-permute-start.13 = (s16[264,128]{1,0:T(8,128)(2,1)S(1)}, s16[264,128]{1,0:T(8,128)(2,1)S(1)}, u32[]{:S(2)}, u32[]{:S(2)}) collective-permute-start(s16[264,128]{1,0:T(8,128)(2,1)S(1)} %get-tuple-element.54), channel_id=1, source_target_pairs={{0,4},{4,0},{8,12},{12,8},{16,20},{20,16},{24,28},{28,24},{1,5},{5... | collective-permute-start | bytes 202760 | tf_op jit(solution)/shard_map/ppermute | solution.py:367
  26.6 10.8 %collective-permute-start.14 = (s16[264,128]{1,0:T(8,128)(2,1)S(1)}, s16[264,128]{1,0:T(8,128)(2,1)S(1)}, u32[]{:S(2)}, u32[]{:S(2)}) collective-permute-start(s16[264,128]{1,0:T(8,128)(2,1)S(1)} %get-tuple-element.55), channel_id=1, source_target_pairs={{0,8},{4,12},{8,0},{12,4},{16,24},{20,28},{24,16},{28,20},{1,9},{5... | collective-permute-start | bytes 202760 | tf_op jit(solution)/shard_map/ppermute | solution.py:367
  28.9 10.9 %collective-permute-start.10 = (s16[264,128]{1,0:T(8,128)(2,1)S(1)}, s16[264,128]{1,0:T(8,128)(2,1)S(1)}, u32[]{:S(2)}, u32[]{:S(2)}) collective-permute-start(s16[264,128]{1,0:T(8,128)(2,1)S(1)} %get-tuple-element.50), channel_id=1, source_target_pairs={{0,20},{4,16},{8,28},{12,24},{16,4},{20,0},{24,12},{28,8},{1,21},{... | collective-permute-start | bytes 202760 | tf_op jit(solution)/shard_map/ppermute | solution.py:367
  31.5 8.3 %collective-permute-start.11 = (s16[264,128]{1,0:T(8,128)(2,1)S(1)}, s16[264,128]{1,0:T(8,128)(2,1)S(1)}, u32[]{:S(2)}, u32[]{:S(2)}) collective-permute-start(s16[264,128]{1,0:T(8,128)(2,1)S(1)} %get-tuple-element.51), channel_id=1, source_target_pairs={{0,24},{4,28},{8,16},{12,20},{16,8},{20,12},{24,0},{28,4},{1,25},{... | collective-permute-start | bytes 202760 | tf_op jit(solution)/shard_map/ppermute | solution.py:367
  32.3 6.8 %collective-permute-start.15 = (s16[264,128]{1,0:T(8,128)(2,1)S(1)}, s16[264,128]{1,0:T(8,128)(2,1)S(1)}, u32[]{:S(2)}, u32[]{:S(2)}) collective-permute-start(s16[264,128]{1,0:T(8,128)(2,1)S(1)} %get-tuple-element.56), channel_id=1, source_target_pairs={{0,12},{4,8},{8,4},{12,0},{16,28},{20,24},{24,20},{28,16},{1,13},{... | collective-permute-start | bytes 202760 | tf_op jit(solution)/shard_map/ppermute | solution.py:367
  33.5 7.8 %collective-permute-start.12 = (s16[264,128]{1,0:T(8,128)(2,1)S(1)}, s16[264,128]{1,0:T(8,128)(2,1)S(1)}, u32[]{:S(2)}, u32[]{:S(2)}) collective-permute-start(s16[264,128]{1,0:T(8,128)(2,1)S(1)} %get-tuple-element.52), channel_id=1, source_target_pairs={{0,28},{4,24},{8,20},{12,16},{16,12},{20,8},{24,4},{28,0},{1,29},{... | collective-permute-start | bytes 202760 | tf_op jit(solution)/shard_map/ppermute | solution.py:367
  37.4 7.2 %collective-permute-start.9 = (s16[264,128]{1,0:T(8,128)(2,1)S(1)}, s16[264,128]{1,0:T(8,128)(2,1)S(1)}, u32[]{:S(2)}, u32[]{:S(2)}) collective-permute-start(s16[264,128]{1,0:T(8,128)(2,1)S(1)} %get-tuple-element.49), channel_id=1, source_target_pairs={{0,16},{4,20},{8,24},{12,28},{16,0},{20,4},{24,8},{28,12},{1,17},{... | collective-permute-start | bytes 202760 | tf_op jit(solution)/shard_map/ppermute | solution.py:367

commit v4 on v3

--- a/solution.py
+++ b/solution.py
@@ -12,7 +12,7 @@
 HALO = 8
 GROUP = 22
 TERMS = 2
-FIRST = 3
+FIRST = 1
 DIRECT_LIMIT = 16
 EXTRA_ROWS = 8
 SUM_SCALE = 2048.0
@@ -57,9 +57,11 @@
     return low
 
 
-def load_kernel(direct, count, slots, offsets_in, count_in, volume_in, table_in, intensity, *refs):
+def load_kernel(
+    direct, count, slots, offsets_in, count_in, volume_in, table_in, taps_in, intensity, *refs
+):
     lists = count if direct else 1
-    near_rows, far_rows, table_out, offsets_out, count_out = refs[:5]
+    near_rows, far_rows, table_out, taps_out, alive = refs[:5]
     pieces = refs[5 : 5 + lists]
     offsets, tile_count, volume, sems = refs[5 + lists :]
     member = lax.axis_index("tile")
@@ -67,25 +69,29 @@
     last = intensity.shape[0] - HALO
     first_copy = pltpu.make_async_copy(offsets_in, offsets, sems.at[0])
     count_copy = pltpu.make_async_copy(count_in, tile_count, sems.at[1])
-    volume_copy = pltpu.make_async_copy(volume_in, volume, sems.at[2])
     near = pl.multiple_of(jnp.where(even, last, 0), HALO)
     far = pl.multiple_of(jnp.where(even, 0, last), HALO)
     near_copy = pltpu.make_async_copy(intensity.at[pl.ds(near, HALO)], near_rows, sems.at[3])
     far_copy = pltpu.make_async_copy(intensity.at[pl.ds(far, HALO)], far_rows, sems.at[4])
     later = [near_copy, far_copy]
     for i, (here, there) in enumerate(
-        ((table_in, table_out), (offsets_in, offsets_out), (count_in, count_out))
+        ((table_in, table_out), (taps_in, taps_out))
     ):
         later.append(pltpu.make_async_copy(here, there, sems.at[5 + i]))
+    volume_copies = [
+        pltpu.make_async_copy(volume_in.at[j], volume.at[j], sems.at[8 + j]) for j in range(slots)
+    ]
+    for copy in volume_copies:
+        copy.start()
     first_copy.start()
     count_copy.start()
-    volume_copy.start()
     for copy in later:
         copy.start()
     first_copy.wait()
     count_copy.wait()
     live = tile_count[member]
-    volume_copy.wait()
+    for copy in volume_copies:
+        copy.wait()
 
     def one(piece, angle):
         start = group_start(offsets, angle, member, slots)
@@ -98,22 +104,29 @@
             piece[s] = total.astype(piece.dtype)
 
     each_piece(direct, count, member, pieces, one)
+    lane = lax.broadcasted_iota(jnp.int32, alive.shape, 1)
+    flags = jnp.zeros(alive.shape, jnp.float32)
+    for g in range(alive.shape[1] // slots):
+        here = (lane >= g * slots) & (lane < g * slots + tile_count[g])
+        flags = jnp.where(here, 1.0, flags)
+    alive[...] = flags
     for copy in later:
         copy.wait()
 
 
-def tables(slots, blocks, offset_rows, tile_count, table, inverse, sums):
+def tables(slots, blocks, offset_rows, alive, table, inverse, sums, starts):
     member = lax.axis_index("tile")
     half = table.shape[1] // 2
     padded = inverse.shape[0]
     total = offset_rows.shape[1]
     by_column = jnp.sum(table.astype(jnp.float32), axis=0, keepdims=True)
     mine = offset_rows[pl.ds(member, 1), :]
-    lane = lax.broadcasted_iota(jnp.int32, (1, total), 1)
-    alive = jnp.zeros((1, total), jnp.float32)
-    for g in range(total // slots):
-        here = (lane >= g * slots) & (lane < g * slots + tile_count[g])
-        alive = jnp.where(here, 1.0, alive)
+    group = lax.broadcasted_iota(jnp.int32, (starts.shape[0], total), 0)
+    lane = lax.broadcasted_iota(jnp.int32, (starts.shape[0], total), 1)
+    own = (lane >= group * slots) & (lane < (group + 1) * slots)
+    lowest = jnp.min(jnp.where(own, mine, 1 << 20), axis=1, keepdims=True)
+    starts[...] = jnp.broadcast_to(lowest, starts.shape)
+    alive = alive[0:1, :]
     block = lax.broadcasted_iota(jnp.int32, (padded, total), 0)
     hits = jnp.where(block == mine, alive, 0.0)
     counts = jnp.sum(hits, axis=1, keepdims=True)
@@ -147,12 +160,11 @@
     return np.concatenate(parts, axis=0)
 
 
-def phase_kernel(slots, tile_count, offset_rows, intensity, near_rows, far_rows, footprint, *refs):
-    taps, phase, inverse, sums, padded, across = refs
+def phase_kernel(slots, alive, offset_rows, intensity, near_rows, far_rows, footprint, *refs):
+    taps, phase, inverse, sums, starts, padded, across = refs
     rows, columns = intensity.shape
     half = footprint.shape[1] // 2
     blocks = columns // half
-    tables(slots, blocks, offset_rows, tile_count, footprint[...], inverse, sums)
     even = lax.rem(lax.axis_index("row"), 2) == 0
     decay = float(np.exp(-1.0 / decay_length))
     centre = float(smoothing_taps()[RIM])
@@ -166,6 +178,7 @@
     far = far_rows[...].astype(jnp.float32)
     padded[:HALO, inner] = jnp.where(even, far, near).astype(padded.dtype)
     padded[HALO + rows :, inner] = jnp.where(even, near, far).astype(padded.dtype)
+    tables(slots, blocks, offset_rows, alive, footprint[...], inverse, sums, starts)
     terms = taps.shape[0] // (4 * half)
     pairs = blocks // 2
     group = max(d for d in range(1, min(GROUP, pairs) + 1) if pairs % d == 0)
@@ -201,7 +214,20 @@
     lax.fori_loop(0, pairs // group, step, 0)
 
 
-def write_kernel(residual, out):
+def write_kernel(count, slots, offsets, tile_count, residual, out, plan):
+    member = lax.axis_index("tile")
+    lane = lax.broadcasted_iota(jnp.int32, (1, plan.shape[1]), 1)
+
+    def one(angle, carry):
+        start = group_start(offsets, angle, member, slots)
+        row = jnp.zeros((1, plan.shape[1]), jnp.int32)
+        for j in range(slots):
+            row = jnp.where(lane == j, offsets[angle, member * slots + j] - start, row)
+        plan[pl.ds(angle, 1), :] = row
+        return carry
+
+    lax.fori_loop(0, count, one, 0)
+    plan[count : count + 1, :] = (lane < tile_count[member]).astype(jnp.int32)
     blocks, _, half = residual.shape
     for block in range(blocks):
         out[:, block * half : (block + 1) * half] = residual[block]
@@ -231,19 +257,24 @@
     piece[base : base + EXTRA_ROWS, :] = extra.astype(jnp.int32).astype(piece.dtype)
 
 
-def angle_kernel(direct, count, slots, first, offsets, phase, footprint, inverse, sums, *refs):
+def angle_kernel(
+    direct, count, first, starts, phase, footprint, inverse, sums, *refs
+):
     lists = count if direct else 1
-    arrived, residual, windows, sent = refs[:lists], refs[lists], refs[lists + 1], refs[lists + 2 :]
+    arrived, residual, windows = refs[:lists], refs[lists], refs[lists + 1]
+    sent, images = refs[lists + 2 : -1], refs[-1]
     member = lax.axis_index("tile")
     table = footprint[...]
     blocks, rows, half = phase.shape
     voxels = footprint.shape[0]
 
-    def subtract(piece, group):
-        start = group_start(offsets, member, group, slots)
-        image = jnp.dot(
+    def project(piece, image):
+        image[...] = jnp.dot(
             piece[...].reshape(SPREAD * rows, voxels), table, preferred_element_type=jnp.float32
         )
+
+    def subtract(image, group):
+        start = starts[group, 0]
         for s in range(SPREAD + 1):
             part = None
             if s < SPREAD:
@@ -257,10 +288,22 @@
                 block = jnp.minimum(block, blocks - 1)
             residual[block] = residual[block] - part
 
-    each_piece(direct, count, member, arrived, subtract)
+    if direct:
+        for k in range(count):
+            project(arrived[k], images.at[k])
+        for k in range(count):
+            subtract(images.at[k], member ^ k)
+    else:
+
+        def one(k, carry):
+            project(arrived[0].at[k], images.at[0])
+            subtract(images.at[0], k)
+            return carry
+
+        lax.fori_loop(0, count, one, 0)
 
     def weigh(window, group):
-        start = group_start(offsets, member, group, slots)
+        start = starts[group, 0]
         for s in range(SPREAD + 1):
             block = jnp.minimum(start + s, blocks - 1)
             scale = inverse[pl.ds(start + s, 1), :]
@@ -289,7 +332,7 @@
         encode(windows[k], footprint[...], sums[...], piece)
 
 
-def gather_kernel(direct, ks, slots, rows, last, offsets, tile_count, *refs):
+def gather_kernel(direct, count, ks, slots, rows, last, plan, *refs):
     lists = len(ks) if direct else 1
     received = refs[:lists]
     refs = refs[lists:]
@@ -298,7 +341,6 @@
         earlier, earlier_sums, refs = refs[0], refs[1], refs[2:]
     correction, column_sums, decoded = refs
     member = lax.axis_index("tile")
-    live = tile_count[member]
     half = column_sums.shape[1]
     base = 2 * SPREAD * rows
 
@@ -307,26 +349,23 @@
         into[...] = piece[0:base, :].astype(jnp.float32) * jnp.exp2(-extra[4:5])
         return (extra[0:2] + extra[2:4] * (1.0 / LOW_SCALE)) * (1.0 / SUM_SCALE)
 
-    def block_of(into, angle, start, j):
-        at = (offsets[angle, member * slots + j] - start) * (2 * rows)
+    def block_of(into, angle, j):
+        at = plan[angle, j] * (2 * rows)
         return into[pl.ds(pl.multiple_of(at, 2 * rows), 2 * rows), :]
 
     if direct:
         total = earlier_sums[0:2] if last else jnp.zeros((2, half), jnp.float32)
         angles = [member ^ k for k in ks]
-        starts = []
         for i, piece in enumerate(received):
             total = total + unpack(piece, decoded.at[i])
-            starts.append(group_start(offsets, angles[i], member, slots))
     else:
         column_sums[...] = jnp.zeros_like(column_sums)
         correction[...] = jnp.zeros_like(correction)
 
         def step(k, carry):
             column_sums[0:2] += unpack(received[0].at[k], decoded.at[0])
-            start = group_start(offsets, k, member, slots)
             for j in range(slots):
-                correction[j] += block_of(decoded.at[0], k, start, j)
+                correction[j] += block_of(decoded.at[0], k, j)
             return carry
 
         lax.fori_loop(0, len(ks), step, 0)
@@ -340,20 +379,20 @@
         if direct:
             sum_here = earlier[j] if last else None
             for i, angle in enumerate(angles):
-                part = block_of(decoded.at[i], angle, starts[i], j)
+                part = block_of(decoded.at[i], angle, j)
                 sum_here = part if sum_here is None else sum_here + part
         else:
             sum_here = correction[j]
         if not last:
             correction[j] = sum_here
         elif direct:
-            weight = jnp.where(j < live, 1.0, 0.0)
+            weight = jnp.where(plan[count, j] > 0, 1.0, 0.0)
             for h in range(2):
                 correction[j, :, h * half : (h + 1) * half] = sum_here[
                     h * rows : (h + 1) * rows
                 ] * (inverse[h : h + 1] * weight)
         else:
-            weight = jnp.where(j < live, 1.0, 0.0)
+            weight = jnp.where(plan[count, j] > 0, 1.0, 0.0)
             correction[j] = sum_here * weight * jnp.concatenate(
                 [jnp.broadcast_to(inverse[h : h + 1], (rows, half)) for h in range(2)], axis=0
             )
@@ -399,45 +438,47 @@
             return [jax.ShapeDtypeStruct(shape, dtype)] * count
         return [jax.ShapeDtypeStruct((count,) + shape, dtype)]
 
+    taps = jnp.asarray(tap_matrix(half, TERMS))
     halo_shape = jax.ShapeDtypeStruct((HALO, columns), intensity.dtype)
     load_shapes = piece_shapes((SPREAD, rows, voxels), jnp.bfloat16)
-    near_rows, far_rows, table, offsets_here, counts_here, *loads = pl.pallas_call(
+    near_rows, far_rows, table, taps, alive, *loads = pl.pallas_call(
         lambda *refs: load_kernel(direct, count, slots, *refs),
         out_shape=[halo_shape, halo_shape]
-        + [jax.ShapeDtypeStruct(x.shape, x.dtype) for x in (table, offsets, tile_count)]
+        + [jax.ShapeDtypeStruct(x.shape, x.dtype) for x in (table, taps)]
+        + [jax.ShapeDtypeStruct((8, offsets.shape[1]), jnp.float32)]
         + load_shapes,
-        in_specs=[HBM] * 5,
+        in_specs=[HBM] * 6,
         out_specs=[VMEM] * (5 + len(load_shapes)),
         scratch_shapes=[
             pltpu.SMEM(offsets.shape, jnp.int32),
             pltpu.SMEM(tile_count.shape, jnp.int32),
             pltpu.VMEM(volume.shape, volume.dtype),
-            pltpu.SemaphoreType.DMA((8,)),
+            pltpu.SemaphoreType.DMA((8 + slots,)),
         ],
         compiler_params=params(16),
         name="loads",
-    )(*[pltpu.with_memory_space_constraint(x, pltpu.HBM) for x in (offsets, tile_count, volume, table, intensity[0])])
+    )(*[pltpu.with_memory_space_constraint(x, pltpu.HBM) for x in (offsets, tile_count, volume, table, taps, intensity[0])])
     near_rows, far_rows = swap_halos(near_rows, far_rows)
     arrived = exchange(direct, count, loads)
 
-    taps = jnp.asarray(tap_matrix(half, TERMS))
     tall = rows + 2 * HALO
-    phase_map, inverse, sums = pl.pallas_call(
+    phase_map, inverse, sums, starts = pl.pallas_call(
         lambda *refs: phase_kernel(slots, *refs),
         out_shape=[
             jax.ShapeDtypeStruct((blocks, rows, half), jnp.float32),
             jax.ShapeDtypeStruct((padded_blocks, half), jnp.float32),
             jax.ShapeDtypeStruct((EXTRA_ROWS, half), jnp.float32),
+            jax.ShapeDtypeStruct((-(-count // 8) * 8, half), jnp.int32),
         ],
-        in_specs=[SMEM] + [VMEM] * 6,
-        out_specs=[VMEM] * 3,
+        in_specs=[VMEM] * 7,
+        out_specs=[VMEM] * 4,
         scratch_shapes=[
             pltpu.VMEM((tall, columns + 2 * half), intensity.dtype),
             pltpu.VMEM((blocks, tall, half), jnp.float32),
         ],
         compiler_params=params(16),
         name="phase",
-    )(counts_here, offsets_here, intensity[0], near_rows, far_rows, table, taps)
+    )(alive, offsets, intensity[0], near_rows, far_rows, table, taps)
 
     piece_shape = (2 * SPREAD * rows + EXTRA_ROWS, half)
     one_piece = jax.ShapeDtypeStruct(piece_shape, jnp.int16)
@@ -445,18 +486,21 @@
     rest = [k for k in range(count) if k not in first]
     sent_shapes = [one_piece] * len(first) if direct else piece_shapes(piece_shape, jnp.int16)
     residual, windows, *sent = pl.pallas_call(
-        lambda *refs: angle_kernel(direct, count, slots, first, *refs),
+        lambda *refs: angle_kernel(direct, count, first, *refs),
         out_shape=[
             jax.ShapeDtypeStruct((blocks, rows, half), jnp.float32),
             jax.ShapeDtypeStruct((count, rows, (SPREAD + 1) * half), jnp.bfloat16),
         ]
         + sent_shapes,
-        in_specs=[SMEM] + [VMEM] * (4 + len(arrived)),
+        in_specs=[VMEM] * (5 + len(arrived)),
         out_specs=[VMEM] * (2 + len(sent_shapes)),
+        scratch_shapes=[
+            pltpu.VMEM((len(arrived), SPREAD * rows, voxels), jnp.float32),
+        ],
         input_output_aliases={1: 0},
         compiler_params=params(16),
         name="angle",
-    )(offsets_here, phase_map, table, inverse, sums, *arrived)
+    )(starts, phase_map, table, inverse, sums, *arrived)
     if direct:
         others = pl.pallas_call(
             lambda *refs: back_kernel(rest, *refs),
@@ -470,32 +514,35 @@
         sent = [by_partner[k] for k in range(count)]
     received = exchange(direct, count, sent)
 
-    residual = pl.pallas_call(
-        write_kernel,
-        out_shape=jax.ShapeDtypeStruct((rows, columns), jnp.float32),
-        in_specs=[VMEM],
-        out_specs=VMEM,
+    residual, plan = pl.pallas_call(
+        lambda *refs: write_kernel(count, slots, *refs),
+        out_shape=[
+            jax.ShapeDtypeStruct((rows, columns), jnp.float32),
+            jax.ShapeDtypeStruct((count + 8, half), jnp.int32),
+        ],
+        in_specs=[SMEM, SMEM, VMEM],
+        out_specs=[VMEM, VMEM],
         compiler_params=params(16),
         name="write",
-    )(residual)
+    )(offsets, tile_count, residual)
 
     def gather(ks, pieces, last, *earlier):
         flat = (slots, 2 * rows, half)
         shape = (slots, rows, voxels) if direct and last else flat
         return pl.pallas_call(
-            lambda *refs: gather_kernel(direct, ks, slots, rows, last, *refs),
+            lambda *refs: gather_kernel(direct, count, ks, slots, rows, last, *refs),
             out_shape=[
                 jax.ShapeDtypeStruct(shape, jnp.float32),
                 jax.ShapeDtypeStruct((8, half), jnp.float32),
             ],
-            in_specs=[SMEM, SMEM] + [VMEM] * (len(pieces) + len(earlier)),
+            in_specs=[VMEM] * (1 + len(pieces) + len(earlier)),
             out_specs=[VMEM, VMEM],
             scratch_shapes=[
                 pltpu.VMEM((len(pieces), 2 * SPREAD * rows, half), jnp.float32),
             ],
             compiler_params=params(16),
             name="gather_last" if last else "gather_first",
-        )(offsets_here, counts_here, *pieces, *earlier)
+        )(plan, *pieces, *earlier)
 
     if direct:
         near = list(range(count // 2))

time: 46.2 us -> 45 us (0.974)
  Pallas kernels: 9.55 us -> 8.14 us
  local copies, waits for them, and re-layouts: 1.05 us -> 0.01 us
  starting transfers between devices: 26.6 us -> 27.5 us
    unnamed x4 -> x6, local copies, waits for them, and re-layouts: 1.05 us -> 0.01 us
    pallas_call x4, Pallas kernels: 4.79 us -> 3.76 us  [the longest x1 2.04 us: local(): pl.pallas_call(lambda *refs: write_kernel(count, slots, *refs), out_shape...]
    ppermute x14, starting transfers between devices: 25.3 us -> 26.3 us  [exchange(): lax.ppermute(pieces[k], 'tile', [(i, i ^ k) for i in range(count)])]
  transfers between devices with their start and end apart: 16 -> 16, of which waited for: 6 -> 5; matrix products, arithmetic and copies ran while one was open for 0% -> 0% of each run, Pallas kernels for 10% -> 10%
where the time goes in v4:
time: 45 us; the launch traced here: 44.9 us
  starting transfers between devices  27.5 us (61%)
  waiting for transfers between devices  8.51 us (19%)
  Pallas kernels  8.14 us (18%)
  between operations  0.74 us (2%)
    ppermute x14, starting transfers between devices, exchange(): lax.ppermute(pieces[k], 'tile', [(i, i ^ k) for i in range(count)])  26.3 us
    ppermute x14, waiting for transfers between devices, exchange(): lax.ppermute(pieces[k], 'tile', [(i, i ^ k) for i in range(count)])  8.5 us
    pallas_call x1, Pallas kernels, local(): pl.pallas_call(lambda *refs: phase_kernel(slots, *refs), out_shape=[jax.S...  2.11 us
    pallas_call x1, Pallas kernels, local(): pl.pallas_call(lambda *refs: write_kernel(count, slots, *refs), out_shape...  2.04 us
    pallas_call x1, Pallas kernels, local(): pl.pallas_call(lambda *refs: load_kernel(direct, count, slots, *refs), ou...  1.68 us
    pallas_call x2, Pallas kernels, gather(): pl.pallas_call(lambda *refs: gather_kernel(direct, count, ks, slots, rows...  1.05 us
  transfers between devices with their start and end apart: 16, of which 5 were waited for; matrix products, arithmetic and copies ran while one was open for 0% of the time, Pallas kernels for 10%

profile of v4, /device:TPU:0, one launch (start us, length us, event | category | flops | bytes accessed | tf_op | source)
XLA Modules:
  0.0 44.9 jit_solution(15416305048146471560)
XLA Ops:
  0.7 1.7 %loads.1 = (bf16[8,11264]{1,0:T(8,128)(2,1)S(1)}, bf16[8,11264]{1,0:T(8,128)(2,1)S(1)}, bf16[256,256]{1,0:T(8,128)(2,1)S(1)}, bf16[1024,256]{1,0:T(8,128)(2,1)S(...) custom-call(s32[8,64]{1,0:T(8,128)} %bitcast.6, ...), custom_call_target="tpu_custom_call" | custom-call | tf_op jit(solution)/shard_map/loads/pallas_call | solution.py:444
  2.3 0.6 %collective-permute-start = (bf16[8,11264]{1,0:T(8,128)(2,1)S(1)}, bf16[8,11264]{1,0:T(8,128)(2,1)S(1)}, u32[]{:S(2)}, u32[]{:S(2)}) collective-permute-start(bf16[8,11264]{1,0:T(8,128)(2,1)S(1)} %get-tuple-element.35), channel_id=1, source_target_pairs={{0,1},{2,3},{1,0},{3,2},{4,5},{6,7},{5,4},{7,6},{8,9},{10,11},{9,8... | collective-permute-start | bytes 540680 | tf_op jit(solution)/shard_map/ppermute | solution.py:415
  2.9 0.7 %collective-permute-start.1 = (bf16[8,11264]{1,0:T(8,128)(2,1)S(1)}, bf16[8,11264]{1,0:T(8,128)(2,1)S(1)}, u32[]{:S(2)}, u32[]{:S(2)}) collective-permute-start(bf16[8,11264]{1,0:T(8,128)(2,1)S(1)} %get-tuple-element.36), channel_id=1, source_target_pairs={{1,2},{2,1},{5,6},{6,5},{9,10},{10,9},{13,14},{14,13},{17,18},{18,... | collective-permute-start | bytes 540680 | tf_op jit(solution)/shard_map/ppermute | solution.py:414
  3.6 2.6 %collective-permute-start.2 = (bf16[4,32,256]{2,1,0:T(8,128)(2,1)S(1)}, bf16[4,32,256]{2,1,0:T(8,128)(2,1)S(1)}, u32[]{:S(2)}, u32[]{:S(2)}) collective-permute-start(bf16[4,32,256]{2,1,0:T(8,128)(2,1)S(1)} %get-tuple-element.44), channel_id=1, source_target_pairs={{0,4},{4,0},{8,12},{12,8},{16,20},{20,16},{24,28},{28,24},{1,5},{5... | collective-permute-start | bytes 196616 | tf_op jit(solution)/shard_map/ppermute | solution.py:406
  6.2 1.6 %collective-permute-start.3 = (bf16[4,32,256]{2,1,0:T(8,128)(2,1)S(1)}, bf16[4,32,256]{2,1,0:T(8,128)(2,1)S(1)}, u32[]{:S(2)}, u32[]{:S(2)}) collective-permute-start(bf16[4,32,256]{2,1,0:T(8,128)(2,1)S(1)} %get-tuple-element.45), channel_id=1, source_target_pairs={{0,8},{4,12},{8,0},{12,4},{16,24},{20,28},{24,16},{28,20},{1,9},{5... | collective-permute-start | bytes 196616 | tf_op jit(solution)/shard_map/ppermute | solution.py:406
  7.7 0.0 collective-permute-start.4
  7.7 0.7 %collective-permute-done.2.refs_6_ = bf16[4,32,256]{2,1,0:T(8,128)(2,1)S(1)} collective-permute-done((bf16[4,32,256]{2,1,0:T(8,128)(2,1)S(1)}, bf16[4,32,256]{2,1,0:T(8,128)(2,1)S(1)}, u32[]{:S(2)}, u32[]{:S(2)}) %collective-permute-start.2) | collective-permute-done | bytes 65568 | tf_op jit(solution)/shard_map/ppermute | solution.py:406
  8.4 3.1 %collective-permute-start.5 = (bf16[4,32,256]{2,1,0:T(8,128)(2,1)S(1)}, bf16[4,32,256]{2,1,0:T(8,128)(2,1)S(1)}, u32[]{:S(2)}, u32[]{:S(2)}) collective-permute-start(bf16[4,32,256]{2,1,0:T(8,128)(2,1)S(1)} %get-tuple-element.47), channel_id=1, source_target_pairs={{0,16},{4,20},{8,24},{12,28},{16,0},{20,4},{24,8},{28,12},{1,17},{... | collective-permute-start | bytes 196616 | tf_op jit(solution)/shard_map/ppermute | solution.py:406
  11.5 0.0 collective-permute-done.3.refs_7_
  11.5 1.5 %collective-permute-start.6 = (bf16[4,32,256]{2,1,0:T(8,128)(2,1)S(1)}, bf16[4,32,256]{2,1,0:T(8,128)(2,1)S(1)}, u32[]{:S(2)}, u32[]{:S(2)}) collective-permute-start(bf16[4,32,256]{2,1,0:T(8,128)(2,1)S(1)} %get-tuple-element.48), channel_id=1, source_target_pairs={{0,20},{4,16},{8,28},{12,24},{16,4},{20,0},{24,12},{28,8},{1,21},{... | collective-permute-start | bytes 196616 | tf_op jit(solution)/shard_map/ppermute | solution.py:406
  13.0 0.0 collective-permute-done.refs_3_
  13.0 3.4 %collective-permute-start.7 = (bf16[4,32,256]{2,1,0:T(8,128)(2,1)S(1)}, bf16[4,32,256]{2,1,0:T(8,128)(2,1)S(1)}, u32[]{:S(2)}, u32[]{:S(2)}) collective-permute-start(bf16[4,32,256]{2,1,0:T(8,128)(2,1)S(1)} %get-tuple-element.49), channel_id=1, source_target_pairs={{0,24},{4,28},{8,16},{12,20},{16,8},{20,12},{24,0},{28,4},{1,25},{... | collective-permute-start | bytes 196616 | tf_op jit(solution)/shard_map/ppermute | solution.py:406
  16.4 0.0 collective-permute-done.1.refs_4_
  16.4 1.3 %collective-permute-start.8 = (bf16[4,32,256]{2,1,0:T(8,128)(2,1)S(1)}, bf16[4,32,256]{2,1,0:T(8,128)(2,1)S(1)}, u32[]{:S(2)}, u32[]{:S(2)}) collective-permute-start(bf16[4,32,256]{2,1,0:T(8,128)(2,1)S(1)} %get-tuple-element.50), channel_id=1, source_target_pairs={{0,28},{4,24},{8,20},{12,16},{16,12},{20,8},{24,4},{28,0},{1,29},{... | collective-permute-start | bytes 196616 | tf_op jit(solution)/shard_map/ppermute | solution.py:406
  17.7 2.1 %phase.1 = (f32[88,32,128]{2,1,0:T(8,128)S(1)}, f32[96,128]{1,0:T(8,128)S(1)}, f32[8,128]{1,0:T(8,128)S(1)}, s32[8,128]{1,0:T(8,128)S(1)}) custom-call(f32[8,64]{1,0:T(8,128)S(1)} %get-tuple-element.34.refs_0_, s32[8,64]{1,0:T(8,128)S(1)} %bitcast.7, bf16[32,11264]{1,0:T(8,128)(2,1)S(1)} %bitcast.5, bf16[8,11264]{1,0:T(8,128)(2,1)S(1)} %collective-permute-done.refs_3_, ...), custom_call_target="tpu_custom_call" | custom-call | tf_op jit(solution)/shard_map/phase/pallas_call | solution.py:465
  19.9 0.0 copy-start.2
  19.9 0.0 collective-permute-done.4.refs_8_
  19.9 1.8 %collective-permute-done.6.refs_10_ = bf16[4,32,256]{2,1,0:T(8,128)(2,1)S(1)} collective-permute-done((bf16[4,32,256]{2,1,0:T(8,128)(2,1)S(1)}, bf16[4,32,256]{2,1,0:T(8,128)(2,1)S(1)}, u32[]{:S(2)}, u32[]{:S(2)}) %collective-permute-start.6) | collective-permute-done | bytes 65568 | tf_op jit(solution)/shard_map/ppermute | solution.py:406
  21.7 1.9 %collective-permute-done.8.refs_12_ = bf16[4,32,256]{2,1,0:T(8,128)(2,1)S(1)} collective-permute-done((bf16[4,32,256]{2,1,0:T(8,128)(2,1)S(1)}, bf16[4,32,256]{2,1,0:T(8,128)(2,1)S(1)}, u32[]{:S(2)}, u32[]{:S(2)}) %collective-permute-start.8) | collective-permute-done | bytes 65568 | tf_op jit(solution)/shard_map/ppermute | solution.py:406
  23.6 0.7 %angle.1 = (f32[88,32,128]{2,1,0:T(8,128)S(1)}, bf16[8,32,640]{2,1,0:T(8,128)(2,1)S(1)}, s16[264,128]{1,0:T(8,128)(2,1)S(1)}) custom-call(s32[8,128]{1,0:T(8,128)S(1)} %get-tuple-element.39.refs_0_, f32[88,32,128]{2,1,0:T(8,128)S(1)} %get-tuple-element.40.refs_1_, ...), custom_call_target="tpu_custom_call", output_to_operand_aliasing={{0}: (1, {})} | custom-call | tf_op jit(solution)/shard_map/angle/pallas_call | solution.py:488
  24.3 0.6 %back.1 = (s16[264,128]{1,0:T(8,128)(2,1)S(1)}, s16[264,128]{1,0:T(8,128)(2,1)S(1)}, s16[264,128]{1,0:T(8,128)(2,1)S(1)}, s16[264,128]{1,0:T(8,128)(2,1)S(1)}, s...) custom-call(bf16[8,32,640]{2,1,0:T(8,128)(2,1)S(1)} %get-tuple-element.54.refs_0_, ...), custom_call_target="tpu_custom_call" | custom-call | tf_op jit(solution)/shard_map/back/pallas_call | solution.py:505
  24.9 1.1 %collective-permute-start.13 = (s16[264,128]{1,0:T(8,128)(2,1)S(1)}, s16[264,128]{1,0:T(8,128)(2,1)S(1)}, u32[]{:S(2)}, u32[]{:S(2)}) collective-permute-start(s16[264,128]{1,0:T(8,128)(2,1)S(1)} %get-tuple-element.60), channel_id=1, source_target_pairs={{0,4},{4,0},{8,12},{12,8},{16,20},{20,16},{24,28},{28,24},{1,5},{5... | collective-permute-start | bytes 202760 | tf_op jit(solution)/shard_map/ppermute | solution.py:406
  25.9 2.3 %collective-permute-start.14 = (s16[264,128]{1,0:T(8,128)(2,1)S(1)}, s16[264,128]{1,0:T(8,128)(2,1)S(1)}, u32[]{:S(2)}, u32[]{:S(2)}) collective-permute-start(s16[264,128]{1,0:T(8,128)(2,1)S(1)} %get-tuple-element.61), channel_id=1, source_target_pairs={{0,8},{4,12},{8,0},{12,4},{16,24},{20,28},{24,16},{28,20},{1,9},{5... | collective-permute-start | bytes 202760 | tf_op jit(solution)/shard_map/ppermute | solution.py:406
  28.3 4.1 %collective-permute-start.12 = (s16[264,128]{1,0:T(8,128)(2,1)S(1)}, s16[264,128]{1,0:T(8,128)(2,1)S(1)}, u32[]{:S(2)}, u32[]{:S(2)}) collective-permute-start(s16[264,128]{1,0:T(8,128)(2,1)S(1)} %get-tuple-element.58), channel_id=1, source_target_pairs={{0,28},{4,24},{8,20},{12,16},{16,12},{20,8},{24,4},{28,0},{1,29},{... | collective-permute-start | bytes 202760 | tf_op jit(solution)/shard_map/ppermute | solution.py:406
  32.3 1.2 %collective-permute-start.9 = (s16[264,128]{1,0:T(8,128)(2,1)S(1)}, s16[264,128]{1,0:T(8,128)(2,1)S(1)}, u32[]{:S(2)}, u32[]{:S(2)}) collective-permute-start(s16[264,128]{1,0:T(8,128)(2,1)S(1)} %get-tuple-element.55), channel_id=1, source_target_pairs={{0,16},{4,20},{8,24},{12,28},{16,0},{20,4},{24,8},{28,12},{1,17},{... | collective-permute-start | bytes 202760 | tf_op jit(solution)/shard_map/ppermute | solution.py:406
  33.6 1.7 %collective-permute-start.10 = (s16[264,128]{1,0:T(8,128)(2,1)S(1)}, s16[264,128]{1,0:T(8,128)(2,1)S(1)}, u32[]{:S(2)}, u32[]{:S(2)}) collective-permute-start(s16[264,128]{1,0:T(8,128)(2,1)S(1)} %get-tuple-element.56), channel_id=1, source_target_pairs={{0,20},{4,16},{8,28},{12,24},{16,4},{20,0},{24,12},{28,8},{1,21},{... | collective-permute-start | bytes 202760 | tf_op jit(solution)/shard_map/ppermute | solution.py:406
  35.3 2.4 %collective-permute-start.11 = (s16[264,128]{1,0:T(8,128)(2,1)S(1)}, s16[264,128]{1,0:T(8,128)(2,1)S(1)}, u32[]{:S(2)}, u32[]{:S(2)}) collective-permute-start(s16[264,128]{1,0:T(8,128)(2,1)S(1)} %get-tuple-element.57), channel_id=1, source_target_pairs={{0,24},{4,28},{8,16},{12,20},{16,8},{20,12},{24,0},{28,4},{1,25},{... | collective-permute-start | bytes 202760 | tf_op jit(solution)/shard_map/ppermute | solution.py:406
  37.6 2.0 %write.1 = (f32[32,11264]{1,0:T(8,128)}, s32[16,128]{1,0:T(8,128)S(1)}) custom-call(s32[8,64]{1,0:T(8,128)S(1)} %bitcast.8, s32[8]{0:T(128)S(1)} %copy-done.2, f32[88,32,128]{2,1,0:T(8,128)S(1)} %get-tuple-element.51.refs_2_), custom_call_target="tpu_custom_call" | custom-call | tf_op jit(solution)/shard_map/write/pallas_call | solution.py:517
  39.7 0.2 gather_first.1
  39.9 2.4 %collective-permute-done.9.refs_1_ = s16[264,128]{1,0:T(8,128)(2,1)S(1)} collective-permute-done((s16[264,128]{1,0:T(8,128)(2,1)S(1)}, s16[264,128]{1,0:T(8,128)(2,1)S(1)}, u32[]{:S(2)}, u32[]{:S(2)}) %collective-permute-start.9) | collective-permute-done | bytes 67616 | tf_op jit(solution)/shard_map/ppermute | solution.py:406
  42.3 1.7 %collective-permute-done.10.refs_2_ = s16[264,128]{1,0:T(8,128)(2,1)S(1)} collective-permute-done((s16[264,128]{1,0:T(8,128)(2,1)S(1)}, s16[264,128]{1,0:T(8,128)(2,1)S(1)}, u32[]{:S(2)}, u32[]{:S(2)}) %collective-permute-start.10) | collective-permute-done | bytes 67616 | tf_op jit(solution)/shard_map/ppermute | solution.py:406
  44.0 0.9 %gather_last.1 = (f32[8,32,256]{2,1,0:T(8,128)}, f32[8,128]{1,0:T(8,128)}) custom-call(s32[16,128]{1,0:T(8,128)S(1)} %get-tuple-element.53.refs_0_, s16[264,128]{1,0:T(8,128)(2,1)S(1)} %collective-permute-done.9.refs_1_, s16[264,128]{1,0:T(8,128)(2,1)S(1)} %collective-permute-done.10.refs_2_, s16[264,128]{1,0:T(8,128)(2,1)S(1)} %collective-permute-done.11.refs_3_, ...), custom_call_target="tpu_custom_call" | custom-call | tf_op jit(solution)/shard_map/gather_last/pallas_call | solution.py:532
  (13 shorter events, 0.0 us)
Async XLA Ops:
  0.6 17.1 %copy-start.1 = (s32[64,8]{0,1:T(8,128)S(1)}, s32[64,8]{0,1:T(8,128)}, u32[]{:S(2)}) copy-start(s32[64,8]{0,1:T(8,128)} %param.9) | copy-start | bytes 6148
  0.6 17.1 %copy-start = (bf16[1,32,11264]{2,1,0:T(8,128)(2,1)S(1)}, bf16[1,32,11264]{2,1,0:T(8,128)(2,1)}, u32[]{:S(2)}) copy-start(bf16[1,32,11264]{2,1,0:T(8,128)(2,1)} %param.6) | copy-start | bytes 2162692
  2.3 10.6 %collective-permute-start = (bf16[8,11264]{1,0:T(8,128)(2,1)S(1)}, bf16[8,11264]{1,0:T(8,128)(2,1)S(1)}, u32[]{:S(2)}, u32[]{:S(2)}) collective-permute-start(bf16[8,11264]{1,0:T(8,128)(2,1)S(1)} %get-tuple-element.35), channel_id=1, source_target_pairs={{0,1},{2,3},{1,0},{3,2},{4,5},{6,7},{5,4},{7,6},{8,9},{10,11},{9,8... | collective-permute-start | bytes 540680 | tf_op jit(solution)/shard_map/ppermute | solution.py:415
  2.9 13.5 %collective-permute-start.1 = (bf16[8,11264]{1,0:T(8,128)(2,1)S(1)}, bf16[8,11264]{1,0:T(8,128)(2,1)S(1)}, u32[]{:S(2)}, u32[]{:S(2)}) collective-permute-start(bf16[8,11264]{1,0:T(8,128)(2,1)S(1)} %get-tuple-element.36), channel_id=1, source_target_pairs={{1,2},{2,1},{5,6},{6,5},{9,10},{10,9},{13,14},{14,13},{17,18},{18,... | collective-permute-start | bytes 540680 | tf_op jit(solution)/shard_map/ppermute | solution.py:414
  3.6 4.8 %collective-permute-start.2 = (bf16[4,32,256]{2,1,0:T(8,128)(2,1)S(1)}, bf16[4,32,256]{2,1,0:T(8,128)(2,1)S(1)}, u32[]{:S(2)}, u32[]{:S(2)}) collective-permute-start(bf16[4,32,256]{2,1,0:T(8,128)(2,1)S(1)} %get-tuple-element.44), channel_id=1, source_target_pairs={{0,4},{4,0},{8,12},{12,8},{16,20},{20,16},{24,28},{28,24},{1,5},{5... | collective-permute-start | bytes 196616 | tf_op jit(solution)/shard_map/ppermute | solution.py:406
  6.2 5.3 %collective-permute-start.3 = (bf16[4,32,256]{2,1,0:T(8,128)(2,1)S(1)}, bf16[4,32,256]{2,1,0:T(8,128)(2,1)S(1)}, u32[]{:S(2)}, u32[]{:S(2)}) collective-permute-start(bf16[4,32,256]{2,1,0:T(8,128)(2,1)S(1)} %get-tuple-element.45), channel_id=1, source_target_pairs={{0,8},{4,12},{8,0},{12,4},{16,24},{20,28},{24,16},{28,20},{1,9},{5... | collective-permute-start | bytes 196616 | tf_op jit(solution)/shard_map/ppermute | solution.py:406
  7.7 12.1 %collective-permute-start.4 = (bf16[4,32,256]{2,1,0:T(8,128)(2,1)S(1)}, bf16[4,32,256]{2,1,0:T(8,128)(2,1)S(1)}, u32[]{:S(2)}, u32[]{:S(2)}) collective-permute-start(bf16[4,32,256]{2,1,0:T(8,128)(2,1)S(1)} %get-tuple-element.46), channel_id=1, source_target_pairs={{0,12},{4,8},{8,4},{12,0},{16,28},{20,24},{24,20},{28,16},{1,13},{... | collective-permute-start | bytes 196616 | tf_op jit(solution)/shard_map/ppermute | solution.py:406
  8.4 11.5 %collective-permute-start.5 = (bf16[4,32,256]{2,1,0:T(8,128)(2,1)S(1)}, bf16[4,32,256]{2,1,0:T(8,128)(2,1)S(1)}, u32[]{:S(2)}, u32[]{:S(2)}) collective-permute-start(bf16[4,32,256]{2,1,0:T(8,128)(2,1)S(1)} %get-tuple-element.47), channel_id=1, source_target_pairs={{0,16},{4,20},{8,24},{12,28},{16,0},{20,4},{24,8},{28,12},{1,17},{... | collective-permute-start | bytes 196616 | tf_op jit(solution)/shard_map/ppermute | solution.py:406
  11.5 10.2 %collective-permute-start.6 = (bf16[4,32,256]{2,1,0:T(8,128)(2,1)S(1)}, bf16[4,32,256]{2,1,0:T(8,128)(2,1)S(1)}, u32[]{:S(2)}, u32[]{:S(2)}) collective-permute-start(bf16[4,32,256]{2,1,0:T(8,128)(2,1)S(1)} %get-tuple-element.48), channel_id=1, source_target_pairs={{0,20},{4,16},{8,28},{12,24},{16,4},{20,0},{24,12},{28,8},{1,21},{... | collective-permute-start | bytes 196616 | tf_op jit(solution)/shard_map/ppermute | solution.py:406
  13.0 8.7 %collective-permute-start.7 = (bf16[4,32,256]{2,1,0:T(8,128)(2,1)S(1)}, bf16[4,32,256]{2,1,0:T(8,128)(2,1)S(1)}, u32[]{:S(2)}, u32[]{:S(2)}) collective-permute-start(bf16[4,32,256]{2,1,0:T(8,128)(2,1)S(1)} %get-tuple-element.49), channel_id=1, source_target_pairs={{0,24},{4,28},{8,16},{12,20},{16,8},{20,12},{24,0},{28,4},{1,25},{... | collective-permute-start | bytes 196616 | tf_op jit(solution)/shard_map/ppermute | solution.py:406
  16.4 7.2 %collective-permute-start.8 = (bf16[4,32,256]{2,1,0:T(8,128)(2,1)S(1)}, bf16[4,32,256]{2,1,0:T(8,128)(2,1)S(1)}, u32[]{:S(2)}, u32[]{:S(2)}) collective-permute-start(bf16[4,32,256]{2,1,0:T(8,128)(2,1)S(1)} %get-tuple-element.50), channel_id=1, source_target_pairs={{0,28},{4,24},{8,20},{12,16},{16,12},{20,8},{24,4},{28,0},{1,29},{... | collective-permute-start | bytes 196616 | tf_op jit(solution)/shard_map/ppermute | solution.py:406
  19.9 17.8 %copy-start.2 = (s32[8]{0:T(128)S(1)}, s32[8]{0:T(128)}, u32[]{:S(2)}) copy-start(s32[8]{0:T(128)} %refs_1_.3) | copy-start | bytes 100
  24.9 8.7 %collective-permute-start.13 = (s16[264,128]{1,0:T(8,128)(2,1)S(1)}, s16[264,128]{1,0:T(8,128)(2,1)S(1)}, u32[]{:S(2)}, u32[]{:S(2)}) collective-permute-start(s16[264,128]{1,0:T(8,128)(2,1)S(1)} %get-tuple-element.60), channel_id=1, source_target_pairs={{0,4},{4,0},{8,12},{12,8},{16,20},{20,16},{24,28},{28,24},{1,5},{5... | collective-permute-start | bytes 202760 | tf_op jit(solution)/shard_map/ppermute | solution.py:406
  25.9 9.3 %collective-permute-start.14 = (s16[264,128]{1,0:T(8,128)(2,1)S(1)}, s16[264,128]{1,0:T(8,128)(2,1)S(1)}, u32[]{:S(2)}, u32[]{:S(2)}) collective-permute-start(s16[264,128]{1,0:T(8,128)(2,1)S(1)} %get-tuple-element.61), channel_id=1, source_target_pairs={{0,8},{4,12},{8,0},{12,4},{16,24},{20,28},{24,16},{28,20},{1,9},{5... | collective-permute-start | bytes 202760 | tf_op jit(solution)/shard_map/ppermute | solution.py:406
  28.3 11.6 %collective-permute-start.12 = (s16[264,128]{1,0:T(8,128)(2,1)S(1)}, s16[264,128]{1,0:T(8,128)(2,1)S(1)}, u32[]{:S(2)}, u32[]{:S(2)}) collective-permute-start(s16[264,128]{1,0:T(8,128)(2,1)S(1)} %get-tuple-element.58), channel_id=1, source_target_pairs={{0,28},{4,24},{8,20},{12,16},{16,12},{20,8},{24,4},{28,0},{1,29},{... | collective-permute-start | bytes 202760 | tf_op jit(solution)/shard_map/ppermute | solution.py:406
  32.3 7.3 %collective-permute-start.15 = (s16[264,128]{1,0:T(8,128)(2,1)S(1)}, s16[264,128]{1,0:T(8,128)(2,1)S(1)}, u32[]{:S(2)}, u32[]{:S(2)}) collective-permute-start(s16[264,128]{1,0:T(8,128)(2,1)S(1)} %get-tuple-element.62), channel_id=1, source_target_pairs={{0,12},{4,8},{8,4},{12,0},{16,28},{20,24},{24,20},{28,16},{1,13},{... | collective-permute-start | bytes 202760 | tf_op jit(solution)/shard_map/ppermute | solution.py:406
  32.3 10.0 %collective-permute-start.9 = (s16[264,128]{1,0:T(8,128)(2,1)S(1)}, s16[264,128]{1,0:T(8,128)(2,1)S(1)}, u32[]{:S(2)}, u32[]{:S(2)}) collective-permute-start(s16[264,128]{1,0:T(8,128)(2,1)S(1)} %get-tuple-element.55), channel_id=1, source_target_pairs={{0,16},{4,20},{8,24},{12,28},{16,0},{20,4},{24,8},{28,12},{1,17},{... | collective-permute-start | bytes 202760 | tf_op jit(solution)/shard_map/ppermute | solution.py:406
  33.6 10.4 %collective-permute-start.10 = (s16[264,128]{1,0:T(8,128)(2,1)S(1)}, s16[264,128]{1,0:T(8,128)(2,1)S(1)}, u32[]{:S(2)}, u32[]{:S(2)}) collective-permute-start(s16[264,128]{1,0:T(8,128)(2,1)S(1)} %get-tuple-element.56), channel_id=1, source_target_pairs={{0,20},{4,16},{8,28},{12,24},{16,4},{20,0},{24,12},{28,8},{1,21},{... | collective-permute-start | bytes 202760 | tf_op jit(solution)/shard_map/ppermute | solution.py:406
  35.3 8.7 %collective-permute-start.11 = (s16[264,128]{1,0:T(8,128)(2,1)S(1)}, s16[264,128]{1,0:T(8,128)(2,1)S(1)}, u32[]{:S(2)}, u32[]{:S(2)}) collective-permute-start(s16[264,128]{1,0:T(8,128)(2,1)S(1)} %get-tuple-element.57), channel_id=1, source_target_pairs={{0,24},{4,28},{8,16},{12,20},{16,8},{20,12},{24,0},{28,4},{1,25},{... | collective-permute-start | bytes 202760 | tf_op jit(solution)/shard_map/ppermute | solution.py:406

commit v5 on v4

--- a/solution.py
+++ b/solution.py
@@ -13,6 +13,7 @@
 GROUP = 22
 TERMS = 2
 FIRST = 1
+HOME_ORDER = (7, 5, 6, 4, 3, 2, 1)
 DIRECT_LIMIT = 16
 EXTRA_ROWS = 8
 SUM_SCALE = 2048.0
@@ -407,6 +408,11 @@
     return arrived
 
 
+def partner_order(count, wanted):
+    known = [k for k in wanted if 0 < k < count]
+    return known + [k for k in range(count - 1, 0, -1) if k not in known]
+
+
 def swap_halos(near_rows, far_rows):
     count = lax.axis_size("row")
     pairs = [(i, i + 1) for i in range(0, count - 1, 2)]
@@ -482,7 +488,7 @@
 
     piece_shape = (2 * SPREAD * rows + EXTRA_ROWS, half)
     one_piece = jax.ShapeDtypeStruct(piece_shape, jnp.int16)
-    first = list(range(count - 1, 0, -1))[:FIRST] if direct else []
+    first = partner_order(count, HOME_ORDER)[:FIRST] if direct else []
     rest = [k for k in range(count) if k not in first]
     sent_shapes = [one_piece] * len(first) if direct else piece_shapes(piece_shape, jnp.int16)
     residual, windows, *sent = pl.pallas_call(

time: 45 us -> 45 us (level)
  no operation moved by 1% of the time
where the time goes in v5:
time: 45 us; the launch traced here: 44.9 us
  starting transfers between devices  27.5 us (61%)
  waiting for transfers between devices  8.51 us (19%)
  Pallas kernels  8.14 us (18%)
  between operations  0.74 us (2%)
    ppermute x14, starting transfers between devices, exchange(): lax.ppermute(pieces[k], 'tile', [(i, i ^ k) for i in range(count)])  26.3 us
    ppermute x14, waiting for transfers between devices, exchange(): lax.ppermute(pieces[k], 'tile', [(i, i ^ k) for i in range(count)])  8.5 us
    pallas_call x1, Pallas kernels, local(): pl.pallas_call(lambda *refs: phase_kernel(slots, *refs), out_shape=[jax.S...  2.11 us
    pallas_call x1, Pallas kernels, local(): pl.pallas_call(lambda *refs: write_kernel(count, slots, *refs), out_shape...  2.04 us
    pallas_call x1, Pallas kernels, local(): pl.pallas_call(lambda *refs: load_kernel(direct, count, slots, *refs), ou...  1.68 us
    pallas_call x2, Pallas kernels, gather(): pl.pallas_call(lambda *refs: gather_kernel(direct, count, ks, slots, rows...  1.05 us
  transfers between devices with their start and end apart: 16, of which 5 were waited for; matrix products, arithmetic and copies ran while one was open for 0% of the time, Pallas kernels for 10%

profile of v5, /device:TPU:0, one launch (start us, length us, event | category | flops | bytes accessed | tf_op | source)
XLA Modules:
  0.0 44.9 jit_solution(15416305048146471560)
XLA Ops:
  0.7 1.7 %loads.1 = (bf16[8,11264]{1,0:T(8,128)(2,1)S(1)}, bf16[8,11264]{1,0:T(8,128)(2,1)S(1)}, bf16[256,256]{1,0:T(8,128)(2,1)S(1)}, bf16[1024,256]{1,0:T(8,128)(2,1)S(...) custom-call(s32[8,64]{1,0:T(8,128)} %bitcast.6, ...), custom_call_target="tpu_custom_call" | custom-call | tf_op jit(solution)/shard_map/loads/pallas_call | solution.py:450
  2.3 0.6 %collective-permute-start = (bf16[8,11264]{1,0:T(8,128)(2,1)S(1)}, bf16[8,11264]{1,0:T(8,128)(2,1)S(1)}, u32[]{:S(2)}, u32[]{:S(2)}) collective-permute-start(bf16[8,11264]{1,0:T(8,128)(2,1)S(1)} %get-tuple-element.35), channel_id=1, source_target_pairs={{0,1},{2,3},{1,0},{3,2},{4,5},{6,7},{5,4},{7,6},{8,9},{10,11},{9,8... | collective-permute-start | bytes 540680 | tf_op jit(solution)/shard_map/ppermute | solution.py:421
  2.9 0.7 %collective-permute-start.1 = (bf16[8,11264]{1,0:T(8,128)(2,1)S(1)}, bf16[8,11264]{1,0:T(8,128)(2,1)S(1)}, u32[]{:S(2)}, u32[]{:S(2)}) collective-permute-start(bf16[8,11264]{1,0:T(8,128)(2,1)S(1)} %get-tuple-element.36), channel_id=1, source_target_pairs={{1,2},{2,1},{5,6},{6,5},{9,10},{10,9},{13,14},{14,13},{17,18},{18,... | collective-permute-start | bytes 540680 | tf_op jit(solution)/shard_map/ppermute | solution.py:420
  3.6 2.6 %collective-permute-start.2 = (bf16[4,32,256]{2,1,0:T(8,128)(2,1)S(1)}, bf16[4,32,256]{2,1,0:T(8,128)(2,1)S(1)}, u32[]{:S(2)}, u32[]{:S(2)}) collective-permute-start(bf16[4,32,256]{2,1,0:T(8,128)(2,1)S(1)} %get-tuple-element.44), channel_id=1, source_target_pairs={{0,4},{4,0},{8,12},{12,8},{16,20},{20,16},{24,28},{28,24},{1,5},{5... | collective-permute-start | bytes 196616 | tf_op jit(solution)/shard_map/ppermute | solution.py:407
  6.2 1.6 %collective-permute-start.3 = (bf16[4,32,256]{2,1,0:T(8,128)(2,1)S(1)}, bf16[4,32,256]{2,1,0:T(8,128)(2,1)S(1)}, u32[]{:S(2)}, u32[]{:S(2)}) collective-permute-start(bf16[4,32,256]{2,1,0:T(8,128)(2,1)S(1)} %get-tuple-element.45), channel_id=1, source_target_pairs={{0,8},{4,12},{8,0},{12,4},{16,24},{20,28},{24,16},{28,20},{1,9},{5... | collective-permute-start | bytes 196616 | tf_op jit(solution)/shard_map/ppermute | solution.py:407
  7.7 0.0 collective-permute-start.4
  7.7 0.7 %collective-permute-done.2.refs_6_ = bf16[4,32,256]{2,1,0:T(8,128)(2,1)S(1)} collective-permute-done((bf16[4,32,256]{2,1,0:T(8,128)(2,1)S(1)}, bf16[4,32,256]{2,1,0:T(8,128)(2,1)S(1)}, u32[]{:S(2)}, u32[]{:S(2)}) %collective-permute-start.2) | collective-permute-done | bytes 65568 | tf_op jit(solution)/shard_map/ppermute | solution.py:407
  8.4 3.1 %collective-permute-start.5 = (bf16[4,32,256]{2,1,0:T(8,128)(2,1)S(1)}, bf16[4,32,256]{2,1,0:T(8,128)(2,1)S(1)}, u32[]{:S(2)}, u32[]{:S(2)}) collective-permute-start(bf16[4,32,256]{2,1,0:T(8,128)(2,1)S(1)} %get-tuple-element.47), channel_id=1, source_target_pairs={{0,16},{4,20},{8,24},{12,28},{16,0},{20,4},{24,8},{28,12},{1,17},{... | collective-permute-start | bytes 196616 | tf_op jit(solution)/shard_map/ppermute | solution.py:407
  11.5 0.0 collective-permute-done.3.refs_7_
  11.5 1.5 %collective-permute-start.6 = (bf16[4,32,256]{2,1,0:T(8,128)(2,1)S(1)}, bf16[4,32,256]{2,1,0:T(8,128)(2,1)S(1)}, u32[]{:S(2)}, u32[]{:S(2)}) collective-permute-start(bf16[4,32,256]{2,1,0:T(8,128)(2,1)S(1)} %get-tuple-element.48), channel_id=1, source_target_pairs={{0,20},{4,16},{8,28},{12,24},{16,4},{20,0},{24,12},{28,8},{1,21},{... | collective-permute-start | bytes 196616 | tf_op jit(solution)/shard_map/ppermute | solution.py:407
  13.0 0.0 collective-permute-done.refs_3_
  13.0 3.4 %collective-permute-start.7 = (bf16[4,32,256]{2,1,0:T(8,128)(2,1)S(1)}, bf16[4,32,256]{2,1,0:T(8,128)(2,1)S(1)}, u32[]{:S(2)}, u32[]{:S(2)}) collective-permute-start(bf16[4,32,256]{2,1,0:T(8,128)(2,1)S(1)} %get-tuple-element.49), channel_id=1, source_target_pairs={{0,24},{4,28},{8,16},{12,20},{16,8},{20,12},{24,0},{28,4},{1,25},{... | collective-permute-start | bytes 196616 | tf_op jit(solution)/shard_map/ppermute | solution.py:407
  16.4 0.0 collective-permute-done.1.refs_4_
  16.4 1.3 %collective-permute-start.8 = (bf16[4,32,256]{2,1,0:T(8,128)(2,1)S(1)}, bf16[4,32,256]{2,1,0:T(8,128)(2,1)S(1)}, u32[]{:S(2)}, u32[]{:S(2)}) collective-permute-start(bf16[4,32,256]{2,1,0:T(8,128)(2,1)S(1)} %get-tuple-element.50), channel_id=1, source_target_pairs={{0,28},{4,24},{8,20},{12,16},{16,12},{20,8},{24,4},{28,0},{1,29},{... | collective-permute-start | bytes 196616 | tf_op jit(solution)/shard_map/ppermute | solution.py:407
  17.7 2.1 %phase.1 = (f32[88,32,128]{2,1,0:T(8,128)S(1)}, f32[96,128]{1,0:T(8,128)S(1)}, f32[8,128]{1,0:T(8,128)S(1)}, s32[8,128]{1,0:T(8,128)S(1)}) custom-call(f32[8,64]{1,0:T(8,128)S(1)} %get-tuple-element.34.refs_0_, s32[8,64]{1,0:T(8,128)S(1)} %bitcast.7, bf16[32,11264]{1,0:T(8,128)(2,1)S(1)} %bitcast.5, bf16[8,11264]{1,0:T(8,128)(2,1)S(1)} %collective-permute-done.refs_3_, ...), custom_call_target="tpu_custom_call" | custom-call | tf_op jit(solution)/shard_map/phase/pallas_call | solution.py:471
  19.9 0.0 copy-start.2
  19.9 0.0 collective-permute-done.4.refs_8_
  19.9 1.8 %collective-permute-done.6.refs_10_ = bf16[4,32,256]{2,1,0:T(8,128)(2,1)S(1)} collective-permute-done((bf16[4,32,256]{2,1,0:T(8,128)(2,1)S(1)}, bf16[4,32,256]{2,1,0:T(8,128)(2,1)S(1)}, u32[]{:S(2)}, u32[]{:S(2)}) %collective-permute-start.6) | collective-permute-done | bytes 65568 | tf_op jit(solution)/shard_map/ppermute | solution.py:407
  21.7 1.9 %collective-permute-done.8.refs_12_ = bf16[4,32,256]{2,1,0:T(8,128)(2,1)S(1)} collective-permute-done((bf16[4,32,256]{2,1,0:T(8,128)(2,1)S(1)}, bf16[4,32,256]{2,1,0:T(8,128)(2,1)S(1)}, u32[]{:S(2)}, u32[]{:S(2)}) %collective-permute-start.8) | collective-permute-done | bytes 65568 | tf_op jit(solution)/shard_map/ppermute | solution.py:407
  23.6 0.7 %angle.1 = (f32[88,32,128]{2,1,0:T(8,128)S(1)}, bf16[8,32,640]{2,1,0:T(8,128)(2,1)S(1)}, s16[264,128]{1,0:T(8,128)(2,1)S(1)}) custom-call(s32[8,128]{1,0:T(8,128)S(1)} %get-tuple-element.39.refs_0_, f32[88,32,128]{2,1,0:T(8,128)S(1)} %get-tuple-element.40.refs_1_, ...), custom_call_target="tpu_custom_call", output_to_operand_aliasing={{0}: (1, {})} | custom-call | tf_op jit(solution)/shard_map/angle/pallas_call | solution.py:494
  24.3 0.6 %back.1 = (s16[264,128]{1,0:T(8,128)(2,1)S(1)}, s16[264,128]{1,0:T(8,128)(2,1)S(1)}, s16[264,128]{1,0:T(8,128)(2,1)S(1)}, s16[264,128]{1,0:T(8,128)(2,1)S(1)}, s...) custom-call(bf16[8,32,640]{2,1,0:T(8,128)(2,1)S(1)} %get-tuple-element.54.refs_0_, ...), custom_call_target="tpu_custom_call" | custom-call | tf_op jit(solution)/shard_map/back/pallas_call | solution.py:511
  24.9 1.1 %collective-permute-start.13 = (s16[264,128]{1,0:T(8,128)(2,1)S(1)}, s16[264,128]{1,0:T(8,128)(2,1)S(1)}, u32[]{:S(2)}, u32[]{:S(2)}) collective-permute-start(s16[264,128]{1,0:T(8,128)(2,1)S(1)} %get-tuple-element.60), channel_id=1, source_target_pairs={{0,4},{4,0},{8,12},{12,8},{16,20},{20,16},{24,28},{28,24},{1,5},{5... | collective-permute-start | bytes 202760 | tf_op jit(solution)/shard_map/ppermute | solution.py:407
  25.9 2.3 %collective-permute-start.14 = (s16[264,128]{1,0:T(8,128)(2,1)S(1)}, s16[264,128]{1,0:T(8,128)(2,1)S(1)}, u32[]{:S(2)}, u32[]{:S(2)}) collective-permute-start(s16[264,128]{1,0:T(8,128)(2,1)S(1)} %get-tuple-element.61), channel_id=1, source_target_pairs={{0,8},{4,12},{8,0},{12,4},{16,24},{20,28},{24,16},{28,20},{1,9},{5... | collective-permute-start | bytes 202760 | tf_op jit(solution)/shard_map/ppermute | solution.py:407
  28.3 4.1 %collective-permute-start.12 = (s16[264,128]{1,0:T(8,128)(2,1)S(1)}, s16[264,128]{1,0:T(8,128)(2,1)S(1)}, u32[]{:S(2)}, u32[]{:S(2)}) collective-permute-start(s16[264,128]{1,0:T(8,128)(2,1)S(1)} %get-tuple-element.58), channel_id=1, source_target_pairs={{0,28},{4,24},{8,20},{12,16},{16,12},{20,8},{24,4},{28,0},{1,29},{... | collective-permute-start | bytes 202760 | tf_op jit(solution)/shard_map/ppermute | solution.py:407
  32.3 1.2 %collective-permute-start.9 = (s16[264,128]{1,0:T(8,128)(2,1)S(1)}, s16[264,128]{1,0:T(8,128)(2,1)S(1)}, u32[]{:S(2)}, u32[]{:S(2)}) collective-permute-start(s16[264,128]{1,0:T(8,128)(2,1)S(1)} %get-tuple-element.55), channel_id=1, source_target_pairs={{0,16},{4,20},{8,24},{12,28},{16,0},{20,4},{24,8},{28,12},{1,17},{... | collective-permute-start | bytes 202760 | tf_op jit(solution)/shard_map/ppermute | solution.py:407
  33.6 1.7 %collective-permute-start.10 = (s16[264,128]{1,0:T(8,128)(2,1)S(1)}, s16[264,128]{1,0:T(8,128)(2,1)S(1)}, u32[]{:S(2)}, u32[]{:S(2)}) collective-permute-start(s16[264,128]{1,0:T(8,128)(2,1)S(1)} %get-tuple-element.56), channel_id=1, source_target_pairs={{0,20},{4,16},{8,28},{12,24},{16,4},{20,0},{24,12},{28,8},{1,21},{... | collective-permute-start | bytes 202760 | tf_op jit(solution)/shard_map/ppermute | solution.py:407
  35.3 2.4 %collective-permute-start.11 = (s16[264,128]{1,0:T(8,128)(2,1)S(1)}, s16[264,128]{1,0:T(8,128)(2,1)S(1)}, u32[]{:S(2)}, u32[]{:S(2)}) collective-permute-start(s16[264,128]{1,0:T(8,128)(2,1)S(1)} %get-tuple-element.57), channel_id=1, source_target_pairs={{0,24},{4,28},{8,16},{12,20},{16,8},{20,12},{24,0},{28,4},{1,25},{... | collective-permute-start | bytes 202760 | tf_op jit(solution)/shard_map/ppermute | solution.py:407
  37.6 2.0 %write.1 = (f32[32,11264]{1,0:T(8,128)}, s32[16,128]{1,0:T(8,128)S(1)}) custom-call(s32[8,64]{1,0:T(8,128)S(1)} %bitcast.8, s32[8]{0:T(128)S(1)} %copy-done.2, f32[88,32,128]{2,1,0:T(8,128)S(1)} %get-tuple-element.51.refs_2_), custom_call_target="tpu_custom_call" | custom-call | tf_op jit(solution)/shard_map/write/pallas_call | solution.py:523
  39.7 0.2 gather_first.1
  39.9 2.4 %collective-permute-done.9.refs_1_ = s16[264,128]{1,0:T(8,128)(2,1)S(1)} collective-permute-done((s16[264,128]{1,0:T(8,128)(2,1)S(1)}, s16[264,128]{1,0:T(8,128)(2,1)S(1)}, u32[]{:S(2)}, u32[]{:S(2)}) %collective-permute-start.9) | collective-permute-done | bytes 67616 | tf_op jit(solution)/shard_map/ppermute | solution.py:407
  42.3 1.7 %collective-permute-done.10.refs_2_ = s16[264,128]{1,0:T(8,128)(2,1)S(1)} collective-permute-done((s16[264,128]{1,0:T(8,128)(2,1)S(1)}, s16[264,128]{1,0:T(8,128)(2,1)S(1)}, u32[]{:S(2)}, u32[]{:S(2)}) %collective-permute-start.10) | collective-permute-done | bytes 67616 | tf_op jit(solution)/shard_map/ppermute | solution.py:407
  44.0 0.9 %gather_last.1 = (f32[8,32,256]{2,1,0:T(8,128)}, f32[8,128]{1,0:T(8,128)}) custom-call(s32[16,128]{1,0:T(8,128)S(1)} %get-tuple-element.53.refs_0_, s16[264,128]{1,0:T(8,128)(2,1)S(1)} %collective-permute-done.9.refs_1_, s16[264,128]{1,0:T(8,128)(2,1)S(1)} %collective-permute-done.10.refs_2_, s16[264,128]{1,0:T(8,128)(2,1)S(1)} %collective-permute-done.11.refs_3_, ...), custom_call_target="tpu_custom_call" | custom-call | tf_op jit(solution)/shard_map/gather_last/pallas_call | solution.py:538
  (13 shorter events, 0.0 us)
Async XLA Ops:
  0.6 17.1 %copy-start.1 = (s32[64,8]{0,1:T(8,128)S(1)}, s32[64,8]{0,1:T(8,128)}, u32[]{:S(2)}) copy-start(s32[64,8]{0,1:T(8,128)} %param.9) | copy-start | bytes 6148
  0.6 17.1 %copy-start = (bf16[1,32,11264]{2,1,0:T(8,128)(2,1)S(1)}, bf16[1,32,11264]{2,1,0:T(8,128)(2,1)}, u32[]{:S(2)}) copy-start(bf16[1,32,11264]{2,1,0:T(8,128)(2,1)} %param.6) | copy-start | bytes 2162692
  2.3 10.6 %collective-permute-start = (bf16[8,11264]{1,0:T(8,128)(2,1)S(1)}, bf16[8,11264]{1,0:T(8,128)(2,1)S(1)}, u32[]{:S(2)}, u32[]{:S(2)}) collective-permute-start(bf16[8,11264]{1,0:T(8,128)(2,1)S(1)} %get-tuple-element.35), channel_id=1, source_target_pairs={{0,1},{2,3},{1,0},{3,2},{4,5},{6,7},{5,4},{7,6},{8,9},{10,11},{9,8... | collective-permute-start | bytes 540680 | tf_op jit(solution)/shard_map/ppermute | solution.py:421
  2.9 13.5 %collective-permute-start.1 = (bf16[8,11264]{1,0:T(8,128)(2,1)S(1)}, bf16[8,11264]{1,0:T(8,128)(2,1)S(1)}, u32[]{:S(2)}, u32[]{:S(2)}) collective-permute-start(bf16[8,11264]{1,0:T(8,128)(2,1)S(1)} %get-tuple-element.36), channel_id=1, source_target_pairs={{1,2},{2,1},{5,6},{6,5},{9,10},{10,9},{13,14},{14,13},{17,18},{18,... | collective-permute-start | bytes 540680 | tf_op jit(solution)/shard_map/ppermute | solution.py:420
  3.6 4.8 %collective-permute-start.2 = (bf16[4,32,256]{2,1,0:T(8,128)(2,1)S(1)}, bf16[4,32,256]{2,1,0:T(8,128)(2,1)S(1)}, u32[]{:S(2)}, u32[]{:S(2)}) collective-permute-start(bf16[4,32,256]{2,1,0:T(8,128)(2,1)S(1)} %get-tuple-element.44), channel_id=1, source_target_pairs={{0,4},{4,0},{8,12},{12,8},{16,20},{20,16},{24,28},{28,24},{1,5},{5... | collective-permute-start | bytes 196616 | tf_op jit(solution)/shard_map/ppermute | solution.py:407
  6.2 5.3 %collective-permute-start.3 = (bf16[4,32,256]{2,1,0:T(8,128)(2,1)S(1)}, bf16[4,32,256]{2,1,0:T(8,128)(2,1)S(1)}, u32[]{:S(2)}, u32[]{:S(2)}) collective-permute-start(bf16[4,32,256]{2,1,0:T(8,128)(2,1)S(1)} %get-tuple-element.45), channel_id=1, source_target_pairs={{0,8},{4,12},{8,0},{12,4},{16,24},{20,28},{24,16},{28,20},{1,9},{5... | collective-permute-start | bytes 196616 | tf_op jit(solution)/shard_map/ppermute | solution.py:407
  7.7 12.1 %collective-permute-start.4 = (bf16[4,32,256]{2,1,0:T(8,128)(2,1)S(1)}, bf16[4,32,256]{2,1,0:T(8,128)(2,1)S(1)}, u32[]{:S(2)}, u32[]{:S(2)}) collective-permute-start(bf16[4,32,256]{2,1,0:T(8,128)(2,1)S(1)} %get-tuple-element.46), channel_id=1, source_target_pairs={{0,12},{4,8},{8,4},{12,0},{16,28},{20,24},{24,20},{28,16},{1,13},{... | collective-permute-start | bytes 196616 | tf_op jit(solution)/shard_map/ppermute | solution.py:407
  8.4 11.5 %collective-permute-start.5 = (bf16[4,32,256]{2,1,0:T(8,128)(2,1)S(1)}, bf16[4,32,256]{2,1,0:T(8,128)(2,1)S(1)}, u32[]{:S(2)}, u32[]{:S(2)}) collective-permute-start(bf16[4,32,256]{2,1,0:T(8,128)(2,1)S(1)} %get-tuple-element.47), channel_id=1, source_target_pairs={{0,16},{4,20},{8,24},{12,28},{16,0},{20,4},{24,8},{28,12},{1,17},{... | collective-permute-start | bytes 196616 | tf_op jit(solution)/shard_map/ppermute | solution.py:407
  11.5 10.2 %collective-permute-start.6 = (bf16[4,32,256]{2,1,0:T(8,128)(2,1)S(1)}, bf16[4,32,256]{2,1,0:T(8,128)(2,1)S(1)}, u32[]{:S(2)}, u32[]{:S(2)}) collective-permute-start(bf16[4,32,256]{2,1,0:T(8,128)(2,1)S(1)} %get-tuple-element.48), channel_id=1, source_target_pairs={{0,20},{4,16},{8,28},{12,24},{16,4},{20,0},{24,12},{28,8},{1,21},{... | collective-permute-start | bytes 196616 | tf_op jit(solution)/shard_map/ppermute | solution.py:407
  13.0 8.7 %collective-permute-start.7 = (bf16[4,32,256]{2,1,0:T(8,128)(2,1)S(1)}, bf16[4,32,256]{2,1,0:T(8,128)(2,1)S(1)}, u32[]{:S(2)}, u32[]{:S(2)}) collective-permute-start(bf16[4,32,256]{2,1,0:T(8,128)(2,1)S(1)} %get-tuple-element.49), channel_id=1, source_target_pairs={{0,24},{4,28},{8,16},{12,20},{16,8},{20,12},{24,0},{28,4},{1,25},{... | collective-permute-start | bytes 196616 | tf_op jit(solution)/shard_map/ppermute | solution.py:407
  16.4 7.2 %collective-permute-start.8 = (bf16[4,32,256]{2,1,0:T(8,128)(2,1)S(1)}, bf16[4,32,256]{2,1,0:T(8,128)(2,1)S(1)}, u32[]{:S(2)}, u32[]{:S(2)}) collective-permute-start(bf16[4,32,256]{2,1,0:T(8,128)(2,1)S(1)} %get-tuple-element.50), channel_id=1, source_target_pairs={{0,28},{4,24},{8,20},{12,16},{16,12},{20,8},{24,4},{28,0},{1,29},{... | collective-permute-start | bytes 196616 | tf_op jit(solution)/shard_map/ppermute | solution.py:407
  19.9 17.8 %copy-start.2 = (s32[8]{0:T(128)S(1)}, s32[8]{0:T(128)}, u32[]{:S(2)}) copy-start(s32[8]{0:T(128)} %refs_1_.3) | copy-start | bytes 100
  24.9 8.7 %collective-permute-start.13 = (s16[264,128]{1,0:T(8,128)(2,1)S(1)}, s16[264,128]{1,0:T(8,128)(2,1)S(1)}, u32[]{:S(2)}, u32[]{:S(2)}) collective-permute-start(s16[264,128]{1,0:T(8,128)(2,1)S(1)} %get-tuple-element.60), channel_id=1, source_target_pairs={{0,4},{4,0},{8,12},{12,8},{16,20},{20,16},{24,28},{28,24},{1,5},{5... | collective-permute-start | bytes 202760 | tf_op jit(solution)/shard_map/ppermute | solution.py:407
  25.9 9.3 %collective-permute-start.14 = (s16[264,128]{1,0:T(8,128)(2,1)S(1)}, s16[264,128]{1,0:T(8,128)(2,1)S(1)}, u32[]{:S(2)}, u32[]{:S(2)}) collective-permute-start(s16[264,128]{1,0:T(8,128)(2,1)S(1)} %get-tuple-element.61), channel_id=1, source_target_pairs={{0,8},{4,12},{8,0},{12,4},{16,24},{20,28},{24,16},{28,20},{1,9},{5... | collective-permute-start | bytes 202760 | tf_op jit(solution)/shard_map/ppermute | solution.py:407
  28.3 11.6 %collective-permute-start.12 = (s16[264,128]{1,0:T(8,128)(2,1)S(1)}, s16[264,128]{1,0:T(8,128)(2,1)S(1)}, u32[]{:S(2)}, u32[]{:S(2)}) collective-permute-start(s16[264,128]{1,0:T(8,128)(2,1)S(1)} %get-tuple-element.58), channel_id=1, source_target_pairs={{0,28},{4,24},{8,20},{12,16},{16,12},{20,8},{24,4},{28,0},{1,29},{... | collective-permute-start | bytes 202760 | tf_op jit(solution)/shard_map/ppermute | solution.py:407
  32.3 7.3 %collective-permute-start.15 = (s16[264,128]{1,0:T(8,128)(2,1)S(1)}, s16[264,128]{1,0:T(8,128)(2,1)S(1)}, u32[]{:S(2)}, u32[]{:S(2)}) collective-permute-start(s16[264,128]{1,0:T(8,128)(2,1)S(1)} %get-tuple-element.62), channel_id=1, source_target_pairs={{0,12},{4,8},{8,4},{12,0},{16,28},{20,24},{24,20},{28,16},{1,13},{... | collective-permute-start | bytes 202760 | tf_op jit(solution)/shard_map/ppermute | solution.py:407
  32.3 10.0 %collective-permute-start.9 = (s16[264,128]{1,0:T(8,128)(2,1)S(1)}, s16[264,128]{1,0:T(8,128)(2,1)S(1)}, u32[]{:S(2)}, u32[]{:S(2)}) collective-permute-start(s16[264,128]{1,0:T(8,128)(2,1)S(1)} %get-tuple-element.55), channel_id=1, source_target_pairs={{0,16},{4,20},{8,24},{12,28},{16,0},{20,4},{24,8},{28,12},{1,17},{... | collective-permute-start | bytes 202760 | tf_op jit(solution)/shard_map/ppermute | solution.py:407
  33.6 10.4 %collective-permute-start.10 = (s16[264,128]{1,0:T(8,128)(2,1)S(1)}, s16[264,128]{1,0:T(8,128)(2,1)S(1)}, u32[]{:S(2)}, u32[]{:S(2)}) collective-permute-start(s16[264,128]{1,0:T(8,128)(2,1)S(1)} %get-tuple-element.56), channel_id=1, source_target_pairs={{0,20},{4,16},{8,28},{12,24},{16,4},{20,0},{24,12},{28,8},{1,21},{... | collective-permute-start | bytes 202760 | tf_op jit(solution)/shard_map/ppermute | solution.py:407
  35.3 8.7 %collective-permute-start.11 = (s16[264,128]{1,0:T(8,128)(2,1)S(1)}, s16[264,128]{1,0:T(8,128)(2,1)S(1)}, u32[]{:S(2)}, u32[]{:S(2)}) collective-permute-start(s16[264,128]{1,0:T(8,128)(2,1)S(1)} %get-tuple-element.57), channel_id=1, source_target_pairs={{0,24},{4,28},{8,16},{12,20},{16,8},{20,12},{24,0},{28,4},{1,25},{... | collective-permute-start | bytes 202760 | tf_op jit(solution)/shard_map/ppermute | solution.py:407

commit v6 on v5

--- a/solution.py
+++ b/solution.py
@@ -13,7 +13,9 @@
 GROUP = 22
 TERMS = 2
 FIRST = 1
-HOME_ORDER = (7, 5, 6, 4, 3, 2, 1)
+LATE = 2
+OUT_ORDER = (7, 5, 6, 4, 3, 2, 1)
+HOME_ORDER = (6, 5, 7, 4, 3, 1, 2)
 DIRECT_LIMIT = 16
 EXTRA_ROWS = 8
 SUM_SCALE = 2048.0
@@ -59,10 +61,10 @@
 
 
 def load_kernel(
-    direct, count, slots, offsets_in, count_in, volume_in, table_in, taps_in, intensity, *refs
+    direct, count, slots, offsets_in, count_in, volume_in, table_in, intensity, *refs
 ):
     lists = count if direct else 1
-    near_rows, far_rows, table_out, taps_out, alive = refs[:5]
+    near_rows, far_rows, table_out, offsets_out, alive = refs[:5]
     pieces = refs[5 : 5 + lists]
     offsets, tile_count, volume, sems = refs[5 + lists :]
     member = lax.axis_index("tile")
@@ -74,13 +76,11 @@
     far = pl.multiple_of(jnp.where(even, 0, last), HALO)
     near_copy = pltpu.make_async_copy(intensity.at[pl.ds(near, HALO)], near_rows, sems.at[3])
     far_copy = pltpu.make_async_copy(intensity.at[pl.ds(far, HALO)], far_rows, sems.at[4])
-    later = [near_copy, far_copy]
-    for i, (here, there) in enumerate(
-        ((table_in, table_out), (taps_in, taps_out))
-    ):
-        later.append(pltpu.make_async_copy(here, there, sems.at[5 + i]))
+    table_copy = pltpu.make_async_copy(table_in, table_out, sems.at[5])
+    rows_copy = pltpu.make_async_copy(offsets_in, offsets_out, sems.at[6])
+    later = [near_copy, far_copy, table_copy, rows_copy]
     volume_copies = [
-        pltpu.make_async_copy(volume_in.at[j], volume.at[j], sems.at[8 + j]) for j in range(slots)
+        pltpu.make_async_copy(volume_in.at[j], volume.at[j], sems.at[7 + j]) for j in range(slots)
     ]
     for copy in volume_copies:
         copy.start()
@@ -148,21 +148,38 @@
     sums[...] = jnp.concatenate([packed, jnp.zeros((4, half), jnp.float32)], axis=0)
 
 
-def tap_matrix(half, terms):
-    place = np.arange(4 * half)[:, None] - half
-    apart = np.abs(place - np.arange(2 * half)[None, :])
-    taps = smoothing_taps()
-    rest = np.where(apart <= RIM, np.exp(-apart / decay_length) * taps[RIM], 0.0)
+def tap_terms(terms):
+    rest = smoothing_taps()[RIM:]
     parts = []
     for _ in range(terms):
-        part = rest.astype(jnp.bfloat16)
-        parts.append(part)
-        rest = rest - part.astype(np.float64)
-    return np.concatenate(parts, axis=0)
+        part = rest.astype(jnp.bfloat16).astype(np.float64)
+        parts.append([float(v) for v in part])
+        rest = rest - part
+    return parts
+
+
+def build_taps(taps, half, terms):
+    row = lax.broadcasted_iota(jnp.int32, (half, half), 0)
+    column = lax.broadcasted_iota(jnp.int32, (half, half), 1)
+    parts = tap_terms(terms)
+    for shift in (-1, 0, 1):
+        apart = jnp.abs(row - column + shift * half)
+        for term in range(terms):
+            value = jnp.zeros((half, half), jnp.float32)
+            for distance in range(RIM + 1):
+                value = jnp.where(apart == distance, parts[term][distance], value)
+            value = value.astype(taps.dtype)
+            for side in range(2):
+                base = (4 * term + 1 + side + shift) * half
+                taps[base : base + half, side * half : (side + 1) * half] = value
+    nothing = jnp.zeros((half, half), taps.dtype)
+    for term in range(terms):
+        taps[4 * term * half : (4 * term + 1) * half, half:] = nothing
+        taps[(4 * term + 3) * half : (4 * term + 4) * half, :half] = nothing
 
 
 def phase_kernel(slots, alive, offset_rows, intensity, near_rows, far_rows, footprint, *refs):
-    taps, phase, inverse, sums, starts, padded, across = refs
+    phase, inverse, sums, starts, padded, across, taps = refs
     rows, columns = intensity.shape
     half = footprint.shape[1] // 2
     blocks = columns // half
@@ -179,8 +196,9 @@
     far = far_rows[...].astype(jnp.float32)
     padded[:HALO, inner] = jnp.where(even, far, near).astype(padded.dtype)
     padded[HALO + rows :, inner] = jnp.where(even, near, far).astype(padded.dtype)
+    build_taps(taps, half, TERMS)
     tables(slots, blocks, offset_rows, alive, footprint[...], inverse, sums, starts)
-    terms = taps.shape[0] // (4 * half)
+    terms = TERMS
     pairs = blocks // 2
     group = max(d for d in range(1, min(GROUP, pairs) + 1) if pairs % d == 0)
     stride = rows // 8
@@ -258,20 +276,15 @@
     piece[base : base + EXTRA_ROWS, :] = extra.astype(jnp.int32).astype(piece.dtype)
 
 
-def angle_kernel(
-    direct, count, first, starts, phase, footprint, inverse, sums, *refs
-):
-    lists = count if direct else 1
-    arrived, residual, windows = refs[:lists], refs[lists], refs[lists + 1]
-    sent, images = refs[lists + 2 : -1], refs[-1]
+def subtract_loads(ks, starts, arrived, table, residual, images):
     member = lax.axis_index("tile")
-    table = footprint[...]
-    blocks, rows, half = phase.shape
-    voxels = footprint.shape[0]
+    blocks, rows, half = residual.shape
 
     def project(piece, image):
         image[...] = jnp.dot(
-            piece[...].reshape(SPREAD * rows, voxels), table, preferred_element_type=jnp.float32
+            piece[...].reshape(SPREAD * rows, table.shape[0]),
+            table,
+            preferred_element_type=jnp.float32,
         )
 
     def subtract(image, group):
@@ -289,11 +302,11 @@
                 block = jnp.minimum(block, blocks - 1)
             residual[block] = residual[block] - part
 
-    if direct:
-        for k in range(count):
-            project(arrived[k], images.at[k])
-        for k in range(count):
-            subtract(images.at[k], member ^ k)
+    if len(arrived) == len(ks):
+        for i, piece in enumerate(arrived):
+            project(piece, images.at[i])
+        for i, k in enumerate(ks):
+            subtract(images.at[i], member ^ k)
     else:
 
         def one(k, carry):
@@ -301,7 +314,22 @@
             subtract(images.at[0], k)
             return carry
 
-        lax.fori_loop(0, count, one, 0)
+        lax.fori_loop(0, len(ks), one, 0)
+
+
+def early_kernel(ks, starts, phase, footprint, *refs):
+    arrived, residual, images = refs[: len(ks)], refs[-2], refs[-1]
+    subtract_loads(ks, starts, arrived, footprint[...], residual, images)
+
+
+def angle_kernel(direct, count, ks, first, starts, phase, footprint, inverse, sums, *refs):
+    lists = len(ks) if direct else 1
+    arrived, residual, windows = refs[:lists], refs[lists], refs[lists + 1]
+    sent, images = refs[lists + 2 : -1], refs[-1]
+    member = lax.axis_index("tile")
+    table = footprint[...]
+    blocks, _, half = phase.shape
+    subtract_loads(ks, starts, arrived, table, residual, images)
 
     def weigh(window, group):
         start = starts[group, 0]
@@ -444,26 +472,25 @@
             return [jax.ShapeDtypeStruct(shape, dtype)] * count
         return [jax.ShapeDtypeStruct((count,) + shape, dtype)]
 
-    taps = jnp.asarray(tap_matrix(half, TERMS))
     halo_shape = jax.ShapeDtypeStruct((HALO, columns), intensity.dtype)
     load_shapes = piece_shapes((SPREAD, rows, voxels), jnp.bfloat16)
-    near_rows, far_rows, table, taps, alive, *loads = pl.pallas_call(
+    near_rows, far_rows, table, offset_rows, alive, *loads = pl.pallas_call(
         lambda *refs: load_kernel(direct, count, slots, *refs),
         out_shape=[halo_shape, halo_shape]
-        + [jax.ShapeDtypeStruct(x.shape, x.dtype) for x in (table, taps)]
+        + [jax.ShapeDtypeStruct(x.shape, x.dtype) for x in (table, offsets)]
         + [jax.ShapeDtypeStruct((8, offsets.shape[1]), jnp.float32)]
         + load_shapes,
-        in_specs=[HBM] * 6,
+        in_specs=[HBM] * 5,
         out_specs=[VMEM] * (5 + len(load_shapes)),
         scratch_shapes=[
             pltpu.SMEM(offsets.shape, jnp.int32),
             pltpu.SMEM(tile_count.shape, jnp.int32),
             pltpu.VMEM(volume.shape, volume.dtype),
-            pltpu.SemaphoreType.DMA((8 + slots,)),
+            pltpu.SemaphoreType.DMA((7 + slots,)),
         ],
         compiler_params=params(16),
         name="loads",
-    )(*[pltpu.with_memory_space_constraint(x, pltpu.HBM) for x in (offsets, tile_count, volume, table, taps, intensity[0])])
+    )(*[pltpu.with_memory_space_constraint(x, pltpu.HBM) for x in (offsets, tile_count, volume, table, intensity[0])])
     near_rows, far_rows = swap_halos(near_rows, far_rows)
     arrived = exchange(direct, count, loads)
 
@@ -476,25 +503,41 @@
             jax.ShapeDtypeStruct((EXTRA_ROWS, half), jnp.float32),
             jax.ShapeDtypeStruct((-(-count // 8) * 8, half), jnp.int32),
         ],
-        in_specs=[VMEM] * 7,
+        in_specs=[VMEM] * 6,
         out_specs=[VMEM] * 4,
         scratch_shapes=[
             pltpu.VMEM((tall, columns + 2 * half), intensity.dtype),
             pltpu.VMEM((blocks, tall, half), jnp.float32),
+            pltpu.VMEM((4 * TERMS * half, 2 * half), jnp.bfloat16),
         ],
         compiler_params=params(16),
         name="phase",
-    )(alive, offsets, intensity[0], near_rows, far_rows, table, taps)
+    )(alive, offset_rows, intensity[0], near_rows, far_rows, table)
 
     piece_shape = (2 * SPREAD * rows + EXTRA_ROWS, half)
     one_piece = jax.ShapeDtypeStruct(piece_shape, jnp.int16)
     first = partner_order(count, HOME_ORDER)[:FIRST] if direct else []
     rest = [k for k in range(count) if k not in first]
     sent_shapes = [one_piece] * len(first) if direct else piece_shapes(piece_shape, jnp.int16)
+    grid_shape = jax.ShapeDtypeStruct((blocks, rows, half), jnp.float32)
+    late = partner_order(count, OUT_ORDER)[-LATE:] if direct else list(range(count))
+    if direct:
+        early = [k for k in range(count) if k not in late]
+        phase_map = pl.pallas_call(
+            lambda *refs: early_kernel(early, *refs),
+            out_shape=grid_shape,
+            in_specs=[VMEM] * (3 + len(early)),
+            out_specs=VMEM,
+            scratch_shapes=[pltpu.VMEM((len(early), SPREAD * rows, voxels), jnp.float32)],
+            input_output_aliases={1: 0},
+            compiler_params=params(16),
+            name="early",
+        )(starts, phase_map, table, *[arrived[k] for k in early])
+        arrived = [arrived[k] for k in late]
     residual, windows, *sent = pl.pallas_call(
-        lambda *refs: angle_kernel(direct, count, first, *refs),
+        lambda *refs: angle_kernel(direct, count, late, first, *refs),
         out_shape=[
-            jax.ShapeDtypeStruct((blocks, rows, half), jnp.float32),
+            grid_shape,
             jax.ShapeDtypeStruct((count, rows, (SPREAD + 1) * half), jnp.bfloat16),
         ]
         + sent_shapes,
@@ -530,7 +573,7 @@
         out_specs=[VMEM, VMEM],
         compiler_params=params(16),
         name="write",
-    )(offsets, tile_count, residual)
+    )(offset_rows, tile_count, residual)
 
     def gather(ks, pieces, last, *earlier):
         flat = (slots, 2 * rows, half)
@@ -551,10 +594,10 @@
         )(plan, *pieces, *earlier)
 
     if direct:
-        near = list(range(count // 2))
-        far = list(range(count // 2, count))
-        partial = gather(near, received[: count // 2], False)
-        correction = gather(far, received[count // 2 :], True, *partial)[0]
+        last = [0] + partner_order(count, HOME_ORDER)[-LATE:]
+        soon = [k for k in range(count) if k not in last]
+        partial = gather(soon, [received[k] for k in soon], False)
+        correction = gather(last, [received[k] for k in last], True, *partial)[0]
     else:
         flat = gather(list(range(count)), received, True)[0]
         correction = jnp.swapaxes(flat.reshape(slots, 2, rows, half), 1, 2)

time: 45 us -> 40.6 us (0.902)
  starting transfers between devices: 27.5 us -> 25.1 us
  waiting for transfers between devices: 8.51 us -> 6.21 us
    ppermute x14, starting transfers between devices: 26.3 us -> 23.8 us  [exchange(): lax.ppermute(pieces[k], 'tile', [(i, i ^ k) for i in range(count)])]
    ppermute x14, waiting for transfers between devices: 8.5 us -> 6.2 us  [exchange(): lax.ppermute(pieces[k], 'tile', [(i, i ^ k) for i in range(count)])]
  transfers between devices with their start and end apart: 16 -> 16, of which waited for: 5 -> 4; matrix products, arithmetic and copies ran while one was open for 0% -> 0% of each run, Pallas kernels for 10% -> 13%
where the time goes in v6:
time: 40.6 us; the launch traced here: 40.4 us
  starting transfers between devices  25.1 us (62%)
  Pallas kernels  8.37 us (21%)
  waiting for transfers between devices  6.21 us (15%)
  between operations  0.74 us (2%)
    ppermute x14, starting transfers between devices, exchange(): lax.ppermute(pieces[k], 'tile', [(i, i ^ k) for i in range(count)])  23.8 us
    ppermute x14, waiting for transfers between devices, exchange(): lax.ppermute(pieces[k], 'tile', [(i, i ^ k) for i in range(count)])  6.2 us
    pallas_call x1, Pallas kernels, local(): pl.pallas_call(lambda *refs: phase_kernel(slots, *refs), out_shape=[jax.S...  2.18 us
    pallas_call x1, Pallas kernels, local(): pl.pallas_call(lambda *refs: write_kernel(count, slots, *refs), out_shape...  2.05 us
    pallas_call x1, Pallas kernels, local(): pl.pallas_call(lambda *refs: load_kernel(direct, count, slots, *refs), ou...  1.67 us
    pallas_call x2, Pallas kernels, gather(): pl.pallas_call(lambda *refs: gather_kernel(direct, count, ks, slots, rows...  1.05 us
  transfers between devices with their start and end apart: 16, of which 4 were waited for; matrix products, arithmetic and copies ran while one was open for 0% of the time, Pallas kernels for 13%

profile of v6, /device:TPU:0, one launch (start us, length us, event | category | flops | bytes accessed | tf_op | source)
XLA Modules:
  0.0 40.4 jit_solution(8304676937856294469)
XLA Ops:
  0.6 1.7 %loads.1 = (bf16[8,11264]{1,0:T(8,128)(2,1)S(1)}, bf16[8,11264]{1,0:T(8,128)(2,1)S(1)}, bf16[256,256]{1,0:T(8,128)(2,1)S(1)}, s32[8,64]{1,0:T(8,128)S(1)}, f32[8...) custom-call(s32[8,64]{1,0:T(8,128)} %bitcast.7, ...), custom_call_target="tpu_custom_call" | custom-call | tf_op jit(solution)/shard_map/loads/pallas_call | solution.py:477
  2.3 0.6 %collective-permute-start = (bf16[8,11264]{1,0:T(8,128)(2,1)S(1)}, bf16[8,11264]{1,0:T(8,128)(2,1)S(1)}, u32[]{:S(2)}, u32[]{:S(2)}) collective-permute-start(bf16[8,11264]{1,0:T(8,128)(2,1)S(1)} %get-tuple-element.36), channel_id=1, source_target_pairs={{0,1},{2,3},{1,0},{3,2},{4,5},{6,7},{5,4},{7,6},{8,9},{10,11},{9,8... | collective-permute-start | bytes 540680 | tf_op jit(solution)/shard_map/ppermute | solution.py:449
  2.9 0.7 %collective-permute-start.1 = (bf16[8,11264]{1,0:T(8,128)(2,1)S(1)}, bf16[8,11264]{1,0:T(8,128)(2,1)S(1)}, u32[]{:S(2)}, u32[]{:S(2)}) collective-permute-start(bf16[8,11264]{1,0:T(8,128)(2,1)S(1)} %get-tuple-element.37), channel_id=1, source_target_pairs={{1,2},{2,1},{5,6},{6,5},{9,10},{10,9},{13,14},{14,13},{17,18},{18,... | collective-permute-start | bytes 540680 | tf_op jit(solution)/shard_map/ppermute | solution.py:448
  3.5 3.6 %collective-permute-start.2 = (bf16[4,32,256]{2,1,0:T(8,128)(2,1)S(1)}, bf16[4,32,256]{2,1,0:T(8,128)(2,1)S(1)}, u32[]{:S(2)}, u32[]{:S(2)}) collective-permute-start(bf16[4,32,256]{2,1,0:T(8,128)(2,1)S(1)} %get-tuple-element.42), channel_id=1, source_target_pairs={{0,12},{4,8},{8,4},{12,0},{16,28},{20,24},{24,20},{28,16},{1,13},{... | collective-permute-start | bytes 196616 | tf_op jit(solution)/shard_map/ppermute | solution.py:435
  7.1 2.6 %collective-permute-start.3 = (bf16[4,32,256]{2,1,0:T(8,128)(2,1)S(1)}, bf16[4,32,256]{2,1,0:T(8,128)(2,1)S(1)}, u32[]{:S(2)}, u32[]{:S(2)}) collective-permute-start(bf16[4,32,256]{2,1,0:T(8,128)(2,1)S(1)} %get-tuple-element.43), channel_id=1, source_target_pairs={{0,16},{4,20},{8,24},{12,28},{16,0},{20,4},{24,8},{28,12},{1,17},{... | collective-permute-start | bytes 196616 | tf_op jit(solution)/shard_map/ppermute | solution.py:435
  9.7 0.3 collective-permute-start.4
  10.0 0.0 collective-permute-done.2.refs_4_
  10.0 3.4 %collective-permute-start.5 = (bf16[4,32,256]{2,1,0:T(8,128)(2,1)S(1)}, bf16[4,32,256]{2,1,0:T(8,128)(2,1)S(1)}, u32[]{:S(2)}, u32[]{:S(2)}) collective-permute-start(bf16[4,32,256]{2,1,0:T(8,128)(2,1)S(1)} %get-tuple-element.45), channel_id=1, source_target_pairs={{0,24},{4,28},{8,16},{12,20},{16,8},{20,12},{24,0},{28,4},{1,25},{... | collective-permute-start | bytes 196616 | tf_op jit(solution)/shard_map/ppermute | solution.py:435
  13.4 1.4 %collective-permute-start.6 = (bf16[4,32,256]{2,1,0:T(8,128)(2,1)S(1)}, bf16[4,32,256]{2,1,0:T(8,128)(2,1)S(1)}, u32[]{:S(2)}, u32[]{:S(2)}) collective-permute-start(bf16[4,32,256]{2,1,0:T(8,128)(2,1)S(1)} %get-tuple-element.46), channel_id=1, source_target_pairs={{0,28},{4,24},{8,20},{12,16},{16,12},{20,8},{24,4},{28,0},{1,29},{... | collective-permute-start | bytes 196616 | tf_op jit(solution)/shard_map/ppermute | solution.py:435
  14.8 0.0 collective-permute-done.refs_3_
  14.8 0.6 %collective-permute-start.7 = (bf16[4,32,256]{2,1,0:T(8,128)(2,1)S(1)}, bf16[4,32,256]{2,1,0:T(8,128)(2,1)S(1)}, u32[]{:S(2)}, u32[]{:S(2)}) collective-permute-start(bf16[4,32,256]{2,1,0:T(8,128)(2,1)S(1)} %get-tuple-element.49), channel_id=1, source_target_pairs={{0,8},{4,12},{8,0},{12,4},{16,24},{20,28},{24,16},{28,20},{1,9},{5... | collective-permute-start | bytes 196616 | tf_op jit(solution)/shard_map/ppermute | solution.py:435
  15.5 1.6 %collective-permute-start.8 = (bf16[4,32,256]{2,1,0:T(8,128)(2,1)S(1)}, bf16[4,32,256]{2,1,0:T(8,128)(2,1)S(1)}, u32[]{:S(2)}, u32[]{:S(2)}) collective-permute-start(bf16[4,32,256]{2,1,0:T(8,128)(2,1)S(1)} %get-tuple-element.50), channel_id=1, source_target_pairs={{0,4},{4,0},{8,12},{12,8},{16,20},{20,16},{24,28},{28,24},{1,5},{5... | collective-permute-start | bytes 196616 | tf_op jit(solution)/shard_map/ppermute | solution.py:435
  17.0 2.2 %phase.1 = (f32[88,32,128]{2,1,0:T(8,128)S(1)}, f32[96,128]{1,0:T(8,128)S(1)}, f32[8,128]{1,0:T(8,128)S(1)}, s32[8,128]{1,0:T(8,128)S(1)}) custom-call(f32[8,64]{1,0:T(8,128)S(1)} %get-tuple-element.35.refs_0_, s32[8,64]{1,0:T(8,128)S(1)} %get-tuple-element.34.refs_1_.refs_0_, bf16[32,11264]{1,0:T(8,128)(2,1)S(1)} %bitcast.5, ...), custom_call_target="tpu_custom_call" | custom-call | tf_op jit(solution)/shard_map/phase/pallas_call | solution.py:498
  19.2 1.3 %collective-permute-done.6.refs_8_ = bf16[4,32,256]{2,1,0:T(8,128)(2,1)S(1)} collective-permute-done((bf16[4,32,256]{2,1,0:T(8,128)(2,1)S(1)}, bf16[4,32,256]{2,1,0:T(8,128)(2,1)S(1)}, u32[]{:S(2)}, u32[]{:S(2)}) %collective-permute-start.6) | collective-permute-done | bytes 65568 | tf_op jit(solution)/shard_map/ppermute | solution.py:435
  20.5 0.3 early.1.refs_1_
  20.8 0.0 copy-start.1
  20.8 0.0 collective-permute-done.8.refs_6_
  20.9 0.5 %angle.1 = (f32[88,32,128]{2,1,0:T(8,128)S(1)}, bf16[8,32,640]{2,1,0:T(8,128)(2,1)S(1)}, s16[264,128]{1,0:T(8,128)(2,1)S(1)}) custom-call(s32[8,128]{1,0:T(8,128)S(1)} %get-tuple-element.39.refs_0_, f32[88,32,128]{2,1,0:T(8,128)S(1)} %early.1.refs_1_, ...), custom_call_target="tpu_custom_call", output_to_operand_aliasing={{0}: (1, {})} | custom-call | tf_op jit(solution)/shard_map/angle/pallas_call | solution.py:537
  21.4 2.2 %collective-permute-start.14 = (s16[264,128]{1,0:T(8,128)(2,1)S(1)}, s16[264,128]{1,0:T(8,128)(2,1)S(1)}, u32[]{:S(2)}, u32[]{:S(2)}) collective-permute-start(s16[264,128]{1,0:T(8,128)(2,1)S(1)} %get-tuple-element.61), channel_id=1, source_target_pairs={{0,24},{4,28},{8,16},{12,20},{16,8},{20,12},{24,0},{28,4},{1,25},{... | collective-permute-start | bytes 202760 | tf_op jit(solution)/shard_map/ppermute | solution.py:435
  23.6 0.6 %back.1 = (s16[264,128]{1,0:T(8,128)(2,1)S(1)}, s16[264,128]{1,0:T(8,128)(2,1)S(1)}, s16[264,128]{1,0:T(8,128)(2,1)S(1)}, s16[264,128]{1,0:T(8,128)(2,1)S(1)}, s...) custom-call(bf16[8,32,640]{2,1,0:T(8,128)(2,1)S(1)} %get-tuple-element.54.refs_0_, ...), custom_call_target="tpu_custom_call" | custom-call | tf_op jit(solution)/shard_map/back/pallas_call | solution.py:554
  24.2 1.4 %collective-permute-start.11 = (s16[264,128]{1,0:T(8,128)(2,1)S(1)}, s16[264,128]{1,0:T(8,128)(2,1)S(1)}, u32[]{:S(2)}, u32[]{:S(2)}) collective-permute-start(s16[264,128]{1,0:T(8,128)(2,1)S(1)} %get-tuple-element.58), channel_id=1, source_target_pairs={{0,12},{4,8},{8,4},{12,0},{16,28},{20,24},{24,20},{28,16},{1,13},{... | collective-permute-start | bytes 202760 | tf_op jit(solution)/shard_map/ppermute | solution.py:435
  25.7 1.7 %collective-permute-start.12 = (s16[264,128]{1,0:T(8,128)(2,1)S(1)}, s16[264,128]{1,0:T(8,128)(2,1)S(1)}, u32[]{:S(2)}, u32[]{:S(2)}) collective-permute-start(s16[264,128]{1,0:T(8,128)(2,1)S(1)} %get-tuple-element.59), channel_id=1, source_target_pairs={{0,16},{4,20},{8,24},{12,28},{16,0},{20,4},{24,8},{28,12},{1,17},{... | collective-permute-start | bytes 202760 | tf_op jit(solution)/shard_map/ppermute | solution.py:435
  27.4 2.4 %collective-permute-start.13 = (s16[264,128]{1,0:T(8,128)(2,1)S(1)}, s16[264,128]{1,0:T(8,128)(2,1)S(1)}, u32[]{:S(2)}, u32[]{:S(2)}) collective-permute-start(s16[264,128]{1,0:T(8,128)(2,1)S(1)} %get-tuple-element.60), channel_id=1, source_target_pairs={{0,20},{4,16},{8,28},{12,24},{16,4},{20,0},{24,12},{28,8},{1,21},{... | collective-permute-start | bytes 202760 | tf_op jit(solution)/shard_map/ppermute | solution.py:435
  29.8 2.2 %collective-permute-start.15 = (s16[264,128]{1,0:T(8,128)(2,1)S(1)}, s16[264,128]{1,0:T(8,128)(2,1)S(1)}, u32[]{:S(2)}, u32[]{:S(2)}) collective-permute-start(s16[264,128]{1,0:T(8,128)(2,1)S(1)} %get-tuple-element.62), channel_id=1, source_target_pairs={{0,28},{4,24},{8,20},{12,16},{16,12},{20,8},{24,4},{28,0},{1,29},{... | collective-permute-start | bytes 202760 | tf_op jit(solution)/shard_map/ppermute | solution.py:435
  32.1 0.0 collective-permute-done.14.refs_4_
  32.1 0.3 collective-permute-start.9
  32.4 2.0 %write.1 = (f32[32,11264]{1,0:T(8,128)}, s32[16,128]{1,0:T(8,128)S(1)}) custom-call(s32[8,64]{1,0:T(8,128)S(1)} %get-tuple-element.34.refs_1_.refs_0_, s32[8]{0:T(128)S(1)} %copy-done.1, f32[88,32,128]{2,1,0:T(8,128)S(1)} %get-tuple-element.51.refs_2_), custom_call_target="tpu_custom_call" | custom-call | tf_op jit(solution)/shard_map/write/pallas_call | solution.py:566
  34.4 3.8 %collective-permute-done.13.refs_3_ = s16[264,128]{1,0:T(8,128)(2,1)S(1)} collective-permute-done((s16[264,128]{1,0:T(8,128)(2,1)S(1)}, s16[264,128]{1,0:T(8,128)(2,1)S(1)}, u32[]{:S(2)}, u32[]{:S(2)}) %collective-permute-start.13) | collective-permute-done | bytes 67616 | tf_op jit(solution)/shard_map/ppermute | solution.py:435
  38.3 0.2 gather_first.1
  38.4 0.9 %collective-permute-done.9.refs_2_ = s16[264,128]{1,0:T(8,128)(2,1)S(1)} collective-permute-done((s16[264,128]{1,0:T(8,128)(2,1)S(1)}, s16[264,128]{1,0:T(8,128)(2,1)S(1)}, u32[]{:S(2)}, u32[]{:S(2)}) %collective-permute-start.9) | collective-permute-done | bytes 67616 | tf_op jit(solution)/shard_map/ppermute | solution.py:435
  39.3 0.2 collective-permute-done.10.refs_3_
  39.5 0.9 %gather_last.1 = (f32[8,32,256]{2,1,0:T(8,128)}, f32[8,128]{1,0:T(8,128)}) custom-call(s32[16,128]{1,0:T(8,128)S(1)} %get-tuple-element.53.refs_0_, s16[264,128]{1,0:T(8,128)(2,1)S(1)} %get-tuple-element.55.refs_1_, s16[264,128]{1,0:T(8,128)(2,1)S(1)} %collective-permute-done.9.refs_2_, s16[264,128]{1,0:T(8,128)(2,1)S(1)} %collective-permute-done.10.refs_3_, ...), custom_call_target="tpu_custom_call" | custom-call | tf_op jit(solution)/shard_map/gather_last/pallas_call | solution.py:581
  (12 shorter events, 0.0 us)
Async XLA Ops:
  0.6 16.4 %copy-start = (bf16[1,32,11264]{2,1,0:T(8,128)(2,1)S(1)}, bf16[1,32,11264]{2,1,0:T(8,128)(2,1)}, u32[]{:S(2)}) copy-start(bf16[1,32,11264]{2,1,0:T(8,128)(2,1)} %param.5) | copy-start | bytes 2162692
  2.3 12.5 %collective-permute-start = (bf16[8,11264]{1,0:T(8,128)(2,1)S(1)}, bf16[8,11264]{1,0:T(8,128)(2,1)S(1)}, u32[]{:S(2)}, u32[]{:S(2)}) collective-permute-start(bf16[8,11264]{1,0:T(8,128)(2,1)S(1)} %get-tuple-element.36), channel_id=1, source_target_pairs={{0,1},{2,3},{1,0},{3,2},{4,5},{6,7},{5,4},{7,6},{8,9},{10,11},{9,8... | collective-permute-start | bytes 540680 | tf_op jit(solution)/shard_map/ppermute | solution.py:449
  2.9 12.6 %collective-permute-start.1 = (bf16[8,11264]{1,0:T(8,128)(2,1)S(1)}, bf16[8,11264]{1,0:T(8,128)(2,1)S(1)}, u32[]{:S(2)}, u32[]{:S(2)}) collective-permute-start(bf16[8,11264]{1,0:T(8,128)(2,1)S(1)} %get-tuple-element.37), channel_id=1, source_target_pairs={{1,2},{2,1},{5,6},{6,5},{9,10},{10,9},{13,14},{14,13},{17,18},{18,... | collective-permute-start | bytes 540680 | tf_op jit(solution)/shard_map/ppermute | solution.py:448
  3.5 6.5 %collective-permute-start.2 = (bf16[4,32,256]{2,1,0:T(8,128)(2,1)S(1)}, bf16[4,32,256]{2,1,0:T(8,128)(2,1)S(1)}, u32[]{:S(2)}, u32[]{:S(2)}) collective-permute-start(bf16[4,32,256]{2,1,0:T(8,128)(2,1)S(1)} %get-tuple-element.42), channel_id=1, source_target_pairs={{0,12},{4,8},{8,4},{12,0},{16,28},{20,24},{24,20},{28,16},{1,13},{... | collective-permute-start | bytes 196616 | tf_op jit(solution)/shard_map/ppermute | solution.py:435
  7.1 6.2 %collective-permute-start.3 = (bf16[4,32,256]{2,1,0:T(8,128)(2,1)S(1)}, bf16[4,32,256]{2,1,0:T(8,128)(2,1)S(1)}, u32[]{:S(2)}, u32[]{:S(2)}) collective-permute-start(bf16[4,32,256]{2,1,0:T(8,128)(2,1)S(1)} %get-tuple-element.43), channel_id=1, source_target_pairs={{0,16},{4,20},{8,24},{12,28},{16,0},{20,4},{24,8},{28,12},{1,17},{... | collective-permute-start | bytes 196616 | tf_op jit(solution)/shard_map/ppermute | solution.py:435
  9.7 9.5 %collective-permute-start.4 = (bf16[4,32,256]{2,1,0:T(8,128)(2,1)S(1)}, bf16[4,32,256]{2,1,0:T(8,128)(2,1)S(1)}, u32[]{:S(2)}, u32[]{:S(2)}) collective-permute-start(bf16[4,32,256]{2,1,0:T(8,128)(2,1)S(1)} %get-tuple-element.44), channel_id=1, source_target_pairs={{0,20},{4,16},{8,28},{12,24},{16,4},{20,0},{24,12},{28,8},{1,21},{... | collective-permute-start | bytes 196616 | tf_op jit(solution)/shard_map/ppermute | solution.py:435
  10.0 9.2 %collective-permute-start.5 = (bf16[4,32,256]{2,1,0:T(8,128)(2,1)S(1)}, bf16[4,32,256]{2,1,0:T(8,128)(2,1)S(1)}, u32[]{:S(2)}, u32[]{:S(2)}) collective-permute-start(bf16[4,32,256]{2,1,0:T(8,128)(2,1)S(1)} %get-tuple-element.45), channel_id=1, source_target_pairs={{0,24},{4,28},{8,16},{12,20},{16,8},{20,12},{24,0},{28,4},{1,25},{... | collective-permute-start | bytes 196616 | tf_op jit(solution)/shard_map/ppermute | solution.py:435
  13.4 7.1 %collective-permute-start.6 = (bf16[4,32,256]{2,1,0:T(8,128)(2,1)S(1)}, bf16[4,32,256]{2,1,0:T(8,128)(2,1)S(1)}, u32[]{:S(2)}, u32[]{:S(2)}) collective-permute-start(bf16[4,32,256]{2,1,0:T(8,128)(2,1)S(1)} %get-tuple-element.46), channel_id=1, source_target_pairs={{0,28},{4,24},{8,20},{12,16},{16,12},{20,8},{24,4},{28,0},{1,29},{... | collective-permute-start | bytes 196616 | tf_op jit(solution)/shard_map/ppermute | solution.py:435
  14.8 6.0 %collective-permute-start.7 = (bf16[4,32,256]{2,1,0:T(8,128)(2,1)S(1)}, bf16[4,32,256]{2,1,0:T(8,128)(2,1)S(1)}, u32[]{:S(2)}, u32[]{:S(2)}) collective-permute-start(bf16[4,32,256]{2,1,0:T(8,128)(2,1)S(1)} %get-tuple-element.49), channel_id=1, source_target_pairs={{0,8},{4,12},{8,0},{12,4},{16,24},{20,28},{24,16},{28,20},{1,9},{5... | collective-permute-start | bytes 196616 | tf_op jit(solution)/shard_map/ppermute | solution.py:435
  15.5 5.4 %collective-permute-start.8 = (bf16[4,32,256]{2,1,0:T(8,128)(2,1)S(1)}, bf16[4,32,256]{2,1,0:T(8,128)(2,1)S(1)}, u32[]{:S(2)}, u32[]{:S(2)}) collective-permute-start(bf16[4,32,256]{2,1,0:T(8,128)(2,1)S(1)} %get-tuple-element.50), channel_id=1, source_target_pairs={{0,4},{4,0},{8,12},{12,8},{16,20},{20,16},{24,28},{28,24},{1,5},{5... | collective-permute-start | bytes 196616 | tf_op jit(solution)/shard_map/ppermute | solution.py:435
  20.8 11.6 %copy-start.1 = (s32[8]{0:T(128)S(1)}, s32[8]{0:T(128)}, u32[]{:S(2)}) copy-start(s32[8]{0:T(128)} %refs_1_.3) | copy-start | bytes 100
  21.4 10.7 %collective-permute-start.14 = (s16[264,128]{1,0:T(8,128)(2,1)S(1)}, s16[264,128]{1,0:T(8,128)(2,1)S(1)}, u32[]{:S(2)}, u32[]{:S(2)}) collective-permute-start(s16[264,128]{1,0:T(8,128)(2,1)S(1)} %get-tuple-element.61), channel_id=1, source_target_pairs={{0,24},{4,28},{8,16},{12,20},{16,8},{20,12},{24,0},{28,4},{1,25},{... | collective-permute-start | bytes 202760 | tf_op jit(solution)/shard_map/ppermute | solution.py:435
  24.2 8.2 %collective-permute-start.11 = (s16[264,128]{1,0:T(8,128)(2,1)S(1)}, s16[264,128]{1,0:T(8,128)(2,1)S(1)}, u32[]{:S(2)}, u32[]{:S(2)}) collective-permute-start(s16[264,128]{1,0:T(8,128)(2,1)S(1)} %get-tuple-element.58), channel_id=1, source_target_pairs={{0,12},{4,8},{8,4},{12,0},{16,28},{20,24},{24,20},{28,16},{1,13},{... | collective-permute-start | bytes 202760 | tf_op jit(solution)/shard_map/ppermute | solution.py:435
  25.7 8.8 %collective-permute-start.12 = (s16[264,128]{1,0:T(8,128)(2,1)S(1)}, s16[264,128]{1,0:T(8,128)(2,1)S(1)}, u32[]{:S(2)}, u32[]{:S(2)}) collective-permute-start(s16[264,128]{1,0:T(8,128)(2,1)S(1)} %get-tuple-element.59), channel_id=1, source_target_pairs={{0,16},{4,20},{8,24},{12,28},{16,0},{20,4},{24,8},{28,12},{1,17},{... | collective-permute-start | bytes 202760 | tf_op jit(solution)/shard_map/ppermute | solution.py:435
  27.4 10.8 %collective-permute-start.13 = (s16[264,128]{1,0:T(8,128)(2,1)S(1)}, s16[264,128]{1,0:T(8,128)(2,1)S(1)}, u32[]{:S(2)}, u32[]{:S(2)}) collective-permute-start(s16[264,128]{1,0:T(8,128)(2,1)S(1)} %get-tuple-element.60), channel_id=1, source_target_pairs={{0,20},{4,16},{8,28},{12,24},{16,4},{20,0},{24,12},{28,8},{1,21},{... | collective-permute-start | bytes 202760 | tf_op jit(solution)/shard_map/ppermute | solution.py:435
  29.8 8.4 %collective-permute-start.15 = (s16[264,128]{1,0:T(8,128)(2,1)S(1)}, s16[264,128]{1,0:T(8,128)(2,1)S(1)}, u32[]{:S(2)}, u32[]{:S(2)}) collective-permute-start(s16[264,128]{1,0:T(8,128)(2,1)S(1)} %get-tuple-element.62), channel_id=1, source_target_pairs={{0,28},{4,24},{8,20},{12,16},{16,12},{20,8},{24,4},{28,0},{1,29},{... | collective-permute-start | bytes 202760 | tf_op jit(solution)/shard_map/ppermute | solution.py:435
  32.1 7.2 %collective-permute-start.9 = (s16[264,128]{1,0:T(8,128)(2,1)S(1)}, s16[264,128]{1,0:T(8,128)(2,1)S(1)}, u32[]{:S(2)}, u32[]{:S(2)}) collective-permute-start(s16[264,128]{1,0:T(8,128)(2,1)S(1)} %get-tuple-element.56), channel_id=1, source_target_pairs={{0,4},{4,0},{8,12},{12,8},{16,20},{20,16},{24,28},{28,24},{1,5},{5... | collective-permute-start | bytes 202760 | tf_op jit(solution)/shard_map/ppermute | solution.py:435
  32.4 7.1 %collective-permute-start.10 = (s16[264,128]{1,0:T(8,128)(2,1)S(1)}, s16[264,128]{1,0:T(8,128)(2,1)S(1)}, u32[]{:S(2)}, u32[]{:S(2)}) collective-permute-start(s16[264,128]{1,0:T(8,128)(2,1)S(1)} %get-tuple-element.57), channel_id=1, source_target_pairs={{0,8},{4,12},{8,0},{12,4},{16,24},{20,28},{24,16},{28,20},{1,9},{5... | collective-permute-start | bytes 202760 | tf_op jit(solution)/shard_map/ppermute | solution.py:435

commit v7 on v6

--- a/solution.py
+++ b/solution.py
@@ -12,10 +12,10 @@
 HALO = 8
 GROUP = 22
 TERMS = 2
-FIRST = 1
-LATE = 2
+FIRST = 2
+LATE = 3
 OUT_ORDER = (7, 5, 6, 4, 3, 2, 1)
-HOME_ORDER = (6, 5, 7, 4, 3, 1, 2)
+HOME_ORDER = (6, 5, 7, 4, 3, 2, 1)
 DIRECT_LIMIT = 16
 EXTRA_ROWS = 8
 SUM_SCALE = 2048.0

time: 40.6 us -> 41.3 us (1.017)
  the two profiles are of different devices: /device:TPU:0 before, /device:TPU:8 now
where the time goes in v7:
time: 41.3 us; the launch traced here: 40.9 us
  starting transfers between devices  25.3 us (61%)
  Pallas kernels  8.32 us (20%)
  waiting for transfers between devices  6.43 us (16%)
  between operations  0.76 us (2%)
    ppermute x14, starting transfers between devices, exchange(): lax.ppermute(pieces[k], 'tile', [(i, i ^ k) for i in range(count)])  24.6 us
    ppermute x14, waiting for transfers between devices, exchange(): lax.ppermute(pieces[k], 'tile', [(i, i ^ k) for i in range(count)])  6.43 us
    pallas_call x1, Pallas kernels, local(): pl.pallas_call(lambda *refs: phase_kernel(slots, *refs), out_shape=[jax.S...  2.18 us
    pallas_call x1, Pallas kernels, local(): pl.pallas_call(lambda *refs: write_kernel(count, slots, *refs), out_shape...  2.04 us
    pallas_call x1, Pallas kernels, local(): pl.pallas_call(lambda *refs: load_kernel(direct, count, slots, *refs), ou...  1.67 us
    pallas_call x2, Pallas kernels, gather(): pl.pallas_call(lambda *refs: gather_kernel(direct, count, ks, slots, rows...  1.05 us
  transfers between devices with their start and end apart: 16, of which 6 were waited for; matrix products, arithmetic and copies ran while one was open for 0% of the time, Pallas kernels for 13%

profile of v7, /device:TPU:8, one launch (start us, length us, event | category | flops | bytes accessed | tf_op | source)
XLA Modules:
  0.0 40.9 jit_solution(17108580152494086916)
XLA Ops:
  0.6 1.7 %loads.1 = (bf16[8,11264]{1,0:T(8,128)(2,1)S(1)}, bf16[8,11264]{1,0:T(8,128)(2,1)S(1)}, bf16[256,256]{1,0:T(8,128)(2,1)S(1)}, s32[8,64]{1,0:T(8,128)S(1)}, f32[8...) custom-call(s32[8,64]{1,0:T(8,128)} %bitcast.7, ...), custom_call_target="tpu_custom_call" | custom-call | tf_op jit(solution)/shard_map/loads/pallas_call | solution.py:477
  2.3 0.1 collective-permute-start
  2.4 0.7 %collective-permute-start.1 = (bf16[8,11264]{1,0:T(8,128)(2,1)S(1)}, bf16[8,11264]{1,0:T(8,128)(2,1)S(1)}, u32[]{:S(2)}, u32[]{:S(2)}) collective-permute-start(bf16[8,11264]{1,0:T(8,128)(2,1)S(1)} %get-tuple-element.37), channel_id=1, source_target_pairs={{1,2},{2,1},{5,6},{6,5},{9,10},{10,9},{13,14},{14,13},{17,18},{18,... | collective-permute-start | bytes 540680 | tf_op jit(solution)/shard_map/ppermute | solution.py:448
  3.1 2.7 %collective-permute-start.2 = (bf16[4,32,256]{2,1,0:T(8,128)(2,1)S(1)}, bf16[4,32,256]{2,1,0:T(8,128)(2,1)S(1)}, u32[]{:S(2)}, u32[]{:S(2)}) collective-permute-start(bf16[4,32,256]{2,1,0:T(8,128)(2,1)S(1)} %get-tuple-element.42), channel_id=1, source_target_pairs={{0,16},{4,20},{8,24},{12,28},{16,0},{20,4},{24,8},{28,12},{1,17},{... | collective-permute-start | bytes 196616 | tf_op jit(solution)/shard_map/ppermute | solution.py:435
  5.7 1.3 %collective-permute-start.3 = (bf16[4,32,256]{2,1,0:T(8,128)(2,1)S(1)}, bf16[4,32,256]{2,1,0:T(8,128)(2,1)S(1)}, u32[]{:S(2)}, u32[]{:S(2)}) collective-permute-start(bf16[4,32,256]{2,1,0:T(8,128)(2,1)S(1)} %get-tuple-element.43), channel_id=1, source_target_pairs={{0,20},{4,16},{8,28},{12,24},{16,4},{20,0},{24,12},{28,8},{1,21},{... | collective-permute-start | bytes 196616 | tf_op jit(solution)/shard_map/ppermute | solution.py:435
  7.0 1.6 %collective-permute-start.4 = (bf16[4,32,256]{2,1,0:T(8,128)(2,1)S(1)}, bf16[4,32,256]{2,1,0:T(8,128)(2,1)S(1)}, u32[]{:S(2)}, u32[]{:S(2)}) collective-permute-start(bf16[4,32,256]{2,1,0:T(8,128)(2,1)S(1)} %get-tuple-element.44), channel_id=1, source_target_pairs={{0,24},{4,28},{8,16},{12,20},{16,8},{20,12},{24,0},{28,4},{1,25},{... | collective-permute-start | bytes 196616 | tf_op jit(solution)/shard_map/ppermute | solution.py:435
  8.6 0.0 collective-permute-done.2.refs_4_
  8.6 2.3 %collective-permute-start.5 = (bf16[4,32,256]{2,1,0:T(8,128)(2,1)S(1)}, bf16[4,32,256]{2,1,0:T(8,128)(2,1)S(1)}, u32[]{:S(2)}, u32[]{:S(2)}) collective-permute-start(bf16[4,32,256]{2,1,0:T(8,128)(2,1)S(1)} %get-tuple-element.45), channel_id=1, source_target_pairs={{0,28},{4,24},{8,20},{12,16},{16,12},{20,8},{24,4},{28,0},{1,29},{... | collective-permute-start | bytes 196616 | tf_op jit(solution)/shard_map/ppermute | solution.py:435
  10.9 1.0 %collective-permute-done.3.refs_5_ = bf16[4,32,256]{2,1,0:T(8,128)(2,1)S(1)} collective-permute-done((bf16[4,32,256]{2,1,0:T(8,128)(2,1)S(1)}, bf16[4,32,256]{2,1,0:T(8,128)(2,1)S(1)}, u32[]{:S(2)}, u32[]{:S(2)}) %collective-permute-start.3) | collective-permute-done | bytes 65568 | tf_op jit(solution)/shard_map/ppermute | solution.py:435
  11.9 3.3 %collective-permute-start.6 = (bf16[4,32,256]{2,1,0:T(8,128)(2,1)S(1)}, bf16[4,32,256]{2,1,0:T(8,128)(2,1)S(1)}, u32[]{:S(2)}, u32[]{:S(2)}) collective-permute-start(bf16[4,32,256]{2,1,0:T(8,128)(2,1)S(1)} %get-tuple-element.48), channel_id=1, source_target_pairs={{0,12},{4,8},{8,4},{12,0},{16,28},{20,24},{24,20},{28,16},{1,13},{... | collective-permute-start | bytes 196616 | tf_op jit(solution)/shard_map/ppermute | solution.py:435
  15.3 1.0 %collective-permute-start.7 = (bf16[4,32,256]{2,1,0:T(8,128)(2,1)S(1)}, bf16[4,32,256]{2,1,0:T(8,128)(2,1)S(1)}, u32[]{:S(2)}, u32[]{:S(2)}) collective-permute-start(bf16[4,32,256]{2,1,0:T(8,128)(2,1)S(1)} %get-tuple-element.49), channel_id=1, source_target_pairs={{0,8},{4,12},{8,0},{12,4},{16,24},{20,28},{24,16},{28,20},{1,9},{5... | collective-permute-start | bytes 196616 | tf_op jit(solution)/shard_map/ppermute | solution.py:435
  16.3 1.5 %collective-permute-start.8 = (bf16[4,32,256]{2,1,0:T(8,128)(2,1)S(1)}, bf16[4,32,256]{2,1,0:T(8,128)(2,1)S(1)}, u32[]{:S(2)}, u32[]{:S(2)}) collective-permute-start(bf16[4,32,256]{2,1,0:T(8,128)(2,1)S(1)} %get-tuple-element.50), channel_id=1, source_target_pairs={{0,4},{4,0},{8,12},{12,8},{16,20},{20,16},{24,28},{28,24},{1,5},{5... | collective-permute-start | bytes 196616 | tf_op jit(solution)/shard_map/ppermute | solution.py:435
  17.8 2.2 %phase.1 = (f32[88,32,128]{2,1,0:T(8,128)S(1)}, f32[96,128]{1,0:T(8,128)S(1)}, f32[8,128]{1,0:T(8,128)S(1)}, s32[8,128]{1,0:T(8,128)S(1)}) custom-call(f32[8,64]{1,0:T(8,128)S(1)} %get-tuple-element.35.refs_0_, s32[8,64]{1,0:T(8,128)S(1)} %get-tuple-element.34.refs_1_.refs_0_, bf16[32,11264]{1,0:T(8,128)(2,1)S(1)} %bitcast.5, ...), custom_call_target="tpu_custom_call" | custom-call | tf_op jit(solution)/shard_map/phase/pallas_call | solution.py:498
  20.0 0.3 early.1.refs_1_
  20.3 0.0 copy-start.1
  20.3 0.5 %collective-permute-done.7.refs_6_ = bf16[4,32,256]{2,1,0:T(8,128)(2,1)S(1)} collective-permute-done((bf16[4,32,256]{2,1,0:T(8,128)(2,1)S(1)}, bf16[4,32,256]{2,1,0:T(8,128)(2,1)S(1)}, u32[]{:S(2)}, u32[]{:S(2)}) %collective-permute-start.7) | collective-permute-done | bytes 65568 | tf_op jit(solution)/shard_map/ppermute | solution.py:435
  20.8 0.4 %collective-permute-done.8.refs_7_ = bf16[4,32,256]{2,1,0:T(8,128)(2,1)S(1)} collective-permute-done((bf16[4,32,256]{2,1,0:T(8,128)(2,1)S(1)}, bf16[4,32,256]{2,1,0:T(8,128)(2,1)S(1)}, u32[]{:S(2)}, u32[]{:S(2)}) %collective-permute-start.8) | collective-permute-done | bytes 65568 | tf_op jit(solution)/shard_map/ppermute | solution.py:435
  21.2 0.6 %angle.1 = (f32[88,32,128]{2,1,0:T(8,128)S(1)}, bf16[8,32,640]{2,1,0:T(8,128)(2,1)S(1)}, s16[264,128]{1,0:T(8,128)(2,1)S(1)}, s16[264,128]{1,0:T(8,128)(2,1)S(1)}) custom-call(s32[8,128]{1,0:T(8,128)S(1)} %get-tuple-element.39.refs_0_, f32[88,32,128]{2,1,0:T(8,128)S(1)} %early.1.refs_1_, ...), custom_call_target="tpu_custom_call", output_to_operand_aliasing={{0}: (1, {})} | custom-call | tf_op jit(solution)/shard_map/angle/pallas_call | solution.py:537
  21.8 4.0 %collective-permute-start.13 = (s16[264,128]{1,0:T(8,128)(2,1)S(1)}, s16[264,128]{1,0:T(8,128)(2,1)S(1)}, u32[]{:S(2)}, u32[]{:S(2)}) collective-permute-start(s16[264,128]{1,0:T(8,128)(2,1)S(1)} %get-tuple-element.60), channel_id=1, source_target_pairs={{0,20},{4,16},{8,28},{12,24},{16,4},{20,0},{24,12},{28,8},{1,21},{... | collective-permute-start | bytes 202760 | tf_op jit(solution)/shard_map/ppermute | solution.py:435
  25.8 0.8 %collective-permute-start.14 = (s16[264,128]{1,0:T(8,128)(2,1)S(1)}, s16[264,128]{1,0:T(8,128)(2,1)S(1)}, u32[]{:S(2)}, u32[]{:S(2)}) collective-permute-start(s16[264,128]{1,0:T(8,128)(2,1)S(1)} %get-tuple-element.61), channel_id=1, source_target_pairs={{0,24},{4,28},{8,16},{12,20},{16,8},{20,12},{24,0},{28,4},{1,25},{... | collective-permute-start | bytes 202760 | tf_op jit(solution)/shard_map/ppermute | solution.py:435
  26.6 0.5 %back.1 = (s16[264,128]{1,0:T(8,128)(2,1)S(1)}, s16[264,128]{1,0:T(8,128)(2,1)S(1)}, s16[264,128]{1,0:T(8,128)(2,1)S(1)}, s16[264,128]{1,0:T(8,128)(2,1)S(1)}, s...) custom-call(bf16[8,32,640]{2,1,0:T(8,128)(2,1)S(1)} %get-tuple-element.54.refs_0_, ...), custom_call_target="tpu_custom_call" | custom-call | tf_op jit(solution)/shard_map/back/pallas_call | solution.py:554
  27.2 0.8 %collective-permute-start.9 = (s16[264,128]{1,0:T(8,128)(2,1)S(1)}, s16[264,128]{1,0:T(8,128)(2,1)S(1)}, u32[]{:S(2)}, u32[]{:S(2)}) collective-permute-start(s16[264,128]{1,0:T(8,128)(2,1)S(1)} %get-tuple-element.56), channel_id=1, source_target_pairs={{0,12},{4,8},{8,4},{12,0},{16,28},{20,24},{24,20},{28,16},{1,13},{... | collective-permute-start | bytes 202760 | tf_op jit(solution)/shard_map/ppermute | solution.py:435
  28.0 2.3 %collective-permute-start.12 = (s16[264,128]{1,0:T(8,128)(2,1)S(1)}, s16[264,128]{1,0:T(8,128)(2,1)S(1)}, u32[]{:S(2)}, u32[]{:S(2)}) collective-permute-start(s16[264,128]{1,0:T(8,128)(2,1)S(1)} %get-tuple-element.59), channel_id=1, source_target_pairs={{0,16},{4,20},{8,24},{12,28},{16,0},{20,4},{24,8},{28,12},{1,17},{... | collective-permute-start | bytes 202760 | tf_op jit(solution)/shard_map/ppermute | solution.py:435
  30.3 1.3 %collective-permute-start.15 = (s16[264,128]{1,0:T(8,128)(2,1)S(1)}, s16[264,128]{1,0:T(8,128)(2,1)S(1)}, u32[]{:S(2)}, u32[]{:S(2)}) collective-permute-start(s16[264,128]{1,0:T(8,128)(2,1)S(1)} %get-tuple-element.62), channel_id=1, source_target_pairs={{0,28},{4,24},{8,20},{12,16},{16,12},{20,8},{24,4},{28,0},{1,29},{... | collective-permute-start | bytes 202760 | tf_op jit(solution)/shard_map/ppermute | solution.py:435
  31.6 1.6 %collective-permute-start.10 = (s16[264,128]{1,0:T(8,128)(2,1)S(1)}, s16[264,128]{1,0:T(8,128)(2,1)S(1)}, u32[]{:S(2)}, u32[]{:S(2)}) collective-permute-start(s16[264,128]{1,0:T(8,128)(2,1)S(1)} %get-tuple-element.57), channel_id=1, source_target_pairs={{0,8},{4,12},{8,0},{12,4},{16,24},{20,28},{24,16},{28,20},{1,9},{5... | collective-permute-start | bytes 202760 | tf_op jit(solution)/shard_map/ppermute | solution.py:435
  33.3 1.7 %collective-permute-done.14.refs_3_ = s16[264,128]{1,0:T(8,128)(2,1)S(1)} collective-permute-done((s16[264,128]{1,0:T(8,128)(2,1)S(1)}, s16[264,128]{1,0:T(8,128)(2,1)S(1)}, u32[]{:S(2)}, u32[]{:S(2)}) %collective-permute-start.14) | collective-permute-done | bytes 67616 | tf_op jit(solution)/shard_map/ppermute | solution.py:435
  34.9 0.0 collective-permute-start.11
  35.0 2.0 %write.1 = (f32[32,11264]{1,0:T(8,128)}, s32[16,128]{1,0:T(8,128)S(1)}) custom-call(s32[8,64]{1,0:T(8,128)S(1)} %get-tuple-element.34.refs_1_.refs_0_, s32[8]{0:T(128)S(1)} %copy-done.1, f32[88,32,128]{2,1,0:T(8,128)S(1)} %get-tuple-element.51.refs_2_), custom_call_target="tpu_custom_call" | custom-call | tf_op jit(solution)/shard_map/write/pallas_call | solution.py:566
  37.0 1.6 %collective-permute-done.15.refs_4_ = s16[264,128]{1,0:T(8,128)(2,1)S(1)} collective-permute-done((s16[264,128]{1,0:T(8,128)(2,1)S(1)}, s16[264,128]{1,0:T(8,128)(2,1)S(1)}, u32[]{:S(2)}, u32[]{:S(2)}) %collective-permute-start.15) | collective-permute-done | bytes 67616 | tf_op jit(solution)/shard_map/ppermute | solution.py:435
  38.6 0.2 gather_first.1
  38.8 1.2 %collective-permute-done.11.refs_4_ = s16[264,128]{1,0:T(8,128)(2,1)S(1)} collective-permute-done((s16[264,128]{1,0:T(8,128)(2,1)S(1)}, s16[264,128]{1,0:T(8,128)(2,1)S(1)}, u32[]{:S(2)}, u32[]{:S(2)}) %collective-permute-start.11) | collective-permute-done | bytes 67616 | tf_op jit(solution)/shard_map/ppermute | solution.py:435
  40.0 0.9 %gather_last.1 = (f32[8,32,256]{2,1,0:T(8,128)}, f32[8,128]{1,0:T(8,128)}) custom-call(s32[16,128]{1,0:T(8,128)S(1)} %get-tuple-element.53.refs_0_, s16[264,128]{1,0:T(8,128)(2,1)S(1)} %get-tuple-element.55.refs_1_, s16[264,128]{1,0:T(8,128)(2,1)S(1)} %collective-permute-done.9.refs_2_, s16[264,128]{1,0:T(8,128)(2,1)S(1)} %collective-permute-done.10.refs_3_, ...), custom_call_target="tpu_custom_call" | custom-call | tf_op jit(solution)/shard_map/gather_last/pallas_call | solution.py:581
  (12 shorter events, 0.0 us)
Async XLA Ops:
  0.6 17.2 %copy-start = (bf16[1,32,11264]{2,1,0:T(8,128)(2,1)S(1)}, bf16[1,32,11264]{2,1,0:T(8,128)(2,1)}, u32[]{:S(2)}) copy-start(bf16[1,32,11264]{2,1,0:T(8,128)(2,1)} %param.5) | copy-start | bytes 2162692
  2.3 13.0 %collective-permute-start = (bf16[8,11264]{1,0:T(8,128)(2,1)S(1)}, bf16[8,11264]{1,0:T(8,128)(2,1)S(1)}, u32[]{:S(2)}, u32[]{:S(2)}) collective-permute-start(bf16[8,11264]{1,0:T(8,128)(2,1)S(1)} %get-tuple-element.36), channel_id=1, source_target_pairs={{0,1},{2,3},{1,0},{3,2},{4,5},{6,7},{5,4},{7,6},{8,9},{10,11},{9,8... | collective-permute-start | bytes 540680 | tf_op jit(solution)/shard_map/ppermute | solution.py:449
  2.4 13.9 %collective-permute-start.1 = (bf16[8,11264]{1,0:T(8,128)(2,1)S(1)}, bf16[8,11264]{1,0:T(8,128)(2,1)S(1)}, u32[]{:S(2)}, u32[]{:S(2)}) collective-permute-start(bf16[8,11264]{1,0:T(8,128)(2,1)S(1)} %get-tuple-element.37), channel_id=1, source_target_pairs={{1,2},{2,1},{5,6},{6,5},{9,10},{10,9},{13,14},{14,13},{17,18},{18,... | collective-permute-start | bytes 540680 | tf_op jit(solution)/shard_map/ppermute | solution.py:448
  3.1 5.5 %collective-permute-start.2 = (bf16[4,32,256]{2,1,0:T(8,128)(2,1)S(1)}, bf16[4,32,256]{2,1,0:T(8,128)(2,1)S(1)}, u32[]{:S(2)}, u32[]{:S(2)}) collective-permute-start(bf16[4,32,256]{2,1,0:T(8,128)(2,1)S(1)} %get-tuple-element.42), channel_id=1, source_target_pairs={{0,16},{4,20},{8,24},{12,28},{16,0},{20,4},{24,8},{28,12},{1,17},{... | collective-permute-start | bytes 196616 | tf_op jit(solution)/shard_map/ppermute | solution.py:435
  5.7 6.2 %collective-permute-start.3 = (bf16[4,32,256]{2,1,0:T(8,128)(2,1)S(1)}, bf16[4,32,256]{2,1,0:T(8,128)(2,1)S(1)}, u32[]{:S(2)}, u32[]{:S(2)}) collective-permute-start(bf16[4,32,256]{2,1,0:T(8,128)(2,1)S(1)} %get-tuple-element.43), channel_id=1, source_target_pairs={{0,20},{4,16},{8,28},{12,24},{16,4},{20,0},{24,12},{28,8},{1,21},{... | collective-permute-start | bytes 196616 | tf_op jit(solution)/shard_map/ppermute | solution.py:435
  7.0 13.0 %collective-permute-start.4 = (bf16[4,32,256]{2,1,0:T(8,128)(2,1)S(1)}, bf16[4,32,256]{2,1,0:T(8,128)(2,1)S(1)}, u32[]{:S(2)}, u32[]{:S(2)}) collective-permute-start(bf16[4,32,256]{2,1,0:T(8,128)(2,1)S(1)} %get-tuple-element.44), channel_id=1, source_target_pairs={{0,24},{4,28},{8,16},{12,20},{16,8},{20,12},{24,0},{28,4},{1,25},{... | collective-permute-start | bytes 196616 | tf_op jit(solution)/shard_map/ppermute | solution.py:435
  8.6 11.4 %collective-permute-start.5 = (bf16[4,32,256]{2,1,0:T(8,128)(2,1)S(1)}, bf16[4,32,256]{2,1,0:T(8,128)(2,1)S(1)}, u32[]{:S(2)}, u32[]{:S(2)}) collective-permute-start(bf16[4,32,256]{2,1,0:T(8,128)(2,1)S(1)} %get-tuple-element.45), channel_id=1, source_target_pairs={{0,28},{4,24},{8,20},{12,16},{16,12},{20,8},{24,4},{28,0},{1,29},{... | collective-permute-start | bytes 196616 | tf_op jit(solution)/shard_map/ppermute | solution.py:435
  11.9 8.4 %collective-permute-start.6 = (bf16[4,32,256]{2,1,0:T(8,128)(2,1)S(1)}, bf16[4,32,256]{2,1,0:T(8,128)(2,1)S(1)}, u32[]{:S(2)}, u32[]{:S(2)}) collective-permute-start(bf16[4,32,256]{2,1,0:T(8,128)(2,1)S(1)} %get-tuple-element.48), channel_id=1, source_target_pairs={{0,12},{4,8},{8,4},{12,0},{16,28},{20,24},{24,20},{28,16},{1,13},{... | collective-permute-start | bytes 196616 | tf_op jit(solution)/shard_map/ppermute | solution.py:435
  15.3 5.5 %collective-permute-start.7 = (bf16[4,32,256]{2,1,0:T(8,128)(2,1)S(1)}, bf16[4,32,256]{2,1,0:T(8,128)(2,1)S(1)}, u32[]{:S(2)}, u32[]{:S(2)}) collective-permute-start(bf16[4,32,256]{2,1,0:T(8,128)(2,1)S(1)} %get-tuple-element.49), channel_id=1, source_target_pairs={{0,8},{4,12},{8,0},{12,4},{16,24},{20,28},{24,16},{28,20},{1,9},{5... | collective-permute-start | bytes 196616 | tf_op jit(solution)/shard_map/ppermute | solution.py:435
  16.3 4.9 %collective-permute-start.8 = (bf16[4,32,256]{2,1,0:T(8,128)(2,1)S(1)}, bf16[4,32,256]{2,1,0:T(8,128)(2,1)S(1)}, u32[]{:S(2)}, u32[]{:S(2)}) collective-permute-start(bf16[4,32,256]{2,1,0:T(8,128)(2,1)S(1)} %get-tuple-element.50), channel_id=1, source_target_pairs={{0,4},{4,0},{8,12},{12,8},{16,20},{20,16},{24,28},{28,24},{1,5},{5... | collective-permute-start | bytes 196616 | tf_op jit(solution)/shard_map/ppermute | solution.py:435
  20.3 14.7 %copy-start.1 = (s32[8]{0:T(128)S(1)}, s32[8]{0:T(128)}, u32[]{:S(2)}) copy-start(s32[8]{0:T(128)} %refs_1_.3) | copy-start | bytes 100
  21.8 9.8 %collective-permute-start.13 = (s16[264,128]{1,0:T(8,128)(2,1)S(1)}, s16[264,128]{1,0:T(8,128)(2,1)S(1)}, u32[]{:S(2)}, u32[]{:S(2)}) collective-permute-start(s16[264,128]{1,0:T(8,128)(2,1)S(1)} %get-tuple-element.60), channel_id=1, source_target_pairs={{0,20},{4,16},{8,28},{12,24},{16,4},{20,0},{24,12},{28,8},{1,21},{... | collective-permute-start | bytes 202760 | tf_op jit(solution)/shard_map/ppermute | solution.py:435
  25.8 9.1 %collective-permute-start.14 = (s16[264,128]{1,0:T(8,128)(2,1)S(1)}, s16[264,128]{1,0:T(8,128)(2,1)S(1)}, u32[]{:S(2)}, u32[]{:S(2)}) collective-permute-start(s16[264,128]{1,0:T(8,128)(2,1)S(1)} %get-tuple-element.61), channel_id=1, source_target_pairs={{0,24},{4,28},{8,16},{12,20},{16,8},{20,12},{24,0},{28,4},{1,25},{... | collective-permute-start | bytes 202760 | tf_op jit(solution)/shard_map/ppermute | solution.py:435
  27.2 11.6 %collective-permute-start.9 = (s16[264,128]{1,0:T(8,128)(2,1)S(1)}, s16[264,128]{1,0:T(8,128)(2,1)S(1)}, u32[]{:S(2)}, u32[]{:S(2)}) collective-permute-start(s16[264,128]{1,0:T(8,128)(2,1)S(1)} %get-tuple-element.56), channel_id=1, source_target_pairs={{0,12},{4,8},{8,4},{12,0},{16,28},{20,24},{24,20},{28,16},{1,13},{... | collective-permute-start | bytes 202760 | tf_op jit(solution)/shard_map/ppermute | solution.py:435
  28.0 9.1 %collective-permute-start.12 = (s16[264,128]{1,0:T(8,128)(2,1)S(1)}, s16[264,128]{1,0:T(8,128)(2,1)S(1)}, u32[]{:S(2)}, u32[]{:S(2)}) collective-permute-start(s16[264,128]{1,0:T(8,128)(2,1)S(1)} %get-tuple-element.59), channel_id=1, source_target_pairs={{0,16},{4,20},{8,24},{12,28},{16,0},{20,4},{24,8},{28,12},{1,17},{... | collective-permute-start | bytes 202760 | tf_op jit(solution)/shard_map/ppermute | solution.py:435
  30.3 8.4 %collective-permute-start.15 = (s16[264,128]{1,0:T(8,128)(2,1)S(1)}, s16[264,128]{1,0:T(8,128)(2,1)S(1)}, u32[]{:S(2)}, u32[]{:S(2)}) collective-permute-start(s16[264,128]{1,0:T(8,128)(2,1)S(1)} %get-tuple-element.62), channel_id=1, source_target_pairs={{0,28},{4,24},{8,20},{12,16},{16,12},{20,8},{24,4},{28,0},{1,29},{... | collective-permute-start | bytes 202760 | tf_op jit(solution)/shard_map/ppermute | solution.py:435
  31.6 7.2 %collective-permute-start.10 = (s16[264,128]{1,0:T(8,128)(2,1)S(1)}, s16[264,128]{1,0:T(8,128)(2,1)S(1)}, u32[]{:S(2)}, u32[]{:S(2)}) collective-permute-start(s16[264,128]{1,0:T(8,128)(2,1)S(1)} %get-tuple-element.57), channel_id=1, source_target_pairs={{0,8},{4,12},{8,0},{12,4},{16,24},{20,28},{24,16},{28,20},{1,9},{5... | collective-permute-start | bytes 202760 | tf_op jit(solution)/shard_map/ppermute | solution.py:435
  34.9 5.1 %collective-permute-start.11 = (s16[264,128]{1,0:T(8,128)(2,1)S(1)}, s16[264,128]{1,0:T(8,128)(2,1)S(1)}, u32[]{:S(2)}, u32[]{:S(2)}) collective-permute-start(s16[264,128]{1,0:T(8,128)(2,1)S(1)} %get-tuple-element.58), channel_id=1, source_target_pairs={{0,4},{4,0},{8,12},{12,8},{16,20},{20,16},{24,28},{28,24},{1,5},{5... | collective-permute-start | bytes 202760 | tf_op jit(solution)/shard_map/ppermute | solution.py:435

commit v8 on v7

--- a/solution.py
+++ b/solution.py
@@ -94,15 +94,22 @@
     for copy in volume_copies:
         copy.wait()
 
+    whole = jnp.zeros(volume.shape[1:], jnp.float32)
+    for j in range(slots):
+        whole = whole + jnp.where(j < live, 1.0, 0.0) * volume[j]
+
     def one(piece, angle):
         start = group_start(offsets, angle, member, slots)
         places = [offsets[angle, member * slots + j] - start for j in range(slots)]
         places = [jnp.where(j < live, places[j], -1) for j in range(slots)]
-        for s in range(SPREAD):
+        rest = whole
+        for s in range(SPREAD - 1):
             total = jnp.zeros(volume.shape[1:], jnp.float32)
             for j in range(slots):
                 total = total + jnp.where(places[j] == s, 1.0, 0.0) * volume[j]
             piece[s] = total.astype(piece.dtype)
+            rest = rest - total
+        piece[SPREAD - 1] = rest.astype(piece.dtype)
 
     each_piece(direct, count, member, pieces, one)
     lane = lax.broadcasted_iota(jnp.int32, alive.shape, 1)
@@ -493,6 +500,7 @@
     )(*[pltpu.with_memory_space_constraint(x, pltpu.HBM) for x in (offsets, tile_count, volume, table, intensity[0])])
     near_rows, far_rows = swap_halos(near_rows, far_rows)
     arrived = exchange(direct, count, loads)
+    intensity, near_rows = lax.optimization_barrier((intensity, near_rows))
 
     tall = rows + 2 * HALO
     phase_map, inverse, sums, starts = pl.pallas_call(

time: 41.3 us -> 41.2 us (level)
  no operation moved by 1% of the time
where the time goes in v8:
time: 41.2 us; the launch traced here: 40.8 us
  starting transfers between devices  25.3 us (61%)
  Pallas kernels  8.25 us (20%)
  waiting for transfers between devices  6.43 us (16%)
  between operations  0.76 us (2%)
    ppermute x14, starting transfers between devices, exchange(): lax.ppermute(pieces[k], 'tile', [(i, i ^ k) for i in range(count)])  24.6 us
    ppermute x14, waiting for transfers between devices, exchange(): lax.ppermute(pieces[k], 'tile', [(i, i ^ k) for i in range(count)])  6.43 us
    pallas_call x1, Pallas kernels, local(): pl.pallas_call(lambda *refs: phase_kernel(slots, *refs), out_shape=[jax.S...  2.18 us
    pallas_call x1, Pallas kernels, local(): pl.pallas_call(lambda *refs: write_kernel(count, slots, *refs), out_shape...  2.04 us
    pallas_call x1, Pallas kernels, local(): pl.pallas_call(lambda *refs: load_kernel(direct, count, slots, *refs), ou...  1.6 us
    pallas_call x2, Pallas kernels, gather(): pl.pallas_call(lambda *refs: gather_kernel(direct, count, ks, slots, rows...  1.05 us
  transfers between devices with their start and end apart: 16, of which 6 were waited for; matrix products, arithmetic and copies ran while one was open for 0% of the time, Pallas kernels for 13%

profile of v8, /device:TPU:8, one launch (start us, length us, event | category | flops | bytes accessed | tf_op | source)
XLA Modules:
  0.0 40.8 jit_solution(13612537731273552257)
XLA Ops:
  0.6 1.6 %loads.1 = (bf16[8,11264]{1,0:T(8,128)(2,1)S(1)}, bf16[8,11264]{1,0:T(8,128)(2,1)S(1)}, bf16[256,256]{1,0:T(8,128)(2,1)S(1)}, s32[8,64]{1,0:T(8,128)S(1)}, f32[8...) custom-call(s32[8,64]{1,0:T(8,128)} %bitcast.8, ...), custom_call_target="tpu_custom_call" | custom-call | tf_op jit(solution)/shard_map/loads/pallas_call | solution.py:484
  2.2 0.1 collective-permute-start
  2.3 0.7 %collective-permute-start.1 = (bf16[8,11264]{1,0:T(8,128)(2,1)S(1)}, bf16[8,11264]{1,0:T(8,128)(2,1)S(1)}, u32[]{:S(2)}, u32[]{:S(2)}) collective-permute-start(bf16[8,11264]{1,0:T(8,128)(2,1)S(1)} %get-tuple-element.41), channel_id=1, source_target_pairs={{1,2},{2,1},{5,6},{6,5},{9,10},{10,9},{13,14},{14,13},{17,18},{18,... | collective-permute-start | bytes 540680 | tf_op jit(solution)/shard_map/ppermute | solution.py:455
  3.0 2.7 %collective-permute-start.2 = (bf16[4,32,256]{2,1,0:T(8,128)(2,1)S(1)}, bf16[4,32,256]{2,1,0:T(8,128)(2,1)S(1)}, u32[]{:S(2)}, u32[]{:S(2)}) collective-permute-start(bf16[4,32,256]{2,1,0:T(8,128)(2,1)S(1)} %get-tuple-element.46), channel_id=1, source_target_pairs={{0,16},{4,20},{8,24},{12,28},{16,0},{20,4},{24,8},{28,12},{1,17},{... | collective-permute-start | bytes 196616 | tf_op jit(solution)/shard_map/ppermute | solution.py:442
  5.7 1.3 %collective-permute-start.3 = (bf16[4,32,256]{2,1,0:T(8,128)(2,1)S(1)}, bf16[4,32,256]{2,1,0:T(8,128)(2,1)S(1)}, u32[]{:S(2)}, u32[]{:S(2)}) collective-permute-start(bf16[4,32,256]{2,1,0:T(8,128)(2,1)S(1)} %get-tuple-element.47), channel_id=1, source_target_pairs={{0,20},{4,16},{8,28},{12,24},{16,4},{20,0},{24,12},{28,8},{1,21},{... | collective-permute-start | bytes 196616 | tf_op jit(solution)/shard_map/ppermute | solution.py:442
  7.0 1.6 %collective-permute-start.4 = (bf16[4,32,256]{2,1,0:T(8,128)(2,1)S(1)}, bf16[4,32,256]{2,1,0:T(8,128)(2,1)S(1)}, u32[]{:S(2)}, u32[]{:S(2)}) collective-permute-start(bf16[4,32,256]{2,1,0:T(8,128)(2,1)S(1)} %get-tuple-element.48), channel_id=1, source_target_pairs={{0,24},{4,28},{8,16},{12,20},{16,8},{20,12},{24,0},{28,4},{1,25},{... | collective-permute-start | bytes 196616 | tf_op jit(solution)/shard_map/ppermute | solution.py:442
  8.5 2.3 %collective-permute-start.5 = (bf16[4,32,256]{2,1,0:T(8,128)(2,1)S(1)}, bf16[4,32,256]{2,1,0:T(8,128)(2,1)S(1)}, u32[]{:S(2)}, u32[]{:S(2)}) collective-permute-start(bf16[4,32,256]{2,1,0:T(8,128)(2,1)S(1)} %get-tuple-element.49), channel_id=1, source_target_pairs={{0,28},{4,24},{8,20},{12,16},{16,12},{20,8},{24,4},{28,0},{1,29},{... | collective-permute-start | bytes 196616 | tf_op jit(solution)/shard_map/ppermute | solution.py:442
  10.8 1.0 %collective-permute-done.3.refs_5_ = bf16[4,32,256]{2,1,0:T(8,128)(2,1)S(1)} collective-permute-done((bf16[4,32,256]{2,1,0:T(8,128)(2,1)S(1)}, bf16[4,32,256]{2,1,0:T(8,128)(2,1)S(1)}, u32[]{:S(2)}, u32[]{:S(2)}) %collective-permute-start.3) | collective-permute-done | bytes 65568 | tf_op jit(solution)/shard_map/ppermute | solution.py:442
  11.9 3.3 %collective-permute-start.6 = (bf16[4,32,256]{2,1,0:T(8,128)(2,1)S(1)}, bf16[4,32,256]{2,1,0:T(8,128)(2,1)S(1)}, u32[]{:S(2)}, u32[]{:S(2)}) collective-permute-start(bf16[4,32,256]{2,1,0:T(8,128)(2,1)S(1)} %get-tuple-element.52), channel_id=1, source_target_pairs={{0,12},{4,8},{8,4},{12,0},{16,28},{20,24},{24,20},{28,16},{1,13},{... | collective-permute-start | bytes 196616 | tf_op jit(solution)/shard_map/ppermute | solution.py:442
  15.2 0.0 collective-permute-done.refs_3_
  15.2 1.0 %collective-permute-start.7 = (bf16[4,32,256]{2,1,0:T(8,128)(2,1)S(1)}, bf16[4,32,256]{2,1,0:T(8,128)(2,1)S(1)}, u32[]{:S(2)}, u32[]{:S(2)}) collective-permute-start(bf16[4,32,256]{2,1,0:T(8,128)(2,1)S(1)} %get-tuple-element.53), channel_id=1, source_target_pairs={{0,8},{4,12},{8,0},{12,4},{16,24},{20,28},{24,16},{28,20},{1,9},{5... | collective-permute-start | bytes 196616 | tf_op jit(solution)/shard_map/ppermute | solution.py:442
  16.2 1.5 %collective-permute-start.8 = (bf16[4,32,256]{2,1,0:T(8,128)(2,1)S(1)}, bf16[4,32,256]{2,1,0:T(8,128)(2,1)S(1)}, u32[]{:S(2)}, u32[]{:S(2)}) collective-permute-start(bf16[4,32,256]{2,1,0:T(8,128)(2,1)S(1)} %get-tuple-element.54), channel_id=1, source_target_pairs={{0,4},{4,0},{8,12},{12,8},{16,20},{20,16},{24,28},{28,24},{1,5},{5... | collective-permute-start | bytes 196616 | tf_op jit(solution)/shard_map/ppermute | solution.py:442
  17.7 2.2 %phase.1 = (f32[88,32,128]{2,1,0:T(8,128)S(1)}, f32[96,128]{1,0:T(8,128)S(1)}, f32[8,128]{1,0:T(8,128)S(1)}, s32[8,128]{1,0:T(8,128)S(1)}) custom-call(f32[8,64]{1,0:T(8,128)S(1)} %get-tuple-element.37.refs_0_, s32[8,64]{1,0:T(8,128)S(1)} %get-tuple-element.36.refs_1_.refs_0_, bf16[32,11264]{1,0:T(8,128)(2,1)S(1)} %bitcast.6, ...), custom_call_target="tpu_custom_call" | custom-call | tf_op jit(solution)/shard_map/phase/pallas_call | solution.py:506
  19.9 0.3 early.1.refs_1_
  20.2 0.0 copy-start.1
  20.2 0.5 %collective-permute-done.7.refs_6_ = bf16[4,32,256]{2,1,0:T(8,128)(2,1)S(1)} collective-permute-done((bf16[4,32,256]{2,1,0:T(8,128)(2,1)S(1)}, bf16[4,32,256]{2,1,0:T(8,128)(2,1)S(1)}, u32[]{:S(2)}, u32[]{:S(2)}) %collective-permute-start.7) | collective-permute-done | bytes 65568 | tf_op jit(solution)/shard_map/ppermute | solution.py:442
  20.7 0.4 %collective-permute-done.8.refs_7_ = bf16[4,32,256]{2,1,0:T(8,128)(2,1)S(1)} collective-permute-done((bf16[4,32,256]{2,1,0:T(8,128)(2,1)S(1)}, bf16[4,32,256]{2,1,0:T(8,128)(2,1)S(1)}, u32[]{:S(2)}, u32[]{:S(2)}) %collective-permute-start.8) | collective-permute-done | bytes 65568 | tf_op jit(solution)/shard_map/ppermute | solution.py:442
  21.1 0.6 %angle.1 = (f32[88,32,128]{2,1,0:T(8,128)S(1)}, bf16[8,32,640]{2,1,0:T(8,128)(2,1)S(1)}, s16[264,128]{1,0:T(8,128)(2,1)S(1)}, s16[264,128]{1,0:T(8,128)(2,1)S(1)}) custom-call(s32[8,128]{1,0:T(8,128)S(1)} %get-tuple-element.43.refs_0_, f32[88,32,128]{2,1,0:T(8,128)S(1)} %early.1.refs_1_, ...), custom_call_target="tpu_custom_call", output_to_operand_aliasing={{0}: (1, {})} | custom-call | tf_op jit(solution)/shard_map/angle/pallas_call | solution.py:545
  21.7 4.0 %collective-permute-start.13 = (s16[264,128]{1,0:T(8,128)(2,1)S(1)}, s16[264,128]{1,0:T(8,128)(2,1)S(1)}, u32[]{:S(2)}, u32[]{:S(2)}) collective-permute-start(s16[264,128]{1,0:T(8,128)(2,1)S(1)} %get-tuple-element.64), channel_id=1, source_target_pairs={{0,20},{4,16},{8,28},{12,24},{16,4},{20,0},{24,12},{28,8},{1,21},{... | collective-permute-start | bytes 202760 | tf_op jit(solution)/shard_map/ppermute | solution.py:442
  25.7 0.8 %collective-permute-start.14 = (s16[264,128]{1,0:T(8,128)(2,1)S(1)}, s16[264,128]{1,0:T(8,128)(2,1)S(1)}, u32[]{:S(2)}, u32[]{:S(2)}) collective-permute-start(s16[264,128]{1,0:T(8,128)(2,1)S(1)} %get-tuple-element.65), channel_id=1, source_target_pairs={{0,24},{4,28},{8,16},{12,20},{16,8},{20,12},{24,0},{28,4},{1,25},{... | collective-permute-start | bytes 202760 | tf_op jit(solution)/shard_map/ppermute | solution.py:442
  26.6 0.5 %back.1 = (s16[264,128]{1,0:T(8,128)(2,1)S(1)}, s16[264,128]{1,0:T(8,128)(2,1)S(1)}, s16[264,128]{1,0:T(8,128)(2,1)S(1)}, s16[264,128]{1,0:T(8,128)(2,1)S(1)}, s...) custom-call(bf16[8,32,640]{2,1,0:T(8,128)(2,1)S(1)} %get-tuple-element.58.refs_0_, ...), custom_call_target="tpu_custom_call" | custom-call | tf_op jit(solution)/shard_map/back/pallas_call | solution.py:562
  27.1 0.8 %collective-permute-start.9 = (s16[264,128]{1,0:T(8,128)(2,1)S(1)}, s16[264,128]{1,0:T(8,128)(2,1)S(1)}, u32[]{:S(2)}, u32[]{:S(2)}) collective-permute-start(s16[264,128]{1,0:T(8,128)(2,1)S(1)} %get-tuple-element.60), channel_id=1, source_target_pairs={{0,12},{4,8},{8,4},{12,0},{16,28},{20,24},{24,20},{28,16},{1,13},{... | collective-permute-start | bytes 202760 | tf_op jit(solution)/shard_map/ppermute | solution.py:442
  27.9 2.3 %collective-permute-start.12 = (s16[264,128]{1,0:T(8,128)(2,1)S(1)}, s16[264,128]{1,0:T(8,128)(2,1)S(1)}, u32[]{:S(2)}, u32[]{:S(2)}) collective-permute-start(s16[264,128]{1,0:T(8,128)(2,1)S(1)} %get-tuple-element.63), channel_id=1, source_target_pairs={{0,16},{4,20},{8,24},{12,28},{16,0},{20,4},{24,8},{28,12},{1,17},{... | collective-permute-start | bytes 202760 | tf_op jit(solution)/shard_map/ppermute | solution.py:442
  30.2 1.3 %collective-permute-start.15 = (s16[264,128]{1,0:T(8,128)(2,1)S(1)}, s16[264,128]{1,0:T(8,128)(2,1)S(1)}, u32[]{:S(2)}, u32[]{:S(2)}) collective-permute-start(s16[264,128]{1,0:T(8,128)(2,1)S(1)} %get-tuple-element.66), channel_id=1, source_target_pairs={{0,28},{4,24},{8,20},{12,16},{16,12},{20,8},{24,4},{28,0},{1,29},{... | collective-permute-start | bytes 202760 | tf_op jit(solution)/shard_map/ppermute | solution.py:442
  31.6 1.6 %collective-permute-start.10 = (s16[264,128]{1,0:T(8,128)(2,1)S(1)}, s16[264,128]{1,0:T(8,128)(2,1)S(1)}, u32[]{:S(2)}, u32[]{:S(2)}) collective-permute-start(s16[264,128]{1,0:T(8,128)(2,1)S(1)} %get-tuple-element.61), channel_id=1, source_target_pairs={{0,8},{4,12},{8,0},{12,4},{16,24},{20,28},{24,16},{28,20},{1,9},{5... | collective-permute-start | bytes 202760 | tf_op jit(solution)/shard_map/ppermute | solution.py:442
  33.2 1.7 %collective-permute-done.14.refs_3_ = s16[264,128]{1,0:T(8,128)(2,1)S(1)} collective-permute-done((s16[264,128]{1,0:T(8,128)(2,1)S(1)}, s16[264,128]{1,0:T(8,128)(2,1)S(1)}, u32[]{:S(2)}, u32[]{:S(2)}) %collective-permute-start.14) | collective-permute-done | bytes 67616 | tf_op jit(solution)/shard_map/ppermute | solution.py:442
  34.9 0.0 collective-permute-start.11
  34.9 2.0 %write.1 = (f32[32,11264]{1,0:T(8,128)}, s32[16,128]{1,0:T(8,128)S(1)}) custom-call(s32[8,64]{1,0:T(8,128)S(1)} %get-tuple-element.36.refs_1_.refs_0_, s32[8]{0:T(128)S(1)} %copy-done.1, f32[88,32,128]{2,1,0:T(8,128)S(1)} %get-tuple-element.55.refs_2_), custom_call_target="tpu_custom_call" | custom-call | tf_op jit(solution)/shard_map/write/pallas_call | solution.py:574
  37.0 1.6 %collective-permute-done.15.refs_4_ = s16[264,128]{1,0:T(8,128)(2,1)S(1)} collective-permute-done((s16[264,128]{1,0:T(8,128)(2,1)S(1)}, s16[264,128]{1,0:T(8,128)(2,1)S(1)}, u32[]{:S(2)}, u32[]{:S(2)}) %collective-permute-start.15) | collective-permute-done | bytes 67616 | tf_op jit(solution)/shard_map/ppermute | solution.py:442
  38.6 0.2 gather_first.1
  38.8 1.2 %collective-permute-done.11.refs_4_ = s16[264,128]{1,0:T(8,128)(2,1)S(1)} collective-permute-done((s16[264,128]{1,0:T(8,128)(2,1)S(1)}, s16[264,128]{1,0:T(8,128)(2,1)S(1)}, u32[]{:S(2)}, u32[]{:S(2)}) %collective-permute-start.11) | collective-permute-done | bytes 67616 | tf_op jit(solution)/shard_map/ppermute | solution.py:442
  39.9 0.9 %gather_last.1 = (f32[8,32,256]{2,1,0:T(8,128)}, f32[8,128]{1,0:T(8,128)}) custom-call(s32[16,128]{1,0:T(8,128)S(1)} %get-tuple-element.57.refs_0_, s16[264,128]{1,0:T(8,128)(2,1)S(1)} %get-tuple-element.59.refs_1_, s16[264,128]{1,0:T(8,128)(2,1)S(1)} %collective-permute-done.9.refs_2_, s16[264,128]{1,0:T(8,128)(2,1)S(1)} %collective-permute-done.10.refs_3_, ...), custom_call_target="tpu_custom_call" | custom-call | tf_op jit(solution)/shard_map/gather_last/pallas_call | solution.py:589
  (12 shorter events, 0.0 us)
Async XLA Ops:
  0.6 17.1 %copy-start = (bf16[1,32,11264]{2,1,0:T(8,128)(2,1)S(1)}, bf16[1,32,11264]{2,1,0:T(8,128)(2,1)}, u32[]{:S(2)}) copy-start(bf16[1,32,11264]{2,1,0:T(8,128)(2,1)} %param.5) | copy-start | bytes 2162692
  2.2 13.0 %collective-permute-start = (bf16[8,11264]{1,0:T(8,128)(2,1)S(1)}, bf16[8,11264]{1,0:T(8,128)(2,1)S(1)}, u32[]{:S(2)}, u32[]{:S(2)}) collective-permute-start(bf16[8,11264]{1,0:T(8,128)(2,1)S(1)} %get-tuple-element.38), channel_id=1, source_target_pairs={{0,1},{2,3},{1,0},{3,2},{4,5},{6,7},{5,4},{7,6},{8,9},{10,11},{9,8... | collective-permute-start | bytes 540680 | tf_op jit(solution)/shard_map/ppermute | solution.py:456
  2.3 13.9 %collective-permute-start.1 = (bf16[8,11264]{1,0:T(8,128)(2,1)S(1)}, bf16[8,11264]{1,0:T(8,128)(2,1)S(1)}, u32[]{:S(2)}, u32[]{:S(2)}) collective-permute-start(bf16[8,11264]{1,0:T(8,128)(2,1)S(1)} %get-tuple-element.41), channel_id=1, source_target_pairs={{1,2},{2,1},{5,6},{6,5},{9,10},{10,9},{13,14},{14,13},{17,18},{18,... | collective-permute-start | bytes 540680 | tf_op jit(solution)/shard_map/ppermute | solution.py:455
  3.0 5.5 %collective-permute-start.2 = (bf16[4,32,256]{2,1,0:T(8,128)(2,1)S(1)}, bf16[4,32,256]{2,1,0:T(8,128)(2,1)S(1)}, u32[]{:S(2)}, u32[]{:S(2)}) collective-permute-start(bf16[4,32,256]{2,1,0:T(8,128)(2,1)S(1)} %get-tuple-element.46), channel_id=1, source_target_pairs={{0,16},{4,20},{8,24},{12,28},{16,0},{20,4},{24,8},{28,12},{1,17},{... | collective-permute-start | bytes 196616 | tf_op jit(solution)/shard_map/ppermute | solution.py:442
  5.7 6.2 %collective-permute-start.3 = (bf16[4,32,256]{2,1,0:T(8,128)(2,1)S(1)}, bf16[4,32,256]{2,1,0:T(8,128)(2,1)S(1)}, u32[]{:S(2)}, u32[]{:S(2)}) collective-permute-start(bf16[4,32,256]{2,1,0:T(8,128)(2,1)S(1)} %get-tuple-element.47), channel_id=1, source_target_pairs={{0,20},{4,16},{8,28},{12,24},{16,4},{20,0},{24,12},{28,8},{1,21},{... | collective-permute-start | bytes 196616 | tf_op jit(solution)/shard_map/ppermute | solution.py:442
  7.0 13.0 %collective-permute-start.4 = (bf16[4,32,256]{2,1,0:T(8,128)(2,1)S(1)}, bf16[4,32,256]{2,1,0:T(8,128)(2,1)S(1)}, u32[]{:S(2)}, u32[]{:S(2)}) collective-permute-start(bf16[4,32,256]{2,1,0:T(8,128)(2,1)S(1)} %get-tuple-element.48), channel_id=1, source_target_pairs={{0,24},{4,28},{8,16},{12,20},{16,8},{20,12},{24,0},{28,4},{1,25},{... | collective-permute-start | bytes 196616 | tf_op jit(solution)/shard_map/ppermute | solution.py:442
  8.5 11.4 %collective-permute-start.5 = (bf16[4,32,256]{2,1,0:T(8,128)(2,1)S(1)}, bf16[4,32,256]{2,1,0:T(8,128)(2,1)S(1)}, u32[]{:S(2)}, u32[]{:S(2)}) collective-permute-start(bf16[4,32,256]{2,1,0:T(8,128)(2,1)S(1)} %get-tuple-element.49), channel_id=1, source_target_pairs={{0,28},{4,24},{8,20},{12,16},{16,12},{20,8},{24,4},{28,0},{1,29},{... | collective-permute-start | bytes 196616 | tf_op jit(solution)/shard_map/ppermute | solution.py:442
  11.9 8.4 %collective-permute-start.6 = (bf16[4,32,256]{2,1,0:T(8,128)(2,1)S(1)}, bf16[4,32,256]{2,1,0:T(8,128)(2,1)S(1)}, u32[]{:S(2)}, u32[]{:S(2)}) collective-permute-start(bf16[4,32,256]{2,1,0:T(8,128)(2,1)S(1)} %get-tuple-element.52), channel_id=1, source_target_pairs={{0,12},{4,8},{8,4},{12,0},{16,28},{20,24},{24,20},{28,16},{1,13},{... | collective-permute-start | bytes 196616 | tf_op jit(solution)/shard_map/ppermute | solution.py:442
  15.2 5.5 %collective-permute-start.7 = (bf16[4,32,256]{2,1,0:T(8,128)(2,1)S(1)}, bf16[4,32,256]{2,1,0:T(8,128)(2,1)S(1)}, u32[]{:S(2)}, u32[]{:S(2)}) collective-permute-start(bf16[4,32,256]{2,1,0:T(8,128)(2,1)S(1)} %get-tuple-element.53), channel_id=1, source_target_pairs={{0,8},{4,12},{8,0},{12,4},{16,24},{20,28},{24,16},{28,20},{1,9},{5... | collective-permute-start | bytes 196616 | tf_op jit(solution)/shard_map/ppermute | solution.py:442
  16.2 4.9 %collective-permute-start.8 = (bf16[4,32,256]{2,1,0:T(8,128)(2,1)S(1)}, bf16[4,32,256]{2,1,0:T(8,128)(2,1)S(1)}, u32[]{:S(2)}, u32[]{:S(2)}) collective-permute-start(bf16[4,32,256]{2,1,0:T(8,128)(2,1)S(1)} %get-tuple-element.54), channel_id=1, source_target_pairs={{0,4},{4,0},{8,12},{12,8},{16,20},{20,16},{24,28},{28,24},{1,5},{5... | collective-permute-start | bytes 196616 | tf_op jit(solution)/shard_map/ppermute | solution.py:442
  20.2 14.7 %copy-start.1 = (s32[8]{0:T(128)S(1)}, s32[8]{0:T(128)}, u32[]{:S(2)}) copy-start(s32[8]{0:T(128)} %refs_1_.3) | copy-start | bytes 100
  21.7 9.8 %collective-permute-start.13 = (s16[264,128]{1,0:T(8,128)(2,1)S(1)}, s16[264,128]{1,0:T(8,128)(2,1)S(1)}, u32[]{:S(2)}, u32[]{:S(2)}) collective-permute-start(s16[264,128]{1,0:T(8,128)(2,1)S(1)} %get-tuple-element.64), channel_id=1, source_target_pairs={{0,20},{4,16},{8,28},{12,24},{16,4},{20,0},{24,12},{28,8},{1,21},{... | collective-permute-start | bytes 202760 | tf_op jit(solution)/shard_map/ppermute | solution.py:442
  25.7 9.1 %collective-permute-start.14 = (s16[264,128]{1,0:T(8,128)(2,1)S(1)}, s16[264,128]{1,0:T(8,128)(2,1)S(1)}, u32[]{:S(2)}, u32[]{:S(2)}) collective-permute-start(s16[264,128]{1,0:T(8,128)(2,1)S(1)} %get-tuple-element.65), channel_id=1, source_target_pairs={{0,24},{4,28},{8,16},{12,20},{16,8},{20,12},{24,0},{28,4},{1,25},{... | collective-permute-start | bytes 202760 | tf_op jit(solution)/shard_map/ppermute | solution.py:442
  27.1 11.6 %collective-permute-start.9 = (s16[264,128]{1,0:T(8,128)(2,1)S(1)}, s16[264,128]{1,0:T(8,128)(2,1)S(1)}, u32[]{:S(2)}, u32[]{:S(2)}) collective-permute-start(s16[264,128]{1,0:T(8,128)(2,1)S(1)} %get-tuple-element.60), channel_id=1, source_target_pairs={{0,12},{4,8},{8,4},{12,0},{16,28},{20,24},{24,20},{28,16},{1,13},{... | collective-permute-start | bytes 202760 | tf_op jit(solution)/shard_map/ppermute | solution.py:442
  27.9 9.1 %collective-permute-start.12 = (s16[264,128]{1,0:T(8,128)(2,1)S(1)}, s16[264,128]{1,0:T(8,128)(2,1)S(1)}, u32[]{:S(2)}, u32[]{:S(2)}) collective-permute-start(s16[264,128]{1,0:T(8,128)(2,1)S(1)} %get-tuple-element.63), channel_id=1, source_target_pairs={{0,16},{4,20},{8,24},{12,28},{16,0},{20,4},{24,8},{28,12},{1,17},{... | collective-permute-start | bytes 202760 | tf_op jit(solution)/shard_map/ppermute | solution.py:442
  30.2 8.4 %collective-permute-start.15 = (s16[264,128]{1,0:T(8,128)(2,1)S(1)}, s16[264,128]{1,0:T(8,128)(2,1)S(1)}, u32[]{:S(2)}, u32[]{:S(2)}) collective-permute-start(s16[264,128]{1,0:T(8,128)(2,1)S(1)} %get-tuple-element.66), channel_id=1, source_target_pairs={{0,28},{4,24},{8,20},{12,16},{16,12},{20,8},{24,4},{28,0},{1,29},{... | collective-permute-start | bytes 202760 | tf_op jit(solution)/shard_map/ppermute | solution.py:442
  31.6 7.2 %collective-permute-start.10 = (s16[264,128]{1,0:T(8,128)(2,1)S(1)}, s16[264,128]{1,0:T(8,128)(2,1)S(1)}, u32[]{:S(2)}, u32[]{:S(2)}) collective-permute-start(s16[264,128]{1,0:T(8,128)(2,1)S(1)} %get-tuple-element.61), channel_id=1, source_target_pairs={{0,8},{4,12},{8,0},{12,4},{16,24},{20,28},{24,16},{28,20},{1,9},{5... | collective-permute-start | bytes 202760 | tf_op jit(solution)/shard_map/ppermute | solution.py:442
  34.9 5.1 %collective-permute-start.11 = (s16[264,128]{1,0:T(8,128)(2,1)S(1)}, s16[264,128]{1,0:T(8,128)(2,1)S(1)}, u32[]{:S(2)}, u32[]{:S(2)}) collective-permute-start(s16[264,128]{1,0:T(8,128)(2,1)S(1)} %get-tuple-element.62), channel_id=1, source_target_pairs={{0,4},{4,0},{8,12},{12,8},{16,20},{20,16},{24,28},{28,24},{1,5},{5... | collective-permute-start | bytes 202760 | tf_op jit(solution)/shard_map/ppermute | solution.py:442
